TPU v7x, 1024 devices: a whole 4x4x32 slice. The times are simulated.
1024 devices in a mesh: cell: 64 (over z, core), inst: 16 (over x, y).
Axes of the slice: x: 4, y: 4, z: 32, core: 2. Of those that a mesh axis runs over, the one named last changes fastest.
Arguments:
- residual: float32 [16, 5, 1024, 256], P('inst', None, 'cell'), may hold values from -6 to 6
- diag_gain: float32 [16, 1024, 256], P('inst', 'cell'), may hold values from 2.7 to 3
- flux_jac: float32 [4, 5, 5], replicated, may hold values from -1.75 to 1.75
- omega: float32 [1], replicated, may hold values from 0.04 to 0.12
- shifts: float32 [7], replicated, may hold values from 1.45 to 1.55
Outputs:
- basis_q: float32 [8, 16, 5, 1024, 256], P(None, 'inst', None, 'cell')
- factor_r: float32 [8, 8], replicated
All inputs are finite; a program needn't handle non-finite values.
Results may differ from a plain program's by a relative error of at most 0.0003.
Values sent between devices are 32-bit elements; how exact they have to be, the bound alone decides.
No kernel may reach another device: no remote copies, remote signals or barrier semaphores. Data moves between devices by JAX's collectives and lax.ppermute only.
A program may use at most 32 MiB of HBM per device.

v0:
```python
import jax
import jax.numpy as jnp
from jax import lax
from jax.sharding import PartitionSpec as P

S = 8


def with_halo(cells, sides, width):
    for axis, dim in sides:
        count = lax.axis_size(axis)
        ends = count - 1
        head = lax.slice_in_dim(cells, 0, width, axis=dim)
        tail = lax.slice_in_dim(cells, cells.shape[dim] - width, cells.shape[dim], axis=dim)
        cells = jnp.concatenate(
            [
                lax.ppermute(tail, axis, [(i, (i + 1) % count) for i in range(ends)]),
                cells,
                lax.ppermute(head, axis, [((i + 1) % count, i) for i in range(ends)]),
            ],
            axis=dim,
        )
    return cells


def spectral_matrix(count):
    index = jnp.arange(count, dtype=jnp.int32)
    offset = index[:, None] - index[None, :]
    parity = (1 - 2 * (jnp.abs(offset) % 2)).astype(jnp.float32)
    angle = jnp.pi * offset.astype(jnp.float32) / count
    denom = jnp.where(offset == 0, 1.0, jnp.sin(angle))
    return jnp.where(offset == 0, 0.0, 0.5 * parity * jnp.cos(angle) / denom)


def couple(field):
    coupling = spectral_matrix(field.shape[0])
    return jnp.einsum("ij,jfrc->ifrc", coupling, field, precision=lax.Precision.HIGHEST)


def stencil(field, padded_rows, gain, flux_jac):
    padded = jnp.pad(padded_rows, ((0, 0), (0, 0), (0, 0), (1, 1)))
    neighbours = [
        padded[:, :, :-2, 1:-1],
        padded[:, :, 2:, 1:-1],
        padded[:, :, 1:-1, :-2],
        padded[:, :, 1:-1, 2:],
    ]
    total = gain[:, None] * field
    for direction in range(4):
        total = total - jnp.einsum(
            "fe,ierc->ifrc",
            flux_jac[direction],
            neighbours[direction],
            precision=lax.Precision.HIGHEST,
        )
    return total


def coupled_back(block):
    mixed = couple(block)
    return lax.all_to_all(mixed, "inst", split_axis=0, concat_axis=2, tiled=True)


def gram_sum(matrix):
    local = jnp.dot(matrix, matrix.T, precision=lax.Precision.HIGHEST)
    return lax.psum(local, ("cell", "inst"))


def on_device(residual, diag_gain, flux_jac, omega, shifts):
    vectors = []
    vectors.append(residual)
    for step in range(S - 1):
        prior = vectors[-1]
        padded_rows = with_halo(prior, (("cell", 2),), 1)
        mixed = coupled_back(lax.all_to_all(prior, "inst", split_axis=2, concat_axis=0, tiled=True))
        vectors.append(
            stencil(prior, padded_rows, diag_gain, flux_jac)
            + omega[0] * mixed
            - shifts[step] * prior
        )
    stacked = jnp.stack(vectors)
    matrix = stacked.reshape(S, -1)
    lower_one = jnp.linalg.cholesky(gram_sum(matrix))
    whitened = jax.scipy.linalg.solve_triangular(lower_one, matrix, lower=True)
    lower_two = jnp.linalg.cholesky(gram_sum(whitened))
    ortho = jax.scipy.linalg.solve_triangular(lower_two, whitened, lower=True).reshape(
        stacked.shape
    )
    factor_r = jnp.dot(lower_one, lower_two, precision=lax.Precision.HIGHEST).T
    return (ortho, factor_r)


def solution(mesh):
    in_specs = (P("inst", None, "cell", None), P("inst", "cell", None), P(), P(), P())
    out_specs = (P(None, "inst", None, "cell", None), P())
    return jax.shard_map(
        on_device, mesh=mesh, in_specs=in_specs, out_specs=out_specs, check_vma=False
    )
```

profile of v0, /device:TPU:1, one launch (start us, length us, event | category | flops | bytes accessed | tf_op | source)
XLA Modules:
  0.0 563.0 jit_solution(15314474639365112771)
XLA Ops:
  1.7 4.9 collective-permute-start
  6.6 12.4 %collective-permute-start.1 = (f32[1,5,1,256]{3,1,2,0:T(8,128)S(1)}, f32[1,5,1,256]{3,1,2,0:T(8,128)S(1)}, u32[]{:S(2)}, u32[]{:S(2)}) collective-permute-start(f32[1,5,1,256]{3,1,2,0:T(8,128)S(1)} %get-tuple-element.23), channel_id=1, source_target_pairs={{16,0},{32,16},{48,32},{64,48},{80,64},{96,80},{112,96},{128,112},... | collective-permute-start | bytes 15368 | tf_op jit(solution)/shard_map/ppermute | solution.py:19
  19.7 3.5 all-to-all-start
  26.6 3.7 all-to-all-done
  31.4 3.5 all-to-all-start.1
  35.2 6.3 %all-to-all-done.1 = f32[16,5,1,256]{3,2,1,0:T(1,128)S(1)} async-done(((f32[16,5,1,256]{3,2,1,0:T(1,128)}), f32[16,5,1,256]{3,2,1,0:T(1,128)S(1)}, u32[]{:S(2)}, u32[]{:S(2)}) %all-to-all-start.1) | async-done | bytes 81952 | tf_op jit(solution)/shard_map/all_to_all | solution.py:61
  48.0 3.5 all-to-all-start.2
  52.2 6.1 %all-to-all-done.2 = f32[1,5,16,256]{3,0,1,2:T(1,128)S(1)} async-done(((f32[1,5,16,256]{3,0,1,2:T(1,128)}), f32[1,5,16,256]{3,0,1,2:T(1,128)S(1)}, u32[]{:S(2)}, u32[]{:S(2)}) %all-to-all-start.2) | async-done | bytes 81952 | tf_op jit(solution)/shard_map/all_to_all | solution.py:75
  59.3 3.5 all-to-all-start.3
  63.1 6.2 %all-to-all-done.3 = f32[16,5,1,256]{3,2,1,0:T(1,128)S(1)} async-done(((f32[16,5,1,256]{3,2,1,0:T(1,128)}), f32[16,5,1,256]{3,2,1,0:T(1,128)S(1)}, u32[]{:S(2)}, u32[]{:S(2)}) %all-to-all-start.3) | async-done | bytes 81952 | tf_op jit(solution)/shard_map/all_to_all | solution.py:61
  70.3 4.8 collective-permute-start.4
  77.8 3.5 all-to-all-start.4
  82.0 5.8 %all-to-all-done.4 = f32[1,5,16,256]{3,0,1,2:T(1,128)S(1)} async-done(((f32[1,5,16,256]{3,0,1,2:T(1,128)}), f32[1,5,16,256]{3,0,1,2:T(1,128)S(1)}, u32[]{:S(2)}, u32[]{:S(2)}) %all-to-all-start.4) | async-done | bytes 81952 | tf_op jit(solution)/shard_map/all_to_all | solution.py:75
  88.8 3.5 all-to-all-start.5
  92.6 6.2 %all-to-all-done.5 = f32[16,5,1,256]{3,2,1,0:T(1,128)S(1)} async-done(((f32[16,5,1,256]{3,2,1,0:T(1,128)}), f32[16,5,1,256]{3,2,1,0:T(1,128)S(1)}, u32[]{:S(2)}, u32[]{:S(2)}) %all-to-all-start.5) | async-done | bytes 81952 | tf_op jit(solution)/shard_map/all_to_all | solution.py:61
  99.6 6.0 %collective-permute-start.6 = (f32[1,5,1,256]{3,1,2,0:T(8,128)S(1)}, f32[1,5,1,256]{3,1,2,0:T(8,128)S(1)}, u32[]{:S(2)}, u32[]{:S(2)}) collective-permute-start(f32[1,5,1,256]{3,1,2,0:T(8,128)S(1)} %get-tuple-element.16), channel_id=1, source_target_pairs={{0,16},{16,32},{32,48},{48,64},{64,80},{80,96},{96,112},{112,128},... | collective-permute-start | bytes 15368 | tf_op jit(solution)/shard_map/ppermute | solution.py:17
  108.3 3.5 all-to-all-start.6
  112.5 5.8 %all-to-all-done.6 = f32[1,5,16,256]{3,0,1,2:T(1,128)S(1)} async-done(((f32[1,5,16,256]{3,0,1,2:T(1,128)}), f32[1,5,16,256]{3,0,1,2:T(1,128)S(1)}, u32[]{:S(2)}, u32[]{:S(2)}) %all-to-all-start.6) | async-done | bytes 81952 | tf_op jit(solution)/shard_map/all_to_all | solution.py:75
  119.3 3.5 all-to-all-start.7
  123.0 6.2 %all-to-all-done.7 = f32[16,5,1,256]{3,2,1,0:T(1,128)S(1)} async-done(((f32[16,5,1,256]{3,2,1,0:T(1,128)}), f32[16,5,1,256]{3,2,1,0:T(1,128)S(1)}, u32[]{:S(2)}, u32[]{:S(2)}) %all-to-all-start.7) | async-done | bytes 81952 | tf_op jit(solution)/shard_map/all_to_all | solution.py:61
  130.3 6.0 %collective-permute-start.8 = (f32[1,5,1,256]{3,1,2,0:T(8,128)S(1)}, f32[1,5,1,256]{3,1,2,0:T(8,128)S(1)}, u32[]{:S(2)}, u32[]{:S(2)}) collective-permute-start(f32[1,5,1,256]{3,1,2,0:T(8,128)S(1)} %get-tuple-element.14), channel_id=1, source_target_pairs={{0,16},{16,32},{32,48},{48,64},{64,80},{80,96},{96,112},{112,128},... | collective-permute-start | bytes 15368 | tf_op jit(solution)/shard_map/ppermute | solution.py:17
  143.2 5.8 %all-to-all-done.8 = f32[1,5,16,256]{3,0,1,2:T(1,128)S(1)} async-done(((f32[1,5,16,256]{3,0,1,2:T(1,128)}), f32[1,5,16,256]{3,0,1,2:T(1,128)S(1)}, u32[]{:S(2)}, u32[]{:S(2)}) %all-to-all-start.8) | async-done | bytes 81952 | tf_op jit(solution)/shard_map/all_to_all | solution.py:75
  153.7 6.2 %all-to-all-done.9 = f32[16,5,1,256]{3,2,1,0:T(1,128)S(1)} async-done(((f32[16,5,1,256]{3,2,1,0:T(1,128)}), f32[16,5,1,256]{3,2,1,0:T(1,128)S(1)}, u32[]{:S(2)}, u32[]{:S(2)}) %all-to-all-start.9) | async-done | bytes 81952 | tf_op jit(solution)/shard_map/all_to_all | solution.py:61
  160.9 6.0 %collective-permute-start.10 = (f32[1,5,1,256]{3,1,2,0:T(8,128)S(1)}, f32[1,5,1,256]{3,1,2,0:T(8,128)S(1)}, u32[]{:S(2)}, u32[]{:S(2)}) collective-permute-start(f32[1,5,1,256]{3,1,2,0:T(8,128)S(1)} %get-tuple-element.12), channel_id=1, source_target_pairs={{0,16},{16,32},{32,48},{48,64},{64,80},{80,96},{96,112},{112,128},... | collective-permute-start | bytes 15368 | tf_op jit(solution)/shard_map/ppermute | solution.py:17
  173.7 5.8 %all-to-all-done.10 = f32[1,5,16,256]{3,0,1,2:T(1,128)S(1)} async-done(((f32[1,5,16,256]{3,0,1,2:T(1,128)}), f32[1,5,16,256]{3,0,1,2:T(1,128)S(1)}, u32[]{:S(2)}, u32[]{:S(2)}) %all-to-all-start.10) | async-done | bytes 81952 | tf_op jit(solution)/shard_map/all_to_all | solution.py:75
  184.3 6.2 %all-to-all-done.11 = f32[16,5,1,256]{3,2,1,0:T(1,128)S(1)} async-done(((f32[16,5,1,256]{3,2,1,0:T(1,128)}), f32[16,5,1,256]{3,2,1,0:T(1,128)S(1)}, u32[]{:S(2)}, u32[]{:S(2)}) %all-to-all-start.11) | async-done | bytes 81952 | tf_op jit(solution)/shard_map/all_to_all | solution.py:61
  191.5 6.0 %collective-permute-start.12 = (f32[1,5,1,256]{3,1,2,0:T(8,128)S(1)}, f32[1,5,1,256]{3,1,2,0:T(8,128)S(1)}, u32[]{:S(2)}, u32[]{:S(2)}) collective-permute-start(f32[1,5,1,256]{3,1,2,0:T(8,128)S(1)} %get-tuple-element.10), channel_id=1, source_target_pairs={{0,16},{16,32},{32,48},{48,64},{64,80},{80,96},{96,112},{112,128},... | collective-permute-start | bytes 15368 | tf_op jit(solution)/shard_map/ppermute | solution.py:17
  201.3 3.5 all-to-all-start.12
  205.5 5.8 %all-to-all-done.12 = f32[1,5,16,256]{3,0,1,2:T(1,128)S(1)} async-done(((f32[1,5,16,256]{3,0,1,2:T(1,128)}), f32[1,5,16,256]{3,0,1,2:T(1,128)S(1)}, u32[]{:S(2)}, u32[]{:S(2)}) %all-to-all-start.12) | async-done | bytes 81952 | tf_op jit(solution)/shard_map/all_to_all | solution.py:75
  216.0 6.2 %all-to-all-done.13 = f32[16,5,1,256]{3,2,1,0:T(1,128)S(1)} async-done(((f32[16,5,1,256]{3,2,1,0:T(1,128)}), f32[16,5,1,256]{3,2,1,0:T(1,128)S(1)}, u32[]{:S(2)}, u32[]{:S(2)}) %all-to-all-start.13) | async-done | bytes 81952 | tf_op jit(solution)/shard_map/all_to_all | solution.py:61
  224.8 170.2 %psum.14 = f32[8,8]{0,1:T(8,128)S(1)} all-reduce(f32[8,8]{0,1:T(8,128)S(1)} %convolution_bitcast_fusion.35), channel_id=1, replica_groups=mesh['cell'=64,'inst'=16] {'cell','inst'}, use_global_device_ids=true, to_apply=%region_0.1 | all-reduce | flops 64 | bytes 512 | tf_op jit(solution)/shard_map/psum | solution.py:66
  403.2 153.2 %psum.15 = f32[8,8]{0,1:T(8,128)S(1)} all-reduce(f32[8,8]{0,1:T(8,128)S(1)} %fusion.250), channel_id=1, replica_groups=mesh['cell'=64,'inst'=16] {'cell','inst'}, use_global_device_ids=true, to_apply=%region_3.6 | all-reduce | flops 64 | bytes 512 | tf_op jit(solution)/shard_map/psum | solution.py:66
  (137 shorter events, 77.3 us)
Async XLA Ops:
  0.6 18.4 %copy-start = (f32[1,5,16,256]{3,2,1,0:T(8,128)S(1)}, f32[1,5,16,256]{3,2,1,0:T(8,128)}, u32[]{:S(2)}) copy-start(f32[1,5,16,256]{3,2,1,0:T(8,128)} %param.8) | copy-start | bytes 245764
  1.7 24.2 %collective-permute-start = (f32[1,5,1,256]{3,1,2,0:T(8,128)S(1)}, f32[1,5,1,256]{3,1,2,0:T(8,128)S(1)}, u32[]{:S(2)}, u32[]{:S(2)}) collective-permute-start(f32[1,5,1,256]{3,1,2,0:T(8,128)S(1)} %get-tuple-element.22), channel_id=1, source_target_pairs={{0,16},{16,32},{32,48},{48,64},{64,80},{80,96},{96,112},{112,128},... | collective-permute-start | bytes 15368 | tf_op jit(solution)/shard_map/ppermute | solution.py:17
  6.6 19.3 %collective-permute-start.1 = (f32[1,5,1,256]{3,1,2,0:T(8,128)S(1)}, f32[1,5,1,256]{3,1,2,0:T(8,128)S(1)}, u32[]{:S(2)}, u32[]{:S(2)}) collective-permute-start(f32[1,5,1,256]{3,1,2,0:T(8,128)S(1)} %get-tuple-element.23), channel_id=1, source_target_pairs={{16,0},{32,16},{48,32},{64,48},{80,64},{96,80},{112,96},{128,112},... | collective-permute-start | bytes 15368 | tf_op jit(solution)/shard_map/ppermute | solution.py:19
  19.7 10.7 %all-to-all-start = ((f32[1,5,16,256]{3,1,0,2:T(8,128)}), f32[1,5,16,256]{3,1,0,2:T(8,128)S(1)}, u32[]{:S(2)}, u32[]{:S(2)}) async-start(f32[1,5,16,256]{3,1,0,2:T(8,128)} %copy.93), calls=%async_computation | async-start | bytes 262144 | tf_op jit(solution)/shard_map/all_to_all | solution.py:75
  23.2 0.7 copy-start.3
  23.9 0.7 copy-start.2
  31.4 10.1 %all-to-all-start.1 = ((f32[16,5,1,256]{3,2,1,0:T(1,128)}), f32[16,5,1,256]{3,2,1,0:T(1,128)S(1)}, u32[]{:S(2)}, u32[]{:S(2)}) async-start(f32[16,5,1,256]{3,2,1,0:T(1,128)} %copy.95), calls=%async_computation.1 | async-start | bytes 163840 | tf_op jit(solution)/shard_map/all_to_all | solution.py:61
  34.9 6.6 %copy-start.1 = (f32[1,16,256]{2,1,0:T(8,128)S(1)}, f32[1,16,256]{2,1,0:T(8,128)}, u32[]{:S(2)}) copy-start(f32[1,16,256]{2,1,0:T(8,128)} %param.9) | copy-start | bytes 49156
  42.3 9.3 %collective-permute-start.2 = (f32[1,5,1,256]{3,1,2,0:T(8,128)S(1)}, f32[1,5,1,256]{3,1,2,0:T(8,128)S(1)}, u32[]{:S(2)}, u32[]{:S(2)}) collective-permute-start(f32[1,5,1,256]{3,1,2,0:T(8,128)S(1)} %get-tuple-element.20), channel_id=1, source_target_pairs={{0,16},{16,32},{32,48},{48,64},{64,80},{80,96},{96,112},{112,128},... | collective-permute-start | bytes 15368 | tf_op jit(solution)/shard_map/ppermute | solution.py:17
  44.2 7.3 %collective-permute-start.3 = (f32[1,5,1,256]{3,1,2,0:T(8,128)S(1)}, f32[1,5,1,256]{3,1,2,0:T(8,128)S(1)}, u32[]{:S(2)}, u32[]{:S(2)}) collective-permute-start(f32[1,5,1,256]{3,1,2,0:T(8,128)S(1)} %get-tuple-element.21), channel_id=1, source_target_pairs={{16,0},{32,16},{48,32},{64,48},{80,64},{96,80},{112,96},{128,112},... | collective-permute-start | bytes 15368 | tf_op jit(solution)/shard_map/ppermute | solution.py:19
  48.0 10.3 %all-to-all-start.2 = ((f32[1,5,16,256]{3,0,1,2:T(1,128)}), f32[1,5,16,256]{3,0,1,2:T(1,128)S(1)}, u32[]{:S(2)}, u32[]{:S(2)}) async-start(f32[1,5,16,256]{3,0,1,2:T(1,128)} %copy.98), calls=%async_computation.2 | async-start | bytes 163840 | tf_op jit(solution)/shard_map/all_to_all | solution.py:75
  59.3 10.0 %all-to-all-start.3 = ((f32[16,5,1,256]{3,2,1,0:T(1,128)}), f32[16,5,1,256]{3,2,1,0:T(1,128)S(1)}, u32[]{:S(2)}, u32[]{:S(2)}) async-start(f32[16,5,1,256]{3,2,1,0:T(1,128)} %copy.100), calls=%async_computation.3 | async-start | bytes 163840 | tf_op jit(solution)/shard_map/all_to_all | solution.py:61
  70.3 11.0 %collective-permute-start.4 = (f32[1,5,1,256]{3,1,2,0:T(8,128)S(1)}, f32[1,5,1,256]{3,1,2,0:T(8,128)S(1)}, u32[]{:S(2)}, u32[]{:S(2)}) collective-permute-start(f32[1,5,1,256]{3,1,2,0:T(8,128)S(1)} %get-tuple-element.18), channel_id=1, source_target_pairs={{0,16},{16,32},{32,48},{48,64},{64,80},{80,96},{96,112},{112,128},... | collective-permute-start | bytes 15368 | tf_op jit(solution)/shard_map/ppermute | solution.py:17
  75.1 6.2 %collective-permute-start.5 = (f32[1,5,1,256]{3,1,2,0:T(8,128)S(1)}, f32[1,5,1,256]{3,1,2,0:T(8,128)S(1)}, u32[]{:S(2)}, u32[]{:S(2)}) collective-permute-start(f32[1,5,1,256]{3,1,2,0:T(8,128)S(1)} %get-tuple-element.19), channel_id=1, source_target_pairs={{16,0},{32,16},{48,32},{64,48},{80,64},{96,80},{112,96},{128,112},... | collective-permute-start | bytes 15368 | tf_op jit(solution)/shard_map/ppermute | solution.py:19
  77.8 10.0 %all-to-all-start.4 = ((f32[1,5,16,256]{3,0,1,2:T(1,128)}), f32[1,5,16,256]{3,0,1,2:T(1,128)S(1)}, u32[]{:S(2)}, u32[]{:S(2)}) async-start(f32[1,5,16,256]{3,0,1,2:T(1,128)} %copy.102), calls=%async_computation.4 | async-start | bytes 163840 | tf_op jit(solution)/shard_map/all_to_all | solution.py:75
  88.8 10.0 %all-to-all-start.5 = ((f32[16,5,1,256]{3,2,1,0:T(1,128)}), f32[16,5,1,256]{3,2,1,0:T(1,128)S(1)}, u32[]{:S(2)}, u32[]{:S(2)}) async-start(f32[16,5,1,256]{3,2,1,0:T(1,128)} %copy.104), calls=%async_computation.5 | async-start | bytes 163840 | tf_op jit(solution)/shard_map/all_to_all | solution.py:61
  99.6 12.2 %collective-permute-start.6 = (f32[1,5,1,256]{3,1,2,0:T(8,128)S(1)}, f32[1,5,1,256]{3,1,2,0:T(8,128)S(1)}, u32[]{:S(2)}, u32[]{:S(2)}) collective-permute-start(f32[1,5,1,256]{3,1,2,0:T(8,128)S(1)} %get-tuple-element.16), channel_id=1, source_target_pairs={{0,16},{16,32},{32,48},{48,64},{64,80},{80,96},{96,112},{112,128},... | collective-permute-start | bytes 15368 | tf_op jit(solution)/shard_map/ppermute | solution.py:17
  105.7 6.2 %collective-permute-start.7 = (f32[1,5,1,256]{3,1,2,0:T(8,128)S(1)}, f32[1,5,1,256]{3,1,2,0:T(8,128)S(1)}, u32[]{:S(2)}, u32[]{:S(2)}) collective-permute-start(f32[1,5,1,256]{3,1,2,0:T(8,128)S(1)} %get-tuple-element.17), channel_id=1, source_target_pairs={{16,0},{32,16},{48,32},{64,48},{80,64},{96,80},{112,96},{128,112},... | collective-permute-start | bytes 15368 | tf_op jit(solution)/shard_map/ppermute | solution.py:19
  108.3 10.0 %all-to-all-start.6 = ((f32[1,5,16,256]{3,0,1,2:T(1,128)}), f32[1,5,16,256]{3,0,1,2:T(1,128)S(1)}, u32[]{:S(2)}, u32[]{:S(2)}) async-start(f32[1,5,16,256]{3,0,1,2:T(1,128)} %copy.106), calls=%async_computation.6 | async-start | bytes 163840 | tf_op jit(solution)/shard_map/all_to_all | solution.py:75
  119.3 10.0 %all-to-all-start.7 = ((f32[16,5,1,256]{3,2,1,0:T(1,128)}), f32[16,5,1,256]{3,2,1,0:T(1,128)S(1)}, u32[]{:S(2)}, u32[]{:S(2)}) async-start(f32[16,5,1,256]{3,2,1,0:T(1,128)} %copy.108), calls=%async_computation.7 | async-start | bytes 163840 | tf_op jit(solution)/shard_map/all_to_all | solution.py:61
  130.3 12.2 %collective-permute-start.8 = (f32[1,5,1,256]{3,1,2,0:T(8,128)S(1)}, f32[1,5,1,256]{3,1,2,0:T(8,128)S(1)}, u32[]{:S(2)}, u32[]{:S(2)}) collective-permute-start(f32[1,5,1,256]{3,1,2,0:T(8,128)S(1)} %get-tuple-element.14), channel_id=1, source_target_pairs={{0,16},{16,32},{32,48},{48,64},{64,80},{80,96},{96,112},{112,128},... | collective-permute-start | bytes 15368 | tf_op jit(solution)/shard_map/ppermute | solution.py:17
  136.3 6.2 %collective-permute-start.9 = (f32[1,5,1,256]{3,1,2,0:T(8,128)S(1)}, f32[1,5,1,256]{3,1,2,0:T(8,128)S(1)}, u32[]{:S(2)}, u32[]{:S(2)}) collective-permute-start(f32[1,5,1,256]{3,1,2,0:T(8,128)S(1)} %get-tuple-element.15), channel_id=1, source_target_pairs={{16,0},{32,16},{48,32},{64,48},{80,64},{96,80},{112,96},{128,112},... | collective-permute-start | bytes 15368 | tf_op jit(solution)/shard_map/ppermute | solution.py:19
  139.0 10.0 %all-to-all-start.8 = ((f32[1,5,16,256]{3,0,1,2:T(1,128)}), f32[1,5,16,256]{3,0,1,2:T(1,128)S(1)}, u32[]{:S(2)}, u32[]{:S(2)}) async-start(f32[1,5,16,256]{3,0,1,2:T(1,128)} %copy.110), calls=%async_computation.8 | async-start | bytes 163840 | tf_op jit(solution)/shard_map/all_to_all | solution.py:75
  150.0 10.0 %all-to-all-start.9 = ((f32[16,5,1,256]{3,2,1,0:T(1,128)}), f32[16,5,1,256]{3,2,1,0:T(1,128)S(1)}, u32[]{:S(2)}, u32[]{:S(2)}) async-start(f32[16,5,1,256]{3,2,1,0:T(1,128)} %copy.112), calls=%async_computation.9 | async-start | bytes 163840 | tf_op jit(solution)/shard_map/all_to_all | solution.py:61
  160.9 12.2 %collective-permute-start.10 = (f32[1,5,1,256]{3,1,2,0:T(8,128)S(1)}, f32[1,5,1,256]{3,1,2,0:T(8,128)S(1)}, u32[]{:S(2)}, u32[]{:S(2)}) collective-permute-start(f32[1,5,1,256]{3,1,2,0:T(8,128)S(1)} %get-tuple-element.12), channel_id=1, source_target_pairs={{0,16},{16,32},{32,48},{48,64},{64,80},{80,96},{96,112},{112,128},... | collective-permute-start | bytes 15368 | tf_op jit(solution)/shard_map/ppermute | solution.py:17
  166.9 6.2 %collective-permute-start.11 = (f32[1,5,1,256]{3,1,2,0:T(8,128)S(1)}, f32[1,5,1,256]{3,1,2,0:T(8,128)S(1)}, u32[]{:S(2)}, u32[]{:S(2)}) collective-permute-start(f32[1,5,1,256]{3,1,2,0:T(8,128)S(1)} %get-tuple-element.13), channel_id=1, source_target_pairs={{16,0},{32,16},{48,32},{64,48},{80,64},{96,80},{112,96},{128,112},... | collective-permute-start | bytes 15368 | tf_op jit(solution)/shard_map/ppermute | solution.py:19
  169.6 10.0 %all-to-all-start.10 = ((f32[1,5,16,256]{3,0,1,2:T(1,128)}), f32[1,5,16,256]{3,0,1,2:T(1,128)S(1)}, u32[]{:S(2)}, u32[]{:S(2)}) async-start(f32[1,5,16,256]{3,0,1,2:T(1,128)} %copy.114), calls=%async_computation.10 | async-start | bytes 163840 | tf_op jit(solution)/shard_map/all_to_all | solution.py:75
  180.6 10.0 %all-to-all-start.11 = ((f32[16,5,1,256]{3,2,1,0:T(1,128)}), f32[16,5,1,256]{3,2,1,0:T(1,128)S(1)}, u32[]{:S(2)}, u32[]{:S(2)}) async-start(f32[16,5,1,256]{3,2,1,0:T(1,128)} %copy.116), calls=%async_computation.11 | async-start | bytes 163840 | tf_op jit(solution)/shard_map/all_to_all | solution.py:61
  191.5 13.3 %collective-permute-start.12 = (f32[1,5,1,256]{3,1,2,0:T(8,128)S(1)}, f32[1,5,1,256]{3,1,2,0:T(8,128)S(1)}, u32[]{:S(2)}, u32[]{:S(2)}) collective-permute-start(f32[1,5,1,256]{3,1,2,0:T(8,128)S(1)} %get-tuple-element.10), channel_id=1, source_target_pairs={{0,16},{16,32},{32,48},{48,64},{64,80},{80,96},{96,112},{112,128},... | collective-permute-start | bytes 15368 | tf_op jit(solution)/shard_map/ppermute | solution.py:17
  197.6 7.2 %collective-permute-start.13 = (f32[1,5,1,256]{3,1,2,0:T(8,128)S(1)}, f32[1,5,1,256]{3,1,2,0:T(8,128)S(1)}, u32[]{:S(2)}, u32[]{:S(2)}) collective-permute-start(f32[1,5,1,256]{3,1,2,0:T(8,128)S(1)} %get-tuple-element.11), channel_id=1, source_target_pairs={{16,0},{32,16},{48,32},{64,48},{80,64},{96,80},{112,96},{128,112},... | collective-permute-start | bytes 15368 | tf_op jit(solution)/shard_map/ppermute | solution.py:19
  201.3 10.0 %all-to-all-start.12 = ((f32[1,5,16,256]{3,0,1,2:T(1,128)}), f32[1,5,16,256]{3,0,1,2:T(1,128)S(1)}, u32[]{:S(2)}, u32[]{:S(2)}) async-start(f32[1,5,16,256]{3,0,1,2:T(1,128)} %copy.118), calls=%async_computation.12 | async-start | bytes 163840 | tf_op jit(solution)/shard_map/all_to_all | solution.py:75
  212.3 10.0 %all-to-all-start.13 = ((f32[16,5,1,256]{3,2,1,0:T(1,128)}), f32[16,5,1,256]{3,2,1,0:T(1,128)S(1)}, u32[]{:S(2)}, u32[]{:S(2)}) async-start(f32[16,5,1,256]{3,2,1,0:T(1,128)} %copy.120), calls=%async_computation.13 | async-start | bytes 163840 | tf_op jit(solution)/shard_map/all_to_all | solution.py:61
where the time goes:
time: 565 us; the launch traced here: 563 us
  blocking collectives  323 us (57%)
  starting transfers between devices  110 us (19%)
  waiting for transfers between devices  82.4 us (15%)
  matrix products  20.4 us (4%)
  local copies, waits for them, and re-layouts  18.4 us (3%)
  other arithmetic  6.17 us (1%)
    psum x2, blocking collectives, gram_sum(): return lax.psum(local, ('cell', 'inst'))  323 us
    all_to_all x7, waiting for transfers between devices, coupled_back(): lax.all_to_all(mixed, 'inst', split_axis=0, concat_axis=2, tiled=True)  43.6 us
    all_to_all x7, waiting for transfers between devices, on_device(): lax.all_to_all(prior, 'inst', split_axis=2, concat_axis=0, tiled=True)  38.8 us
    ppermute x7, starting transfers between devices, with_halo(): lax.ppermute(tail, axis, [(i, (i + 1) % count) for i in range(ends)])  35.8 us
    ppermute x7, starting transfers between devices, with_halo(): lax.ppermute(head, axis, [((i + 1) % count, i) for i in range(ends)])  25.3 us
    all_to_all x7, starting transfers between devices, coupled_back(): lax.all_to_all(mixed, 'inst', split_axis=0, concat_axis=2, tiled=True)  24.6 us
    all_to_all x7, starting transfers between devices, on_device(): lax.all_to_all(prior, 'inst', split_axis=2, concat_axis=0, tiled=True)  24.6 us
    dot_general x28, matrix products, stencil(): jnp.einsum('fe,ierc->ifrc', flux_jac[direction], neighbours[direction], p...  11.9 us
  transfers between devices with their start and end apart: 28, of which 14 were waited for; matrix products, arithmetic and copies ran while one was open for 2% of the time, Pallas kernels for 0%

commit v1 on v0

v1 whole, which is shorter than its diff:
```python
import functools

import jax
import jax.numpy as jnp
import numpy as np
from jax import lax
from jax.experimental import pallas as pl
from jax.experimental.pallas import tpu as pltpu
from jax.sharding import PartitionSpec as P

S = 8
FIELDS = 5
INST = 16
CELLS = 64
HALO = 8
ROWS = 16
COLS = 16
NC = 256
NR = 1024
STATE = FIELDS + 1
PACKED = FIELDS * 2
VMEM = pl.BlockSpec(memory_space=pltpu.VMEM)
SMEM = pl.BlockSpec(memory_space=pltpu.SMEM)
TILE = (8, 128)


def lanes():
    return lax.broadcasted_iota(jnp.int32, TILE, 1)


def sublanes():
    return lax.broadcasted_iota(jnp.int32, TILE, 0)


def two_sum(a, b):
    total = a + b
    part = total - a
    return total, (a - (total - part)) + (b - part)


def split(a):
    scaled = a * 4097.0
    high = scaled - (scaled - a)
    return high, a - high


def two_prod(a, b):
    product = a * b
    a_high, a_low = split(a)
    b_high, b_low = split(b)
    error = ((a_high * b_high - product) + a_high * b_low + a_low * b_high) + a_low * b_low
    return product, error


def pack_kernel(res_ref, gain_ref, below_ref, above_ref, out_ref):
    lane = lanes()
    group = lane // 32
    for field in range(STATE):
        own = res_ref.at[0, field] if field < FIELDS else gain_ref.at[0]
        rows = [below_ref[field], own[0:8, :], own[8:16, :], above_ref[field]]
        chunks = [None] * INST
        for part in range(4):
            left, right = rows[part][:, :128], rows[part][:, 128:]
            for turn in range(8):
                shift = 16 * turn + 8
                rolled_left = pltpu.roll(left, shift, 1)
                rolled_right = pltpu.roll(right, shift, 1)
                first = lane < shift
                for turns, moved in (
                    (turn, jnp.where(first, rolled_right, rolled_left)),
                    (turn + 8, jnp.where(first, rolled_left, rolled_right)),
                ):
                    chunk = (2 * part - turns) % 16
                    old = chunks[chunk]
                    chunks[chunk] = moved if old is None else jnp.where(group == part, moved, old)
        for chunk in range(INST):
            out_ref[chunk, field * 8 : field * 8 + 8, :] = chunks[chunk]


def merge_pair(first, second, mask, shift, axis):
    high = [jnp.where(mask, second[0], first[0]), jnp.where(mask, first[0], second[0])]
    total, error = two_sum(high[0], pltpu.roll(high[1], shift, axis))
    if first[1] is None:
        return total, error
    low = jnp.where(mask, second[1], first[1]) + pltpu.roll(
        jnp.where(mask, first[1], second[1]), shift, axis
    )
    return total, error + low


def fold_pair(pair, shift, axis):
    total, error = two_sum(pair[0], pltpu.roll(pair[0], shift, axis))
    return total, error + (pair[1] + pltpu.roll(pair[1], shift, axis))


def step_kernel(table, in_ref, jac_ref, omega_ref, shift_ref, out_ref, vec_ref, coef_ref, mix_ref, gain_ref):
    lane, sub = lanes(), sublanes()
    cell, inst = lax.axis_index("cell"), lax.axis_index("inst")
    row = cell * ROWS - HALO + (lane // 32) * 8 + sub
    col = inst * COLS - HALO + lane % 32
    inside = (row >= 0) & (row < NR) & (col >= 0) & (col < NC)
    first_row, last_row = sub == 0, sub == 7
    for d in range(4):
        for f in range(FIELDS):
            for e in range(FIELDS):
                coef_ref[(d * FIELDS + f) * FIELDS + e] = jnp.full(TILE, jac_ref[d, f, e])
    for i in range(INST):
        for f in range(FIELDS):
            vec_ref[0, i, f] = jnp.where(inside, in_ref[i, f * 8 : f * 8 + 8, :], 0.0)
        gain_ref[i] = in_ref[i, FIELDS * 8 : FIELDS * 8 + 8, :]
    weights = [None] + [jnp.full(TILE, omega_ref[0] * table[d]) for d in range(1, 9)]

    def step(n, carry):
        shift = shift_ref[n]
        for f in range(FIELDS):
            v = [vec_ref[n, i, f] for i in range(INST)]
            mixed = [weights[8] * v[(i + 8) % INST] for i in range(INST)]
            for i in range(8):
                for d in range(1, 8):
                    gap = v[(i - d) % INST] - v[(i + d) % INST]
                    mixed[i] = mixed[i] + weights[d] * gap
                    mixed[i + 8] = mixed[i + 8] - weights[8 - d] * gap
            for i in range(INST):
                mix_ref[i, f] = mixed[i]
        for pair in range(0, INST, 2):
            members = (pair, pair + 1)
            near, center = {}, {}
            for i in members:
                for e in range(FIELDS):
                    v = vec_ref[n, i, e]
                    center[i, e] = v
                    down = pltpu.roll(v, 1, 0)
                    up = pltpu.roll(v, 7, 0)
                    near[i, 0, e] = jnp.where(first_row, pltpu.roll(down, 32, 1), down)
                    near[i, 1, e] = jnp.where(last_row, pltpu.roll(up, 96, 1), up)
                    near[i, 2, e] = pltpu.roll(v, 1, 1)
                    near[i, 3, e] = pltpu.roll(v, 127, 1)
            for f in range(FIELDS):
                total = {i: mix_ref[i, f] + (gain_ref[i] - shift) * center[i, f] for i in members}
                for d in range(4):
                    for e in range(FIELDS):
                        c = coef_ref[(d * FIELDS + f) * FIELDS + e]
                        for i in members:
                            total[i] = total[i] - c * near[i, d, e]
                for i in members:
                    vec_ref[n + 1, i, f] = jnp.where(inside, total[i], 0.0)
        return carry

    lax.fori_loop(0, S - 1, step, 0)

    pairs = [(a, b) for a in range(S) for b in range(a, S)]
    seg = lane // 16

    def gather(i, sums):
        sums = list(sums)
        for f in range(FIELDS):
            v = [vec_ref[s, i, f] for s in range(S)]
            for p, (a, b) in enumerate(pairs):
                sums[p] = sums[p] + v[a] * v[b]
            for half in range(2):
                a, b, c, d = v[4 * half : 4 * half + 4]
                a, b, c, d = pltpu.roll(a, 120, 1), pltpu.roll(b, 8, 1), pltpu.roll(c, 56, 1), pltpu.roll(d, 72, 1)
                tile = jnp.where(
                    (seg == 2) | (seg == 4),
                    a,
                    jnp.where((seg == 3) | (seg == 5), b, jnp.where((seg == 0) | (seg == 6), c, d)),
                )
                out_ref[i, (2 * f + half) * 8 : (2 * f + half) * 8 + 8, :] = tile
        return tuple(sums)

    sums = lax.fori_loop(0, INST, gather, tuple(jnp.zeros(TILE, jnp.float32) for _ in pairs))
    column = lane % 32
    own = (lane >= 32) & (lane < 96) & (column >= HALO) & (column < HALO + COLS)
    entry = {}
    for p, (a, b) in enumerate(pairs):
        entry[a, b] = entry[b, a] = (jnp.where(own, sums[p], 0.0), None)
    columns = []
    for b in range(S):
        level = [entry[a, b] for a in range(S)]
        for bit in (1, 2, 4):
            mask = (sub & bit) != 0
            level = [merge_pair(level[2 * q], level[2 * q + 1], mask, bit, 0) for q in range(len(level) // 2)]
        columns.append(level[0])
    for bit in (1, 2, 4):
        mask = (lane & bit) != 0
        columns = [merge_pair(columns[2 * q], columns[2 * q + 1], mask, bit, 1) for q in range(len(columns) // 2)]
    high, low = columns[0]
    for i in range(INST):
        out_ref[i, PACKED * 8 : PACKED * 8 + 8, :] = high
        out_ref[i, PACKED * 8 + 8 : PACKED * 8 + 16, :] = low


def gram_kernel(in_ref, out_ref):
    lane, sub = lanes(), sublanes()
    level = [
        (in_ref[i, PACKED * 8 : PACKED * 8 + 8, :], in_ref[i, PACKED * 8 + 8 : PACKED * 8 + 16, :])
        for i in range(INST)
    ]
    while len(level) > 1:
        merged = []
        for q in range(0, len(level), 2):
            total, error = two_sum(level[q][0], level[q + 1][0])
            merged.append((total, error + (level[q][1] + level[q + 1][1])))
        level = merged
    pair = level[0]
    for shift in (8, 16, 32, 64):
        pair = fold_pair(pair, shift, 1)
    slot = lane // 8
    row = jnp.where(slot == sub, pair[0], jnp.where(slot == sub + 8, pair[1], 0.0))
    row = jnp.broadcast_to(jnp.sum(row, axis=0, keepdims=True), TILE)
    for q in range(CELLS // 8):
        out_ref[q * 8 : q * 8 + 8, :] = row


def unpack_kernel(in_ref, out_ref):
    seg = lanes() // 16
    places = ((2, 1), (3, 1), (0, 0), (1, 0), (0, 1), (1, 1), (2, 0), (3, 0))
    for f in range(FIELDS):
        for half in range(2):
            for wide in range(2):
                start = (2 * f + half) * 8
                tiles = [in_ref[8 * wide + q, start : start + 8, :] for q in range(8)]
                for bit in (1, 2, 4):
                    off = (seg & bit) == 0
                    for q in range(8):
                        if q & bit:
                            continue
                        a, b = tiles[q], tiles[q + bit]
                        tiles[q] = jnp.where(off, a, pltpu.roll(b, 16 * bit, 1))
                        tiles[q + bit] = jnp.where(off, pltpu.roll(a, 128 - 16 * bit, 1), b)
                for q, (s, part) in enumerate(places):
                    out_ref[4 * half + s, 0, f, 8 * part : 8 * part + 8, 128 * wide : 128 * wide + 128] = tiles[q]


def lane_of(x, k):
    return jnp.broadcast_to(x[:, k : k + 1], TILE)


def row_of(x, k):
    return jnp.broadcast_to(x[k : k + 1, :], TILE)


def factor(high, low):
    lane, sub = lanes(), sublanes()
    high = jnp.where(lane < S, high, jnp.where(lane == sub + S, 1.0, 0.0))
    lower, inverse = jnp.zeros(TILE, jnp.float32), jnp.zeros(TILE, jnp.float32)
    for k in range(S):
        full = high if low is None else high + jnp.where(lane < S, low, 0.0)
        pivot = jnp.broadcast_to(full[k : k + 1, k : k + 1], TILE)
        scale = 1.0 / jnp.sqrt(pivot)
        left = jnp.where(sub >= k, lane_of(full, k) * scale, 0.0)
        right = jnp.where((lane >= k) & (lane < 2 * S), row_of(full, k) * scale, 0.0)
        lower = jnp.where(lane == k, left, lower)
        inverse = jnp.where(sub == k, right, inverse)
        if low is None:
            high = high - left * right
        else:
            product, error = two_prod(left, right)
            high, rest = two_sum(high, -product)
            low = low + (rest - error)
    inverse = jnp.where(lane < S, pltpu.roll(inverse, 128 - S, 1), 0.0)
    return lower, inverse, None if low is None else jnp.where(lane < S, high + low, 0.0)


def small_dot(a, b, flip=False):
    dims = (((1,), (1 if flip else 0,)), ((), ()))
    return lax.dot_general(
        a if flip else a[:, :S], b, dims, precision=lax.Precision.HIGHEST, preferred_element_type=jnp.float32
    )


def finish_kernel(rows_ref, vec_ref, out_ref, factor_ref):
    lane, sub = lanes(), sublanes()
    level = [(rows_ref[q * 8 : q * 8 + 8, :], jnp.zeros(TILE, jnp.float32)) for q in range(CELLS // 8)]
    while len(level) > 1:
        merged = []
        for q in range(0, len(level), 2):
            total, error = two_sum(level[q][0], level[q + 1][0])
            merged.append((total, error + (level[q][1] + level[q + 1][1])))
        level = merged
    pair = level[0]
    for shift in (1, 2, 4):
        pair = fold_pair(pair, shift, 0)
    high, low = pair[0], pair[1] + pltpu.roll(pair[0], 64, 1)
    for bit in (1, 2, 4):
        mask = (sub & bit) != 0
        high = jnp.where(mask, pltpu.roll(high, 128 - 8 * bit, 1), high)
        low = jnp.where(mask, pltpu.roll(low, 128 - 8 * bit, 1), low)
    lower_one, inverse_one, rest = factor(high, low)
    half = small_dot(inverse_one, rest)
    square = jnp.zeros(TILE, jnp.float32)
    flipped = jnp.transpose(jnp.concatenate([inverse_one] * 16, axis=0))[:S, :]
    flipped = jnp.where(lane < S, flipped, 0.0)
    square = small_dot(half, flipped)
    gram_two = square + jnp.where(lane == sub, 1.0, 0.0)
    lower_two, inverse_two, _ = factor(gram_two, None)
    factor_ref[...] = small_dot(lower_one, lower_two)[:, :S]
    inverse = small_dot(inverse_two, inverse_one)
    weight = {(a, b): jnp.broadcast_to(inverse[a : a + 1, b : b + 1], TILE) for a in range(S) for b in range(a + 1)}
    for f in range(FIELDS):
        for part in range(2):
            for wide in range(2):
                place = (0, f, pl.ds(8 * part, 8), pl.ds(128 * wide, 128))
                v = [vec_ref[(s, *place)] for s in range(S)]
                for a in range(S):
                    total = weight[a, 0] * v[0]
                    for b in range(1, a + 1):
                        total = total + weight[a, b] * v[b]
                    out_ref[(a, *place)] = total


def call(kernel, out_shape, in_specs, args, scratch=(), flops=10**6):
    shapes = jax.tree.map(lambda s: jax.ShapeDtypeStruct(s, jnp.float32), out_shape, is_leaf=lambda s: isinstance(s[0], int))
    return pl.pallas_call(
        kernel,
        out_shape=shapes,
        in_specs=in_specs,
        out_specs=jax.tree.map(lambda _: VMEM, shapes),
        scratch_shapes=scratch,
        compiler_params=pltpu.CompilerParams(vmem_limit_bytes=40 * 2**20),
        cost_estimate=pl.CostEstimate(flops=flops, transcendentals=0, bytes_accessed=2 * 10**6),
    )(*args)


def coupling_table():
    table = []
    for d in range(9):
        angle = np.float32(np.pi) * np.float32(d) / np.float32(INST)
        sign = -1.0 if d % 2 else 1.0
        table.append(float(np.float32(0.5 * sign * np.cos(angle) / np.sin(angle))) if d else 0.0)
    return tuple(table)


def on_device(residual, diag_gain, flux_jac, omega, shifts):
    def edge(rows):
        return jnp.concatenate([residual[0, :, rows, :], diag_gain[:, rows, :]], axis=0)

    ends = CELLS - 1
    below = lax.ppermute(edge(slice(8, 16)), "cell", [(i, i + 1) for i in range(ends)])
    above = lax.ppermute(edge(slice(0, 8)), "cell", [(i + 1, i) for i in range(ends)])
    chunks = call(pack_kernel, (INST, STATE * 8, 128), [VMEM] * 4, (residual, diag_gain, below, above))
    patches = lax.all_to_all(chunks, "inst", 0, 0, tiled=True)
    vectors = call(
        functools.partial(step_kernel, coupling_table()),
        (INST, PACKED * 8 + 16, 128),
        [VMEM, SMEM, SMEM, SMEM],
        (patches, flux_jac, omega, shifts),
        scratch=[
            pltpu.VMEM((S, INST, FIELDS, *TILE), jnp.float32),
            pltpu.VMEM((4 * FIELDS * FIELDS, *TILE), jnp.float32),
            pltpu.VMEM((INST, FIELDS, *TILE), jnp.float32),
            pltpu.VMEM((INST, *TILE), jnp.float32),
        ],
        flops=10**8,
    )
    back = lax.all_to_all(vectors, "inst", 0, 0, tiled=True)
    rows = lax.all_to_all(call(gram_kernel, (CELLS, 128), [VMEM], (back,)), "cell", 0, 0, tiled=True)
    basis = call(unpack_kernel, (S, 1, FIELDS, ROWS, NC), [VMEM], (back,))
    ortho, factor_l = call(
        finish_kernel, ((S, 1, FIELDS, ROWS, NC), (S, S)), [VMEM, VMEM], (rows, basis)
    )
    return (ortho, factor_l.T)


def solution(mesh):
    in_specs = (P("inst", None, "cell", None), P("inst", "cell", None), P(), P(), P())
    out_specs = (P(None, "inst", None, "cell", None), P())
    return jax.shard_map(
        on_device, mesh=mesh, in_specs=in_specs, out_specs=out_specs, check_vma=False
    )
```

time: 565 us -> 114 us (0.20)
  blocking collectives: 323 us -> 15.7 us
  starting transfers between devices: 110 us -> 47.7 us
  waiting for transfers between devices: 82.4 us -> 29.7 us
  matrix products: 20.4 us -> 0 us
  Pallas kernels: 0 us -> 16.7 us
  local copies, waits for them, and re-layouts: 18.4 us -> 2.21 us
  other arithmetic: 6.17 us -> 0.01 us
    psum x2 -> x0, blocking collectives: 323 us -> none  [gram_sum(): return lax.psum(local, ('cell', 'inst'))]
    all_to_all x14 -> x2, waiting for transfers between devices: 82.3 us -> 28.8 us  [the longest x1 20.2 us: on_device(): lax.all_to_all(call(gram_kernel, (CELLS, 128), [VMEM], (back,)), 'cell',...]
    ppermute x14 -> x2, starting transfers between devices: 61.1 us -> 17.4 us  [the longest x1 12.4 us: on_device(): lax.ppermute(edge(slice(0, 8)), 'cell', [(i + 1, i) for i in range(ends)])]
    dot_general x38 -> x0, matrix products: 18.9 us -> none  [the longest x28 11.9 us: stencil(): jnp.einsum('fe,ierc->ifrc', flux_jac[direction], neighbours[direction], p...]
    all_to_all x14 -> x2, starting transfers between devices: 49.1 us -> 30.2 us  [the longest x1 26.6 us: on_device(): lax.all_to_all(call(gram_kernel, (CELLS, 128), [VMEM], (back,)), 'cell',...]
    pallas_call x0 -> x5, Pallas kernels: none -> 16.7 us  [call(): pl.pallas_call(kernel, out_shape=shapes, in_specs=in_specs, out_specs=jax...]
    all_to_all x0 -> x1, blocking collectives: none -> 15.7 us  [on_device(): back = lax.all_to_all(vectors, 'inst', 0, 0, tiled=True)]
  transfers between devices with their start and end apart: 28 -> 4, of which waited for: 14 -> 3; matrix products, arithmetic and copies ran while one was open for 2% -> 0% of each run, Pallas kernels for 0% -> 2%
where the time goes in v1:
time: 114 us; the launch traced here: 113 us
  starting transfers between devices  47.7 us (42%)
  waiting for transfers between devices  29.7 us (26%)
  Pallas kernels  16.7 us (15%)
  blocking collectives  15.7 us (14%)
  local copies, waits for them, and re-layouts  2.21 us (2%)
  between operations  1.37 us (1%)
    all_to_all x1, starting transfers between devices, on_device(): lax.all_to_all(call(gram_kernel, (CELLS, 128), [VMEM], (back,)), 'cell',...  26.6 us
    all_to_all x1, waiting for transfers between devices, on_device(): lax.all_to_all(call(gram_kernel, (CELLS, 128), [VMEM], (back,)), 'cell',...  20.2 us
    pallas_call x5, Pallas kernels, call(): pl.pallas_call(kernel, out_shape=shapes, in_specs=in_specs, out_specs=jax...  16.7 us
    all_to_all x1, blocking collectives, on_device(): back = lax.all_to_all(vectors, 'inst', 0, 0, tiled=True)  15.7 us
    ppermute x1, starting transfers between devices, on_device(): lax.ppermute(edge(slice(0, 8)), 'cell', [(i + 1, i) for i in range(ends)])  12.4 us
    all_to_all x1, waiting for transfers between devices, on_device(): patches = lax.all_to_all(chunks, 'inst', 0, 0, tiled=True)  8.58 us
    ppermute x1, starting transfers between devices, on_device(): lax.ppermute(edge(slice(8, 16)), 'cell', [(i, i + 1) for i in range(ends)])  5.06 us
    all_to_all x1, starting transfers between devices, on_device(): patches = lax.all_to_all(chunks, 'inst', 0, 0, tiled=True)  3.68 us
  transfers between devices with their start and end apart: 4, of which 3 were waited for; matrix products, arithmetic and copies ran while one was open for 0% of the time, Pallas kernels for 2%

profile of v1, /device:TPU:1, one launch (start us, length us, event | category | flops | bytes accessed | tf_op | source)
XLA Modules:
  0.0 113.4 jit_solution(953770284659027955)
XLA Ops:
  0.6 0.7 fusion
  1.3 0.8 slice_bitcast_fusion
  2.2 0.0 copy-start
  2.2 5.1 %collective-permute-start = (f32[6,8,256]{2,1,0:T(8,128)S(1)}, f32[6,8,256]{2,1,0:T(8,128)S(1)}, u32[]{:S(2)}, u32[]{:S(2)}) collective-permute-start(f32[6,8,256]{2,1,0:T(8,128)S(1)} %pad_maximum_fusion), channel_id=1, source_target_pairs={{0,16},{16,32},{32,48},{48,64},{64,80},{80,96},{96,112},{112,128},... | collective-permute-start | bytes 147464 | tf_op jit(solution)/shard_map/ppermute | solution.py:339
  7.2 0.0 copy-start.1
  7.3 12.4 %collective-permute-start.1 = (f32[6,8,256]{2,1,0:T(8,128)S(1)}, f32[6,8,256]{2,1,0:T(8,128)S(1)}, u32[]{:S(2)}, u32[]{:S(2)}) collective-permute-start(f32[6,8,256]{2,1,0:T(8,128)S(1)} %pad_maximum_fusion.1), channel_id=1, source_target_pairs={{16,0},{32,16},{48,32},{64,48},{80,64},{96,80},{112,96},{128,112},... | collective-permute-start | bytes 147464 | tf_op jit(solution)/shard_map/ppermute | solution.py:340
  19.7 0.0 collective-permute-done.below_ref
  19.7 0.8 collective-permute-done.1.above_ref
  20.5 0.0 copy-done
  20.5 0.0 copy-done.1
  20.5 1.2 %shard_map.68 = f32[16,48,128]{2,1,0:T(8,128)} custom-call(f32[1,5,16,256]{3,2,1,0:T(8,128)S(1)} %copy-done, f32[1,16,256]{2,1,0:T(8,128)S(1)} %copy-done.1, f32[6,8,256]{2,1,0:T(8,128)S(1)} %collective-permute-done.below_ref, f32[6,8,256]{2,1,0:T(8,128)S(1)} %collective-permute-done.1.above_ref), custom_call_target="tpu_custom_call" | custom-call | flops 1000000 | bytes 2000000 | tf_op jit(solution)/shard_map/pallas_call | solution.py:314
  21.7 0.0 copy-start.3
  21.7 3.7 %all-to-all-start = ((f32[16,48,128]{2,1,0:T(8,128)}), f32[16,48,128]{2,1,0:T(8,128)S(1)}, u32[]{:S(2)}, u32[]{:S(2)}) async-start(f32[16,48,128]{2,1,0:T(8,128)} %shard_map.68), calls=%async_computation | async-start | bytes 786432 | tf_op jit(solution)/shard_map/all_to_all | solution.py:342
  26.1 0.0 copy-done.3
  26.1 0.0 copy-start.2
  26.1 8.6 %all-to-all-done.in_ref = f32[16,48,128]{2,1,0:T(8,128)S(1)} async-done(((f32[16,48,128]{2,1,0:T(8,128)}), f32[16,48,128]{2,1,0:T(8,128)S(1)}, u32[]{:S(2)}, u32[]{:S(2)}) %all-to-all-start) | async-done | bytes 393248 | tf_op jit(solution)/shard_map/all_to_all | solution.py:342
  34.7 0.0 copy-done.2
  34.7 8.6 %shard_map.69 = f32[16,96,128]{2,1,0:T(8,128)S(1)} custom-call(f32[16,48,128]{2,1,0:T(8,128)S(1)} %all-to-all-done.in_ref, f32[4,5,5]{2,1,0:T(8,128)S(1)} %copy.9.jac_ref, f32[1]{0:T(128)S(6)} %copy.12.omega_ref, f32[7]{0:T(128)S(1)} %copy-done.2), custom_call_target="tpu_custom_call" | custom-call | flops 100000000 | bytes 2000000 | tf_op jit(solution)/shard_map/pallas_call | solution.py:314
  43.3 15.7 %all_to_all.21.in_ref = f32[16,96,128]{2,1,0:T(8,128)S(1)} all-to-all(f32[16,96,128]{2,1,0:T(8,128)S(1)} %shard_map.69), channel_id=1, replica_groups=mesh['cell'=64,'inst'=16] {'inst'}, dimensions={0} | all-to-all | bytes 1572864 | tf_op jit(solution)/shard_map/all_to_all | solution.py:356
  59.0 0.9 shard_map.70
  59.9 26.6 %all-to-all-start.2 = ((f32[64,1,128]{2,1,0:T(1,128)}), f32[64,1,128]{2,1,0:T(1,128)S(1)}, u32[]{:S(2)}, u32[]{:S(2)}) async-start(f32[64,1,128]{2,1,0:T(1,128)} %bitcast.3), calls=%async_computation.2 | async-start | bytes 65536 | tf_op jit(solution)/shard_map/all_to_all | solution.py:357
  86.5 2.1 %shard_map.71.vec_ref = f32[8,1,5,16,256]{4,3,2,1,0:T(8,128)S(1)} custom-call(f32[16,96,128]{2,1,0:T(8,128)S(1)} %all_to_all.21.in_ref), custom_call_target="tpu_custom_call" | custom-call | flops 1000000 | bytes 2000000 | tf_op jit(solution)/shard_map/pallas_call | solution.py:314
  88.6 20.2 %all-to-all-done.2 = f32[64,1,128]{2,1,0:T(1,128)S(1)} async-done(((f32[64,1,128]{2,1,0:T(1,128)}), f32[64,1,128]{2,1,0:T(1,128)S(1)}, u32[]{:S(2)}, u32[]{:S(2)}) %all-to-all-start.2) | async-done | bytes 32800 | tf_op jit(solution)/shard_map/all_to_all | solution.py:357
  108.8 3.9 %shard_map.72 = (f32[8,1,5,16,256]{4,3,2,1,0:T(8,128)}, f32[8,8]{1,0:T(8,128)S(1)}) custom-call(f32[64,128]{1,0:T(8,128)S(1)} %bitcast.9, f32[8,1,5,16,256]{4,3,2,1,0:T(8,128)S(1)} %shard_map.71.vec_ref), custom_call_target="tpu_custom_call" | custom-call | flops 1000000 | bytes 2000000 | tf_op jit(solution)/shard_map/pallas_call | solution.py:314
  112.7 0.7 copy.11
  (3 shorter events, 0.0 us)
Async XLA Ops:
  2.2 18.4 %copy-start = (f32[1,5,16,256]{3,2,1,0:T(8,128)S(1)}, f32[1,5,16,256]{3,2,1,0:T(8,128)}, u32[]{:S(2)}) copy-start(f32[1,5,16,256]{3,2,1,0:T(8,128)} %res_ref.1) | copy-start | bytes 245764
  2.2 17.5 %collective-permute-start = (f32[6,8,256]{2,1,0:T(8,128)S(1)}, f32[6,8,256]{2,1,0:T(8,128)S(1)}, u32[]{:S(2)}, u32[]{:S(2)}) collective-permute-start(f32[6,8,256]{2,1,0:T(8,128)S(1)} %pad_maximum_fusion), channel_id=1, source_target_pairs={{0,16},{16,32},{32,48},{48,64},{64,80},{80,96},{96,112},{112,128},... | collective-permute-start | bytes 147464 | tf_op jit(solution)/shard_map/ppermute | solution.py:339
  7.2 13.3 %copy-start.1 = (f32[1,16,256]{2,1,0:T(8,128)S(1)}, f32[1,16,256]{2,1,0:T(8,128)}, u32[]{:S(2)}) copy-start(f32[1,16,256]{2,1,0:T(8,128)} %gain_ref.1) | copy-start | bytes 49156
  7.3 13.3 %collective-permute-start.1 = (f32[6,8,256]{2,1,0:T(8,128)S(1)}, f32[6,8,256]{2,1,0:T(8,128)S(1)}, u32[]{:S(2)}, u32[]{:S(2)}) collective-permute-start(f32[6,8,256]{2,1,0:T(8,128)S(1)} %pad_maximum_fusion.1), channel_id=1, source_target_pairs={{16,0},{32,16},{48,32},{64,48},{80,64},{96,80},{112,96},{128,112},... | collective-permute-start | bytes 147464 | tf_op jit(solution)/shard_map/ppermute | solution.py:340
  21.7 4.3 %copy-start.3 = (f32[4,5,5]{2,0,1:T(4,128)S(1)}, f32[4,5,5]{2,0,1:T(4,128)}, u32[]{:S(2)}) copy-start(f32[4,5,5]{2,0,1:T(4,128)} %param.7) | copy-start | bytes 1204
  21.7 12.9 %all-to-all-start = ((f32[16,48,128]{2,1,0:T(8,128)}), f32[16,48,128]{2,1,0:T(8,128)S(1)}, u32[]{:S(2)}, u32[]{:S(2)}) async-start(f32[16,48,128]{2,1,0:T(8,128)} %shard_map.68), calls=%async_computation | async-start | bytes 786432 | tf_op jit(solution)/shard_map/all_to_all | solution.py:342
  26.1 8.6 %copy-start.2 = (f32[7]{0:T(128)S(1)}, f32[7]{0:T(128)}, u32[]{:S(2)}) copy-start(f32[7]{0:T(128)} %shift_ref.1) | copy-start | bytes 88
  59.9 48.9 %all-to-all-start.2 = ((f32[64,1,128]{2,1,0:T(1,128)}), f32[64,1,128]{2,1,0:T(1,128)S(1)}, u32[]{:S(2)}, u32[]{:S(2)}) async-start(f32[64,1,128]{2,1,0:T(1,128)} %bitcast.3), calls=%async_computation.2 | async-start | bytes 65536 | tf_op jit(solution)/shard_map/all_to_all | solution.py:357

commit v2 on v1

v2 whole, which is shorter than its diff:
```python
import functools

import jax
import jax.numpy as jnp
import numpy as np
from jax import lax
from jax.experimental import pallas as pl
from jax.experimental.pallas import tpu as pltpu
from jax.sharding import PartitionSpec as P

S = 8
FIELDS = 5
INST = 16
CELLS = 64
HALO = 8
ROWS = 16
COLS = 16
NC = 256
NR = 1024
STATE = FIELDS + 1
VMEM = pl.BlockSpec(memory_space=pltpu.VMEM)
SMEM = pl.BlockSpec(memory_space=pltpu.SMEM)
TILE = (8, 128)


def lanes():
    return lax.broadcasted_iota(jnp.int32, TILE, 1)


def sublanes():
    return lax.broadcasted_iota(jnp.int32, TILE, 0)


def two_sum(a, b):
    total = a + b
    part = total - a
    return total, (a - (total - part)) + (b - part)


def split(a):
    scaled = a * 4097.0
    high = scaled - (scaled - a)
    return high, a - high


def pack_kernel(res_ref, gain_ref, below_ref, above_ref, out_ref):
    lane = lanes()
    group = lane // 32
    for field in range(STATE):
        own = res_ref.at[0, field] if field < FIELDS else gain_ref.at[0]
        rows = [below_ref[field], own[0:8, :], own[8:16, :], above_ref[field]]
        chunks = [None] * INST
        for part in range(4):
            left, right = rows[part][:, :128], rows[part][:, 128:]
            for turn in range(8):
                shift = 16 * turn + 8
                rolled_left = pltpu.roll(left, shift, 1)
                rolled_right = pltpu.roll(right, shift, 1)
                first = lane < shift
                for turns, moved in (
                    (turn, jnp.where(first, rolled_right, rolled_left)),
                    (turn + 8, jnp.where(first, rolled_left, rolled_right)),
                ):
                    chunk = (2 * part - turns) % 16
                    old = chunks[chunk]
                    chunks[chunk] = moved if old is None else jnp.where(group == part, moved, old)
        for chunk in range(INST):
            out_ref[chunk, field * 8 : field * 8 + 8, :] = chunks[chunk]


def merge_pair(first, second, mask, shift, axis):
    high = [jnp.where(mask, second[0], first[0]), jnp.where(mask, first[0], second[0])]
    total, error = two_sum(high[0], pltpu.roll(high[1], shift, axis))
    if first[1] is None:
        return total, error
    low = jnp.where(mask, second[1], first[1]) + pltpu.roll(
        jnp.where(mask, first[1], second[1]), shift, axis
    )
    return total, error + low


def fold_pair(pair, shift, axis):
    total, error = two_sum(pair[0], pltpu.roll(pair[0], shift, axis))
    return total, error + (pair[1] + pltpu.roll(pair[1], shift, axis))


def rotations(table):
    c = [0.0, *table]
    plus = [None] + [c[d] - c[8 - d] for d in (1, 2, 3)]
    minus = [None] + [(c[d] + c[8 - d]) / 2 for d in (1, 2, 3, 4)]
    return ((plus[1] - plus[3]) / 4, (plus[1] + plus[3]) / 4, plus[2] / 2, *minus[1:])


def gap(x, i, d):
    n = len(x)
    before, after = x[(i - d) % n], x[(i + d) % n]
    if i - d < 0:
        return before + after, -1
    return (before - after if i + d < n else before + after), 1


def turned(x, i, weights):
    n = len(x)
    total = None
    for d, weight in enumerate(weights, 1):
        if 2 * d < n:
            value, sign = gap(x, i, d)
        else:
            value, sign = x[(i - d) % n], (1 if i >= d else -1)
        term = weight * value
        if total is None:
            total = term if sign > 0 else -term
        else:
            total = total + term if sign > 0 else total - term
    return total


def coupled(v, weights):
    inner, first, second = weights[:3]
    plus = [v[i] + v[i + 8] for i in range(8)]
    minus = [v[i] - v[i + 8] for i in range(8)]
    sums = [plus[i] + plus[i + 4] for i in range(4)]
    gaps = [plus[i] - plus[i + 4] for i in range(4)]
    even, odd = inner * (sums[3] - sums[1]), inner * (sums[0] - sums[2])
    circle = [even, odd, -even, -odd]
    twisted = [turned(gaps, i, (first, second)) for i in range(4)]
    outer = [circle[i] + twisted[i] for i in range(4)] + [circle[i] - twisted[i] for i in range(4)]
    flipped = [turned(minus, i, weights[3:]) for i in range(8)]
    return [outer[i] + flipped[i] for i in range(8)] + [outer[i] - flipped[i] for i in range(8)]


SLOTS = ((2, 4), (3, 5), (6, 0), (7, 1))
OFFSETS = (0, 1, 4, 5)
MOVES = {(0, 0): (0, 1, 4, 5), (1, 1): (0, 1, 4, 5), (0, 1): (0, 1, 3, 4, 5, 7)}


def in_slot(seg, q):
    return (seg == SLOTS[q][0]) | (seg == SLOTS[q][1])


def pack_four(seg, a, b, c, d):
    a, b, c, d = pltpu.roll(a, 120, 1), pltpu.roll(b, 8, 1), pltpu.roll(c, 56, 1), pltpu.roll(d, 72, 1)
    return jnp.where(in_slot(seg, 0), a, jnp.where(in_slot(seg, 1), b, jnp.where(in_slot(seg, 2), c, d)))


def step_kernel(rotation, in_ref, jac_ref, omega_ref, shift_ref, out_ref, vec_ref, coef_ref, mix_ref, gain_ref):
    lane, sub = lanes(), sublanes()
    seg = lane // 16
    cell, inst = lax.axis_index("cell"), lax.axis_index("inst")
    row = cell * ROWS - HALO + (lane // 32) * 8 + sub
    col = inst * COLS - HALO + lane % 32
    inside = (row >= 0) & (row < NR) & (col >= 0) & (col < NC)
    first_row, last_row = sub == 0, sub == 7
    for d in range(4):
        for f in range(FIELDS):
            for e in range(FIELDS):
                coef_ref[(d * FIELDS + f) * FIELDS + e] = jnp.full(TILE, jac_ref[d, f, e])
    for i in range(INST):
        for f in range(FIELDS):
            vec_ref[0, i, f] = jnp.where(inside, in_ref[i, f * 8 : f * 8 + 8, :], 0.0)
        gain_ref[i] = in_ref[i, FIELDS * 8 : FIELDS * 8 + 8, :]
    weights = [jnp.full(TILE, omega_ref[0] * w) for w in rotation]

    def step(n, carry):
        shift = shift_ref[n]
        for f in range(FIELDS):
            mixed = coupled([vec_ref[n, i, f] for i in range(INST)], weights)
            for i in range(INST):
                mix_ref[i, f] = mixed[i]
        for pair in range(0, INST, 2):
            members = (pair, pair + 1)
            near, center = {}, {}
            for i in members:
                for e in range(FIELDS):
                    v = vec_ref[n, i, e]
                    center[i, e] = v
                    down = pltpu.roll(v, 1, 0)
                    up = pltpu.roll(v, 7, 0)
                    near[i, 0, e] = jnp.where(first_row, pltpu.roll(down, 32, 1), down)
                    near[i, 1, e] = jnp.where(last_row, pltpu.roll(up, 96, 1), up)
                    near[i, 2, e] = pltpu.roll(v, 1, 1)
                    near[i, 3, e] = pltpu.roll(v, 127, 1)
            for f in range(FIELDS):
                total = {i: mix_ref[i, f] + (gain_ref[i] - shift) * center[i, f] for i in members}
                for d in range(4):
                    for e in range(FIELDS):
                        c = coef_ref[(d * FIELDS + f) * FIELDS + e]
                        for i in members:
                            total[i] = total[i] - c * near[i, d, e]
                for i in members:
                    vec_ref[n + 1, i, f] = jnp.where(inside, total[i], 0.0)
        return carry

    lax.fori_loop(0, S - 1, step, 0)

    keys = [(x, y, move) for (x, y), moves in MOVES.items() for move in moves]

    def gather(i, sums):
        sums = list(sums)
        tiles = {}
        for f in range(FIELDS):
            for x in range(2):
                tiles[x, f] = pack_four(seg, *[vec_ref[4 * x + q, i, f] for q in range(4)])
            moved = {}
            for p, (x, y, move) in enumerate(keys):
                if (y, move) not in moved:
                    moved[y, move] = pltpu.roll(tiles[y, f], 16 * move, 1) if move else tiles[y, f]
                sums[p] = sums[p] + tiles[x, f] * moved[y, move]
            out_ref[i, (4 + f) * 8 : (4 + f) * 8 + 8, :] = tiles[1, f]
        for f in range(4):
            tile = tiles[0, f]
            if f < 3:
                move = (OFFSETS[0] - OFFSETS[f + 1]) % 8
                tile = jnp.where(in_slot(seg, 0), pltpu.roll(tiles[0, 4], 16 * move, 1), tile)
            out_ref[i, f * 8 : f * 8 + 8, :] = tile
        return tuple(sums)

    sums = lax.fori_loop(0, INST, gather, tuple(jnp.zeros(TILE, jnp.float32) for _ in keys))
    entry = {}
    for p, (x, y, move) in enumerate(keys):
        for q in range(4):
            for r in range(4):
                a, b = 4 * x + q, 4 * y + r
                if (OFFSETS[q] - OFFSETS[r]) % 8 == move and (a, b) not in entry:
                    entry[a, b] = entry[b, a] = (jnp.where(in_slot(seg, q), sums[p], 0.0), None)
    columns = []
    for b in range(S):
        level = [entry[a, b] for a in range(S)]
        for bit in (1, 2, 4):
            mask = (sub & bit) != 0
            level = [merge_pair(level[2 * q], level[2 * q + 1], mask, bit, 0) for q in range(len(level) // 2)]
        columns.append(level[0])
    for bit in (1, 2, 4):
        mask = (lane & bit) != 0
        columns = [merge_pair(columns[2 * q], columns[2 * q + 1], mask, bit, 1) for q in range(len(columns) // 2)]
    high, low = fold_pair(columns[0], 64, 1)
    pair = jnp.where(lane < 64, high, low)
    for i in range(INST):
        out_ref[i, 72:80, :] = pair


def gram_kernel(in_ref, out_ref):
    lane, sub = lanes(), sublanes()
    total, error = sum_pairs([in_ref[i, 72:80, :] for i in range(INST)])
    lower = lane < 64
    other = pltpu.roll(total, 64, 1)
    low = jnp.where(lower, other, total) + jnp.where(lower, error, pltpu.roll(error, 64, 1))
    pair = (jnp.where(lower, total, other), low)
    for shift in (8, 16, 32):
        pair = fold_pair(pair, shift, 1)
    slot = lane // 8
    row = jnp.where(slot == sub, pair[0], jnp.where(slot == sub + 8, pair[1], 0.0))
    row = jnp.broadcast_to(jnp.sum(row, axis=0, keepdims=True), TILE)
    for q in range(CELLS // 8):
        out_ref[q * 8 : q * 8 + 8, :] = row


def sum_pairs(values):
    level = [(v, None) for v in values]
    while len(level) > 1:
        merged = []
        for q in range(0, len(level), 2):
            total, error = two_sum(level[q][0], level[q + 1][0])
            if level[q][1] is not None:
                error = error + (level[q][1] + level[q + 1][1])
            merged.append((total, error))
        level = merged
    return level[0]


def unpack_kernel(in_ref, out_ref):
    seg = lanes() // 16
    places = {}
    for q, segs in enumerate(SLOTS):
        for part in range(2):
            places[segs[part]] = (q, part)
    for tile in range(9):
        for wide in range(2):
            tiles = [in_ref[8 * wide + q, tile * 8 : tile * 8 + 8, :] for q in range(8)]
            for bit in (1, 2, 4):
                off = (seg & bit) == 0
                for q in range(8):
                    if q & bit:
                        continue
                    a, b = tiles[q], tiles[q + bit]
                    tiles[q] = jnp.where(off, a, pltpu.roll(b, 16 * bit, 1))
                    tiles[q + bit] = jnp.where(off, pltpu.roll(a, 128 - 16 * bit, 1), b)
            for q in range(8):
                s, part = places[q]
                if tile >= 4:
                    s, f = 4 + s, tile - 4
                elif s:
                    f = tile
                elif tile < 3:
                    s, f = tile + 1, 4
                else:
                    continue
                out_ref[s - 1, 0, f, 8 * part : 8 * part + 8, 128 * wide : 128 * wide + 128] = tiles[q]


TRIANGLE = [(i, j) for i in range(S) for j in range(i + 1)]


def inverse_of(lower, scale):
    inverse = {}
    for i in range(S):
        inverse[i, i] = scale[i]
        for j in range(i):
            total = lower[i, j] * inverse[j, j]
            for k in range(j + 1, i):
                total = total + lower[i, k] * inverse[k, j]
            inverse[i, j] = -(scale[i] * total)
    return inverse


def product_of(a, b):
    out = {}
    for i, j in TRIANGLE:
        total = a[i, j] * b[j, j]
        for k in range(j + 1, i + 1):
            total = total + a[i, k] * b[k, j]
        out[i, j] = total
    return out


def factor_pairs(high, low):
    lower, scale = {}, {}
    for k in range(S):
        full = {i: high[i, k] + low[i, k] for i in range(k, S)}
        scale[k] = lax.rsqrt(full[k])
        parts = {}
        for i in range(k, S):
            lower[i, k] = full[i] * scale[k]
            parts[i] = split(lower[i, k])
        for i in range(k, S):
            for j in range(k, i + 1):
                (a_high, a_low), (b_high, b_low) = parts[i], parts[j]
                product = lower[i, k] * lower[j, k]
                error = ((a_high * b_high - product) + a_high * b_low + a_low * b_high) + a_low * b_low
                high[i, j], rest = two_sum(high[i, j], -product)
                low[i, j] = low[i, j] + (rest - error)
    return lower, inverse_of(lower, scale), {at: high[at] + low[at] for at in TRIANGLE}


def factor_plain(matrix):
    lower, scale = {}, {}
    for k in range(S):
        scale[k] = lax.rsqrt(matrix[k, k])
        for i in range(k, S):
            lower[i, k] = matrix[i, k] * scale[k]
        for i in range(k + 1, S):
            for j in range(k + 1, i + 1):
                matrix[i, j] = matrix[i, j] - lower[i, k] * lower[j, k]
    return lower, inverse_of(lower, scale)


def finish_kernel(rows_ref, res_ref, vec_ref, out_ref, factor_ref):
    lane, sub = lanes(), sublanes()
    pair = sum_pairs([rows_ref[q * 8 : q * 8 + 8, :] for q in range(CELLS // 8)])
    for shift in (1, 2, 4):
        pair = fold_pair(pair, shift, 0)
    low_row = pair[1] + pltpu.roll(pair[0], 64, 1)
    high = {(i, j): jnp.broadcast_to(pair[0][:, 8 * i + j : 8 * i + j + 1], TILE) for i, j in TRIANGLE}
    low = {(i, j): jnp.broadcast_to(low_row[:, 8 * i + j : 8 * i + j + 1], TILE) for i, j in TRIANGLE}
    lower_one, inverse_one, rest = factor_pairs(high, low)
    half = {}
    for i in range(S):
        for j in range(i + 1):
            total = None
            for k in range(i + 1):
                term = inverse_one[i, k] * rest[max(k, j), min(k, j)]
                total = term if total is None else total + term
            half[i, j] = total
    square = {}
    for i, j in TRIANGLE:
        total = half[i, 0] * inverse_one[j, 0]
        for k in range(1, j + 1):
            total = total + half[i, k] * inverse_one[j, k]
        square[i, j] = total + 1.0 if i == j else total
    lower_two, inverse_two = factor_plain(square)
    lower = product_of(lower_one, lower_two)
    weight = product_of(inverse_two, inverse_one)
    block = jnp.zeros(TILE, jnp.float32)
    for i, j in TRIANGLE:
        block = jnp.where((sub == j) & (lane == i), lower[i, j], block)
    factor_ref[...] = block[:, :S]
    for f in range(FIELDS):
        for part in range(2):
            for wide in range(2):
                place = (0, f, pl.ds(8 * part, 8), pl.ds(128 * wide, 128))
                v = [res_ref[place]] + [vec_ref[(s, *place)] for s in range(S - 1)]
                for a in range(S):
                    total = weight[a, 0] * v[0]
                    for b in range(1, a + 1):
                        total = total + weight[a, b] * v[b]
                    out_ref[(a, *place)] = total


def edge_kernel(res_ref, gain_ref, tail_ref, head_ref):
    for ref, start in ((tail_ref, 8), (head_ref, 0)):
        for f in range(FIELDS):
            ref[f] = res_ref[0, f, start : start + 8, :]
        ref[FIELDS] = gain_ref[0, start : start + 8, :]


def call(kernel, out_shape, in_specs, args, scratch=(), flops=10**6):
    shapes = jax.tree.map(lambda s: jax.ShapeDtypeStruct(s, jnp.float32), out_shape, is_leaf=lambda s: isinstance(s[0], int))
    return pl.pallas_call(
        kernel,
        out_shape=shapes,
        in_specs=in_specs,
        out_specs=jax.tree.map(lambda _: VMEM, shapes),
        scratch_shapes=scratch,
        compiler_params=pltpu.CompilerParams(vmem_limit_bytes=40 * 2**20),
        cost_estimate=pl.CostEstimate(flops=flops, transcendentals=0, bytes_accessed=2 * 10**6),
    )(*args)


def coupling_table():
    angles = np.pi * np.arange(1, 8) / INST
    return [float(c) for c in 0.5 * (-1.0) ** np.arange(1, 8) * np.cos(angles) / np.sin(angles)]


def on_device(residual, diag_gain, flux_jac, omega, shifts):
    ends = CELLS - 1
    tail, head = call(edge_kernel, ((STATE, 8, NC), (STATE, 8, NC)), [VMEM] * 2, (residual, diag_gain))
    below = lax.ppermute(tail, "cell", [(i, i + 1) for i in range(ends)])
    above = lax.ppermute(head, "cell", [(i + 1, i) for i in range(ends)])
    chunks = call(pack_kernel, (INST, STATE * 8, 128), [VMEM] * 4, (residual, diag_gain, below, above))
    patches = lax.all_to_all(chunks, "inst", 0, 0, tiled=True)
    vectors = call(
        functools.partial(step_kernel, rotations(coupling_table())),
        (INST, 80, 128),
        [VMEM, SMEM, SMEM, SMEM],
        (patches, flux_jac, omega, shifts),
        scratch=[
            pltpu.VMEM((S, INST, FIELDS, *TILE), jnp.float32),
            pltpu.VMEM((4 * FIELDS * FIELDS, *TILE), jnp.float32),
            pltpu.VMEM((INST, FIELDS, *TILE), jnp.float32),
            pltpu.VMEM((INST, *TILE), jnp.float32),
        ],
        flops=10**8,
    )
    back = lax.all_to_all(vectors, "inst", 0, 0, tiled=True)
    rows = lax.all_to_all(call(gram_kernel, (CELLS, 128), [VMEM], (back,)), "cell", 0, 0, tiled=True)
    others = call(unpack_kernel, (S - 1, 1, FIELDS, ROWS, NC), [VMEM], (back,))
    return call(
        finish_kernel, ((S, 1, FIELDS, ROWS, NC), (S, S)), [VMEM] * 3, (rows, residual, others)
    )


def solution(mesh):
    in_specs = (P("inst", None, "cell", None), P("inst", "cell", None), P(), P(), P())
    out_specs = (P(None, "inst", None, "cell", None), P())
    return jax.shard_map(
        on_device, mesh=mesh, in_specs=in_specs, out_specs=out_specs, check_vma=False
    )
```

time: 114 us -> 110 us (0.965)
  Pallas kernels: 16.7 us -> 14.9 us
    pallas_call x5 -> x6, Pallas kernels: 16.7 us -> 14.9 us  [call(): pl.pallas_call(kernel, out_shape=shapes, in_specs=in_specs, out_specs=jax...]
where the time goes in v2:
time: 110 us
  starting transfers between devices  47.3 us (43%)
  waiting for transfers between devices  29.9 us (27%)
  Pallas kernels  14.9 us (14%)
  blocking collectives  14.6 us (13%)
  local copies, waits for them, and re-layouts  1.62 us (1%)
  between operations  1.37 us (1%)
    all_to_all x1, starting transfers between devices, on_device(): lax.all_to_all(call(gram_kernel, (CELLS, 128), [VMEM], (back,)), 'cell',...  26.3 us
    all_to_all x1, waiting for transfers between devices, on_device(): lax.all_to_all(call(gram_kernel, (CELLS, 128), [VMEM], (back,)), 'cell',...  20.5 us
    pallas_call x6, Pallas kernels, call(): pl.pallas_call(kernel, out_shape=shapes, in_specs=in_specs, out_specs=jax...  14.9 us
    all_to_all x1, blocking collectives, on_device(): back = lax.all_to_all(vectors, 'inst', 0, 0, tiled=True)  14.6 us
    ppermute x1, starting transfers between devices, on_device(): above = lax.ppermute(head, 'cell', [(i + 1, i) for i in range(ends)])  12.4 us
    all_to_all x1, waiting for transfers between devices, on_device(): patches = lax.all_to_all(chunks, 'inst', 0, 0, tiled=True)  8.58 us
    ppermute x1, starting transfers between devices, on_device(): below = lax.ppermute(tail, 'cell', [(i, i + 1) for i in range(ends)])  4.92 us
    all_to_all x1, starting transfers between devices, on_device(): patches = lax.all_to_all(chunks, 'inst', 0, 0, tiled=True)  3.68 us
  transfers between devices with their start and end apart: 4, of which 3 were waited for; matrix products, arithmetic and copies ran while one was open for 0% of the time, Pallas kernels for 2%

profile of v2, /device:TPU:1, one launch (start us, length us, event | category | flops | bytes accessed | tf_op | source)
XLA Modules:
  0.0 109.7 jit_solution(258513752000985334)
XLA Ops:
  0.6 0.0 copy-start
  0.6 0.9 copy-done
  1.5 0.0 copy-start.2
  1.5 0.7 copy-done.2
  2.2 4.9 %collective-permute-start = (f32[6,8,256]{2,1,0:T(8,128)S(1)}, f32[6,8,256]{2,1,0:T(8,128)S(1)}, u32[]{:S(2)}, u32[]{:S(2)}) collective-permute-start(f32[6,8,256]{2,1,0:T(8,128)S(1)} %get-tuple-element.4), channel_id=1, source_target_pairs={{0,16},{16,32},{32,48},{48,64},{64,80},{80,96},{96,112},{112,128},... | collective-permute-start | bytes 147464 | tf_op jit(solution)/shard_map/ppermute | solution.py:427
  7.2 12.4 %collective-permute-start.1 = (f32[6,8,256]{2,1,0:T(8,128)S(1)}, f32[6,8,256]{2,1,0:T(8,128)S(1)}, u32[]{:S(2)}, u32[]{:S(2)}) collective-permute-start(f32[6,8,256]{2,1,0:T(8,128)S(1)} %get-tuple-element.5), channel_id=1, source_target_pairs={{16,0},{32,16},{48,32},{64,48},{80,64},{96,80},{112,96},{128,112},... | collective-permute-start | bytes 147464 | tf_op jit(solution)/shard_map/ppermute | solution.py:428
  19.6 0.0 collective-permute-done.below_ref
  19.6 0.8 collective-permute-done.1.above_ref
  20.4 1.2 %shard_map.69 = f32[16,48,128]{2,1,0:T(8,128)} custom-call(f32[1,5,16,256]{3,2,1,0:T(8,128)S(1)} %copy-done, f32[1,16,256]{2,1,0:T(8,128)S(1)} %copy-done.2, f32[6,8,256]{2,1,0:T(8,128)S(1)} %collective-permute-done.below_ref, f32[6,8,256]{2,1,0:T(8,128)S(1)} %collective-permute-done.1.above_ref), custom_call_target="tpu_custom_call" | custom-call | flops 1000000 | bytes 2000000 | tf_op jit(solution)/shard_map/pallas_call | solution.py:408
  21.6 0.0 copy-start.4
  21.6 3.7 %all-to-all-start = ((f32[16,48,128]{2,1,0:T(8,128)}), f32[16,48,128]{2,1,0:T(8,128)S(1)}, u32[]{:S(2)}, u32[]{:S(2)}) async-start(f32[16,48,128]{2,1,0:T(8,128)} %shard_map.69), calls=%async_computation | async-start | bytes 786432 | tf_op jit(solution)/shard_map/all_to_all | solution.py:430
  26.0 0.0 copy-done.4
  26.0 0.0 copy-start.3
  26.0 8.6 %all-to-all-done.in_ref = f32[16,48,128]{2,1,0:T(8,128)S(1)} async-done(((f32[16,48,128]{2,1,0:T(8,128)}), f32[16,48,128]{2,1,0:T(8,128)S(1)}, u32[]{:S(2)}, u32[]{:S(2)}) %all-to-all-start) | async-done | bytes 393248 | tf_op jit(solution)/shard_map/all_to_all | solution.py:430
  34.6 0.0 copy-done.3
  34.6 9.3 %shard_map.70 = f32[16,80,128]{2,1,0:T(8,128)S(1)} custom-call(f32[16,48,128]{2,1,0:T(8,128)S(1)} %all-to-all-done.in_ref, f32[4,5,5]{2,1,0:T(8,128)S(1)} %copy.8.jac_ref, f32[1]{0:T(128)S(6)} %copy.10.omega_ref, f32[7]{0:T(128)S(1)} %copy-done.3), custom_call_target="tpu_custom_call" | custom-call | flops 100000000 | bytes 2000000 | tf_op jit(solution)/shard_map/pallas_call | solution.py:408
  43.9 14.6 %all_to_all.21.in_ref = f32[16,80,128]{2,1,0:T(8,128)S(1)} all-to-all(f32[16,80,128]{2,1,0:T(8,128)S(1)} %shard_map.70), channel_id=1, replica_groups=mesh['cell'=64,'inst'=16] {'inst'}, dimensions={0} | all-to-all | bytes 1310720 | tf_op jit(solution)/shard_map/all_to_all | solution.py:444
  58.5 0.9 shard_map.71
  59.4 26.3 %all-to-all-start.2 = ((f32[64,1,128]{2,1,0:T(1,128)}), f32[64,1,128]{2,1,0:T(1,128)S(1)}, u32[]{:S(2)}, u32[]{:S(2)}) async-start(f32[64,1,128]{2,1,0:T(1,128)} %bitcast.1), calls=%async_computation.2 | async-start | bytes 65536 | tf_op jit(solution)/shard_map/all_to_all | solution.py:445
  85.7 0.0 copy-start.1
  85.7 1.8 %shard_map.72.vec_ref = f32[7,1,5,16,256]{4,3,2,1,0:T(8,128)S(1)} custom-call(f32[16,80,128]{2,1,0:T(8,128)S(1)} %all_to_all.21.in_ref), custom_call_target="tpu_custom_call" | custom-call | flops 1000000 | bytes 2000000 | tf_op jit(solution)/shard_map/pallas_call | solution.py:408
  87.5 20.5 %all-to-all-done.2 = f32[64,1,128]{2,1,0:T(1,128)S(1)} async-done(((f32[64,1,128]{2,1,0:T(1,128)}), f32[64,1,128]{2,1,0:T(1,128)S(1)}, u32[]{:S(2)}, u32[]{:S(2)}) %all-to-all-start.2) | async-done | bytes 32800 | tf_op jit(solution)/shard_map/all_to_all | solution.py:445
  108.0 0.0 copy-done.1
  108.0 1.7 %shard_map.73 = (f32[8,1,5,16,256]{4,3,2,1,0:T(8,128)}, f32[8,8]{1,0:T(8,128)}) custom-call(f32[64,128]{1,0:T(8,128)S(1)} %bitcast.4, f32[1,5,16,256]{3,2,1,0:T(8,128)S(1)} %copy-done.1, f32[7,1,5,16,256]{4,3,2,1,0:T(8,128)S(1)} %shard_map.72.vec_ref), custom_call_target="tpu_custom_call" | custom-call | flops 1000000 | bytes 2000000 | tf_op jit(solution)/shard_map/pallas_call | solution.py:408
  (2 shorter events, 0.0 us)
Async XLA Ops:
  0.6 0.9 copy-start
  1.5 0.7 copy-start.2
  2.2 17.3 %collective-permute-start = (f32[6,8,256]{2,1,0:T(8,128)S(1)}, f32[6,8,256]{2,1,0:T(8,128)S(1)}, u32[]{:S(2)}, u32[]{:S(2)}) collective-permute-start(f32[6,8,256]{2,1,0:T(8,128)S(1)} %get-tuple-element.4), channel_id=1, source_target_pairs={{0,16},{16,32},{32,48},{48,64},{64,80},{80,96},{96,112},{112,128},... | collective-permute-start | bytes 147464 | tf_op jit(solution)/shard_map/ppermute | solution.py:427
  7.2 13.3 %collective-permute-start.1 = (f32[6,8,256]{2,1,0:T(8,128)S(1)}, f32[6,8,256]{2,1,0:T(8,128)S(1)}, u32[]{:S(2)}, u32[]{:S(2)}) collective-permute-start(f32[6,8,256]{2,1,0:T(8,128)S(1)} %get-tuple-element.5), channel_id=1, source_target_pairs={{16,0},{32,16},{48,32},{64,48},{80,64},{96,80},{112,96},{128,112},... | collective-permute-start | bytes 147464 | tf_op jit(solution)/shard_map/ppermute | solution.py:428
  21.6 4.3 %copy-start.4 = (f32[4,5,5]{2,0,1:T(4,128)S(1)}, f32[4,5,5]{2,0,1:T(4,128)}, u32[]{:S(2)}) copy-start(f32[4,5,5]{2,0,1:T(4,128)} %param.7) | copy-start | bytes 1204
  21.6 12.9 %all-to-all-start = ((f32[16,48,128]{2,1,0:T(8,128)}), f32[16,48,128]{2,1,0:T(8,128)S(1)}, u32[]{:S(2)}, u32[]{:S(2)}) async-start(f32[16,48,128]{2,1,0:T(8,128)} %shard_map.69), calls=%async_computation | async-start | bytes 786432 | tf_op jit(solution)/shard_map/all_to_all | solution.py:430
  26.0 8.6 %copy-start.3 = (f32[7]{0:T(128)S(1)}, f32[7]{0:T(128)}, u32[]{:S(2)}) copy-start(f32[7]{0:T(128)} %shift_ref.1) | copy-start | bytes 88
  59.4 48.7 %all-to-all-start.2 = ((f32[64,1,128]{2,1,0:T(1,128)}), f32[64,1,128]{2,1,0:T(1,128)S(1)}, u32[]{:S(2)}, u32[]{:S(2)}) async-start(f32[64,1,128]{2,1,0:T(1,128)} %bitcast.1), calls=%async_computation.2 | async-start | bytes 65536 | tf_op jit(solution)/shard_map/all_to_all | solution.py:445
  85.7 22.3 %copy-start.1 = (f32[1,5,16,256]{3,2,1,0:T(8,128)S(1)}, f32[1,5,16,256]{3,2,1,0:T(8,128)}, u32[]{:S(2)}) copy-start(f32[1,5,16,256]{3,2,1,0:T(8,128)} %res_ref.5) | copy-start | bytes 245764

commit v3 on v2

--- a/solution.py
+++ b/solution.py
@@ -18,6 +18,7 @@
 NC = 256
 NR = 1024
 STATE = FIELDS + 1
+MEETING = [[(i + CELLS // 2) % CELLS for i in range(CELLS)]]
 VMEM = pl.BlockSpec(memory_space=pltpu.VMEM)
 SMEM = pl.BlockSpec(memory_space=pltpu.SMEM)
 TILE = (8, 128)
@@ -442,7 +443,8 @@
         flops=10**8,
     )
     back = lax.all_to_all(vectors, "inst", 0, 0, tiled=True)
-    rows = lax.all_to_all(call(gram_kernel, (CELLS, 128), [VMEM], (back,)), "cell", 0, 0, tiled=True)
+    row = call(gram_kernel, (CELLS, 128), [VMEM], (back,))
+    rows = lax.all_to_all(row, "cell", 0, 0, axis_index_groups=MEETING, tiled=True)
     others = call(unpack_kernel, (S - 1, 1, FIELDS, ROWS, NC), [VMEM], (back,))
     return call(
         finish_kernel, ((S, 1, FIELDS, ROWS, NC), (S, S)), [VMEM] * 3, (rows, residual, others)

time: 110 us -> 98.8 us (0.90)
  waiting for transfers between devices: 29.9 us -> 11.4 us
  starting transfers between devices: 47.3 us -> 54.4 us
    all_to_all x1, waiting for transfers between devices: 20.5 us -> 1.98 us  [on_device(): lax.all_to_all(row, 'cell', 0, 0, axis_index_groups=MEETING, tiled=True)]
    all_to_all x1, starting transfers between devices: 26.3 us -> 33.4 us  [on_device(): lax.all_to_all(row, 'cell', 0, 0, axis_index_groups=MEETING, tiled=True)]
where the time goes in v3:
time: 98.8 us; the launch traced here: 98.3 us
  starting transfers between devices  54.4 us (55%)
  Pallas kernels  14.9 us (15%)
  blocking collectives  14.6 us (15%)
  waiting for transfers between devices  11.4 us (12%)
  local copies, waits for them, and re-layouts  1.62 us (2%)
  between operations  1.37 us (1%)
    all_to_all x1, starting transfers between devices, on_device(): lax.all_to_all(row, 'cell', 0, 0, axis_index_groups=MEETING, tiled=True)  33.4 us
    pallas_call x6, Pallas kernels, call(): pl.pallas_call(kernel, out_shape=shapes, in_specs=in_specs, out_specs=jax...  14.9 us
    all_to_all x1, blocking collectives, on_device(): back = lax.all_to_all(vectors, 'inst', 0, 0, tiled=True)  14.6 us
    ppermute x1, starting transfers between devices, on_device(): above = lax.ppermute(head, 'cell', [(i + 1, i) for i in range(ends)])  12.4 us
    all_to_all x1, waiting for transfers between devices, on_device(): patches = lax.all_to_all(chunks, 'inst', 0, 0, tiled=True)  8.58 us
    ppermute x1, starting transfers between devices, on_device(): below = lax.ppermute(tail, 'cell', [(i, i + 1) for i in range(ends)])  4.92 us
    all_to_all x1, starting transfers between devices, on_device(): patches = lax.all_to_all(chunks, 'inst', 0, 0, tiled=True)  3.68 us
    all_to_all x1, waiting for transfers between devices, on_device(): lax.all_to_all(row, 'cell', 0, 0, axis_index_groups=MEETING, tiled=True)  1.98 us
  transfers between devices with their start and end apart: 4, of which 3 were waited for; matrix products, arithmetic and copies ran while one was open for 0% of the time, Pallas kernels for 2%

profile of v3, /device:TPU:1, one launch (start us, length us, event | category | flops | bytes accessed | tf_op | source)
XLA Modules:
  0.0 98.3 jit_solution(12218149995173488963)
XLA Ops:
  0.6 0.0 copy-start
  0.6 0.9 copy-done
  1.5 0.0 copy-start.2
  1.5 0.7 copy-done.2
  2.2 4.9 %collective-permute-start = (f32[6,8,256]{2,1,0:T(8,128)S(1)}, f32[6,8,256]{2,1,0:T(8,128)S(1)}, u32[]{:S(2)}, u32[]{:S(2)}) collective-permute-start(f32[6,8,256]{2,1,0:T(8,128)S(1)} %get-tuple-element.4), channel_id=1, source_target_pairs={{0,16},{16,32},{32,48},{48,64},{64,80},{80,96},{96,112},{112,128},... | collective-permute-start | bytes 147464 | tf_op jit(solution)/shard_map/ppermute | solution.py:428
  7.2 12.4 %collective-permute-start.1 = (f32[6,8,256]{2,1,0:T(8,128)S(1)}, f32[6,8,256]{2,1,0:T(8,128)S(1)}, u32[]{:S(2)}, u32[]{:S(2)}) collective-permute-start(f32[6,8,256]{2,1,0:T(8,128)S(1)} %get-tuple-element.5), channel_id=1, source_target_pairs={{16,0},{32,16},{48,32},{64,48},{80,64},{96,80},{112,96},{128,112},... | collective-permute-start | bytes 147464 | tf_op jit(solution)/shard_map/ppermute | solution.py:429
  19.6 0.0 collective-permute-done.below_ref
  19.6 0.8 collective-permute-done.1.above_ref
  20.4 1.2 %shard_map.69 = f32[16,48,128]{2,1,0:T(8,128)} custom-call(f32[1,5,16,256]{3,2,1,0:T(8,128)S(1)} %copy-done, f32[1,16,256]{2,1,0:T(8,128)S(1)} %copy-done.2, f32[6,8,256]{2,1,0:T(8,128)S(1)} %collective-permute-done.below_ref, f32[6,8,256]{2,1,0:T(8,128)S(1)} %collective-permute-done.1.above_ref), custom_call_target="tpu_custom_call" | custom-call | flops 1000000 | bytes 2000000 | tf_op jit(solution)/shard_map/pallas_call | solution.py:409
  21.6 0.0 copy-start.4
  21.6 3.7 %all-to-all-start = ((f32[16,48,128]{2,1,0:T(8,128)}), f32[16,48,128]{2,1,0:T(8,128)S(1)}, u32[]{:S(2)}, u32[]{:S(2)}) async-start(f32[16,48,128]{2,1,0:T(8,128)} %shard_map.69), calls=%async_computation | async-start | bytes 786432 | tf_op jit(solution)/shard_map/all_to_all | solution.py:431
  26.0 0.0 copy-done.4
  26.0 0.0 copy-start.3
  26.0 8.6 %all-to-all-done.in_ref = f32[16,48,128]{2,1,0:T(8,128)S(1)} async-done(((f32[16,48,128]{2,1,0:T(8,128)}), f32[16,48,128]{2,1,0:T(8,128)S(1)}, u32[]{:S(2)}, u32[]{:S(2)}) %all-to-all-start) | async-done | bytes 393248 | tf_op jit(solution)/shard_map/all_to_all | solution.py:431
  34.6 0.0 copy-done.3
  34.6 9.3 %shard_map.70 = f32[16,80,128]{2,1,0:T(8,128)S(1)} custom-call(f32[16,48,128]{2,1,0:T(8,128)S(1)} %all-to-all-done.in_ref, f32[4,5,5]{2,1,0:T(8,128)S(1)} %copy.8.jac_ref, f32[1]{0:T(128)S(6)} %copy.10.omega_ref, f32[7]{0:T(128)S(1)} %copy-done.3), custom_call_target="tpu_custom_call" | custom-call | flops 100000000 | bytes 2000000 | tf_op jit(solution)/shard_map/pallas_call | solution.py:409
  43.9 14.6 %all_to_all.21.in_ref = f32[16,80,128]{2,1,0:T(8,128)S(1)} all-to-all(f32[16,80,128]{2,1,0:T(8,128)S(1)} %shard_map.70), channel_id=1, replica_groups=mesh['cell'=64,'inst'=16] {'inst'}, dimensions={0} | all-to-all | bytes 1310720 | tf_op jit(solution)/shard_map/all_to_all | solution.py:445
  58.5 0.9 shard_map.71
  59.4 33.4 %all-to-all-start.2 = ((f32[64,1,128]{2,1,0:T(1,128)}), f32[64,1,128]{2,1,0:T(1,128)S(1)}, u32[]{:S(2)}, u32[]{:S(2)}) async-start(f32[64,1,128]{2,1,0:T(1,128)} %bitcast.1), calls=%async_computation.2 | async-start | bytes 65536 | tf_op jit(solution)/shard_map/all_to_all | solution.py:447
  92.8 0.0 copy-start.1
  92.8 1.8 %shard_map.72.vec_ref = f32[7,1,5,16,256]{4,3,2,1,0:T(8,128)S(1)} custom-call(f32[16,80,128]{2,1,0:T(8,128)S(1)} %all_to_all.21.in_ref), custom_call_target="tpu_custom_call" | custom-call | flops 1000000 | bytes 2000000 | tf_op jit(solution)/shard_map/pallas_call | solution.py:409
  94.6 2.0 %all-to-all-done.2 = f32[64,1,128]{2,1,0:T(1,128)S(1)} async-done(((f32[64,1,128]{2,1,0:T(1,128)}), f32[64,1,128]{2,1,0:T(1,128)S(1)}, u32[]{:S(2)}, u32[]{:S(2)}) %all-to-all-start.2) | async-done | bytes 32800 | tf_op jit(solution)/shard_map/all_to_all | solution.py:447
  96.6 0.0 copy-done.1
  96.6 1.7 %shard_map.73 = (f32[8,1,5,16,256]{4,3,2,1,0:T(8,128)}, f32[8,8]{1,0:T(8,128)}) custom-call(f32[64,128]{1,0:T(8,128)S(1)} %bitcast.4, f32[1,5,16,256]{3,2,1,0:T(8,128)S(1)} %copy-done.1, f32[7,1,5,16,256]{4,3,2,1,0:T(8,128)S(1)} %shard_map.72.vec_ref), custom_call_target="tpu_custom_call" | custom-call | flops 1000000 | bytes 2000000 | tf_op jit(solution)/shard_map/pallas_call | solution.py:409
  (2 shorter events, 0.0 us)
Async XLA Ops:
  0.6 0.9 copy-start
  1.5 0.7 copy-start.2
  2.2 17.3 %collective-permute-start = (f32[6,8,256]{2,1,0:T(8,128)S(1)}, f32[6,8,256]{2,1,0:T(8,128)S(1)}, u32[]{:S(2)}, u32[]{:S(2)}) collective-permute-start(f32[6,8,256]{2,1,0:T(8,128)S(1)} %get-tuple-element.4), channel_id=1, source_target_pairs={{0,16},{16,32},{32,48},{48,64},{64,80},{80,96},{96,112},{112,128},... | collective-permute-start | bytes 147464 | tf_op jit(solution)/shard_map/ppermute | solution.py:428
  7.2 13.3 %collective-permute-start.1 = (f32[6,8,256]{2,1,0:T(8,128)S(1)}, f32[6,8,256]{2,1,0:T(8,128)S(1)}, u32[]{:S(2)}, u32[]{:S(2)}) collective-permute-start(f32[6,8,256]{2,1,0:T(8,128)S(1)} %get-tuple-element.5), channel_id=1, source_target_pairs={{16,0},{32,16},{48,32},{64,48},{80,64},{96,80},{112,96},{128,112},... | collective-permute-start | bytes 147464 | tf_op jit(solution)/shard_map/ppermute | solution.py:429
  21.6 4.3 %copy-start.4 = (f32[4,5,5]{2,0,1:T(4,128)S(1)}, f32[4,5,5]{2,0,1:T(4,128)}, u32[]{:S(2)}) copy-start(f32[4,5,5]{2,0,1:T(4,128)} %param.7) | copy-start | bytes 1204
  21.6 12.9 %all-to-all-start = ((f32[16,48,128]{2,1,0:T(8,128)}), f32[16,48,128]{2,1,0:T(8,128)S(1)}, u32[]{:S(2)}, u32[]{:S(2)}) async-start(f32[16,48,128]{2,1,0:T(8,128)} %shard_map.69), calls=%async_computation | async-start | bytes 786432 | tf_op jit(solution)/shard_map/all_to_all | solution.py:431
  26.0 8.6 %copy-start.3 = (f32[7]{0:T(128)S(1)}, f32[7]{0:T(128)}, u32[]{:S(2)}) copy-start(f32[7]{0:T(128)} %shift_ref.1) | copy-start | bytes 88
  59.4 37.2 %all-to-all-start.2 = ((f32[64,1,128]{2,1,0:T(1,128)}), f32[64,1,128]{2,1,0:T(1,128)S(1)}, u32[]{:S(2)}, u32[]{:S(2)}) async-start(f32[64,1,128]{2,1,0:T(1,128)} %bitcast.1), calls=%async_computation.2 | async-start | bytes 65536 | tf_op jit(solution)/shard_map/all_to_all | solution.py:447
  92.8 3.8 %copy-start.1 = (f32[1,5,16,256]{3,2,1,0:T(8,128)S(1)}, f32[1,5,16,256]{3,2,1,0:T(8,128)}, u32[]{:S(2)}) copy-start(f32[1,5,16,256]{3,2,1,0:T(8,128)} %res_ref.5) | copy-start | bytes 245764

commit v4 on v3

--- a/solution.py
+++ b/solution.py
@@ -46,27 +46,24 @@
 
 def pack_kernel(res_ref, gain_ref, below_ref, above_ref, out_ref):
     lane = lanes()
-    group = lane // 32
+    group, place = lane // 32, lane % 32
     for field in range(STATE):
         own = res_ref.at[0, field] if field < FIELDS else gain_ref.at[0]
         rows = [below_ref[field], own[0:8, :], own[8:16, :], above_ref[field]]
-        chunks = [None] * INST
-        for part in range(4):
-            left, right = rows[part][:, :128], rows[part][:, 128:]
-            for turn in range(8):
-                shift = 16 * turn + 8
-                rolled_left = pltpu.roll(left, shift, 1)
-                rolled_right = pltpu.roll(right, shift, 1)
-                first = lane < shift
-                for turns, moved in (
-                    (turn, jnp.where(first, rolled_right, rolled_left)),
-                    (turn + 8, jnp.where(first, rolled_left, rolled_right)),
-                ):
-                    chunk = (2 * part - turns) % 16
-                    old = chunks[chunk]
-                    chunks[chunk] = moved if old is None else jnp.where(group == part, moved, old)
-        for chunk in range(INST):
-            out_ref[chunk, field * 8 : field * 8 + 8, :] = chunks[chunk]
+        for parity in range(2):
+            moved = []
+            for part in range(4):
+                shift = (32 * part + HALO - COLS * parity) % 128
+                moved.append([pltpu.roll(rows[part][:, 128 * h : 128 * h + 128], shift, 1) for h in range(2)])
+            for inst in range(parity, INST, 2):
+                chunk = None
+                for part in range(4):
+                    left, right = moved[part]
+                    piece = left if inst < 8 else right
+                    if inst in (7, 8):
+                        piece = jnp.where(place < (24 if inst == 7 else 8), left, right)
+                    chunk = piece if chunk is None else jnp.where(group == (part + inst // 2) % 4, piece, chunk)
+                out_ref[inst, field * 8 : field * 8 + 8, :] = chunk
 
 
 def merge_pair(first, second, mask, shift, axis):
@@ -131,99 +128,119 @@
 
 
 SLOTS = ((2, 4), (3, 5), (6, 0), (7, 1))
-OFFSETS = (0, 1, 4, 5)
-MOVES = {(0, 0): (0, 1, 4, 5), (1, 1): (0, 1, 4, 5), (0, 1): (0, 1, 3, 4, 5, 7)}
+SLOT_MOVES = (0, 16, 64, 80)
+
+
+def segments():
+    return ((lanes() + 128 - HALO) % 128) // 16
 
 
 def in_slot(seg, q):
     return (seg == SLOTS[q][0]) | (seg == SLOTS[q][1])
 
 
-def pack_four(seg, a, b, c, d):
-    a, b, c, d = pltpu.roll(a, 120, 1), pltpu.roll(b, 8, 1), pltpu.roll(c, 56, 1), pltpu.roll(d, 72, 1)
-    return jnp.where(in_slot(seg, 0), a, jnp.where(in_slot(seg, 1), b, jnp.where(in_slot(seg, 2), c, d)))
-
-
-def step_kernel(rotation, in_ref, jac_ref, omega_ref, shift_ref, out_ref, vec_ref, coef_ref, mix_ref, gain_ref):
+TILES = INST * FIELDS
+PITCH = 16
+
+
+def tile_at(i, f):
+    return PITCH * (i * FIELDS + f) + 8
+
+
+def step_kernel(rotation, in_ref, jac_ref, omega_ref, shift_ref, out_ref, vec_ref, coef_ref, mix_ref, gain_ref, slot_ref):
     lane, sub = lanes(), sublanes()
-    seg = lane // 16
+    seg = segments()
     cell, inst = lax.axis_index("cell"), lax.axis_index("inst")
-    row = cell * ROWS - HALO + (lane // 32) * 8 + sub
+    turn = lax.rem(inst // 2, 4)
+    part = (lane // 32 + 4 - turn) % 4
+    row = cell * ROWS - HALO + part * 8 + sub
     col = inst * COLS - HALO + lane % 32
     inside = (row >= 0) & (row < NR) & (col >= 0) & (col < NC)
-    first_row, last_row = sub == 0, sub == 7
     for d in range(4):
         for f in range(FIELDS):
             for e in range(FIELDS):
                 coef_ref[(d * FIELDS + f) * FIELDS + e] = jnp.full(TILE, jac_ref[d, f, e])
     for i in range(INST):
         for f in range(FIELDS):
-            vec_ref[0, i, f] = jnp.where(inside, in_ref[i, f * 8 : f * 8 + 8, :], 0.0)
+            vec_ref[0, pl.ds(tile_at(i, f), 8), :] = jnp.where(inside, in_ref[i, f * 8 : f * 8 + 8, :], 0.0)
         gain_ref[i] = in_ref[i, FIELDS * 8 : FIELDS * 8 + 8, :]
     weights = [jnp.full(TILE, omega_ref[0] * w) for w in rotation]
 
     def step(n, carry):
         shift = shift_ref[n]
+        slot = lax.rem(n, 4)
+        aligned = lax.rem(lax.rem(slot, 2) * 16 + (slot // 2) * 64 + 128 - 32 * turn, 128)
+        now, later = vec_ref.at[n], vec_ref.at[n + 1]
+        for group in range(TILES // 8):
+            start = PITCH * 8 * group
+            last = now[pl.ds(start + 15, 8, stride=PITCH), :]
+            now[pl.ds(start + 7, 8, stride=PITCH), :] = pltpu.roll(last, 32, 1)
+            first = now[pl.ds(start + 8, 8, stride=PITCH), :]
+            now[pl.ds(start + 16, 8, stride=PITCH), :] = pltpu.roll(first, 96, 1)
         for f in range(FIELDS):
-            mixed = coupled([vec_ref[n, i, f] for i in range(INST)], weights)
+            mixed = coupled([now[pl.ds(tile_at(i, f), 8), :] for i in range(INST)], weights)
             for i in range(INST):
                 mix_ref[i, f] = mixed[i]
         for pair in range(0, INST, 2):
             members = (pair, pair + 1)
-            near, center = {}, {}
+            near, center, gain = {}, {}, {}
             for i in members:
+                gain[i] = gain_ref[i] - shift
                 for e in range(FIELDS):
-                    v = vec_ref[n, i, e]
+                    at = tile_at(i, e)
+                    v = now[pl.ds(at, 8), :]
                     center[i, e] = v
-                    down = pltpu.roll(v, 1, 0)
-                    up = pltpu.roll(v, 7, 0)
-                    near[i, 0, e] = jnp.where(first_row, pltpu.roll(down, 32, 1), down)
-                    near[i, 1, e] = jnp.where(last_row, pltpu.roll(up, 96, 1), up)
+                    slot_ref[n, i, e] = pltpu.roll(v, aligned, 1)
+                    near[i, 0, e] = now[pl.ds(at - 1, 8), :]
+                    near[i, 1, e] = now[pl.ds(at + 1, 8), :]
                     near[i, 2, e] = pltpu.roll(v, 1, 1)
                     near[i, 3, e] = pltpu.roll(v, 127, 1)
             for f in range(FIELDS):
-                total = {i: mix_ref[i, f] + (gain_ref[i] - shift) * center[i, f] for i in members}
+                total = {i: mix_ref[i, f] + gain[i] * center[i, f] for i in members}
                 for d in range(4):
                     for e in range(FIELDS):
                         c = coef_ref[(d * FIELDS + f) * FIELDS + e]
                         for i in members:
                             total[i] = total[i] - c * near[i, d, e]
                 for i in members:
-                    vec_ref[n + 1, i, f] = jnp.where(inside, total[i], 0.0)
+                    later[pl.ds(tile_at(i, f), 8), :] = jnp.where(inside, total[i], 0.0)
         return carry
 
     lax.fori_loop(0, S - 1, step, 0)
 
-    keys = [(x, y, move) for (x, y), moves in MOVES.items() for move in moves]
-
-    def gather(i, sums):
+    pairs = [(a, b) for a in range(S) for b in range(a, S)]
+    last_move = lax.rem(SLOT_MOVES[3] + 128 - 32 * turn, 128)
+
+    def gather(quarter, sums):
         sums = list(sums)
-        tiles = {}
-        for f in range(FIELDS):
-            for x in range(2):
-                tiles[x, f] = pack_four(seg, *[vec_ref[4 * x + q, i, f] for q in range(4)])
-            moved = {}
-            for p, (x, y, move) in enumerate(keys):
-                if (y, move) not in moved:
-                    moved[y, move] = pltpu.roll(tiles[y, f], 16 * move, 1) if move else tiles[y, f]
-                sums[p] = sums[p] + tiles[x, f] * moved[y, move]
-            out_ref[i, (4 + f) * 8 : (4 + f) * 8 + 8, :] = tiles[1, f]
-        for f in range(4):
-            tile = tiles[0, f]
-            if f < 3:
-                move = (OFFSETS[0] - OFFSETS[f + 1]) % 8
-                tile = jnp.where(in_slot(seg, 0), pltpu.roll(tiles[0, 4], 16 * move, 1), tile)
-            out_ref[i, f * 8 : f * 8 + 8, :] = tile
+        for i in [quarter * 4 + q for q in range(4)]:
+            tiles = {}
+            for f in range(FIELDS):
+                at = pl.multiple_of(PITCH * FIELDS * i + tile_at(0, f), 8)
+                v = [vec_ref[s, pl.ds(at, 8), :] for s in range(S)]
+                for p, (a, b) in enumerate(pairs):
+                    sums[p] = sums[p] + v[a] * v[b]
+                moved = [slot_ref[s, i, f] for s in range(S - 1)] + [pltpu.roll(v[S - 1], last_move, 1)]
+                for x in range(2):
+                    a, b, c, d = moved[4 * x : 4 * x + 4]
+                    tiles[x, f] = jnp.where(
+                        in_slot(seg, 0), a, jnp.where(in_slot(seg, 1), b, jnp.where(in_slot(seg, 2), c, d))
+                    )
+                out_ref[i, (4 + f) * 8 : (4 + f) * 8 + 8, :] = tiles[1, f]
+            for f in range(4):
+                tile = tiles[0, f]
+                if f < 3:
+                    move = (SLOT_MOVES[0] - SLOT_MOVES[f + 1]) % 128
+                    tile = jnp.where(in_slot(seg, 0), pltpu.roll(tiles[0, 4], move, 1), tile)
+                out_ref[i, f * 8 : f * 8 + 8, :] = tile
         return tuple(sums)
 
-    sums = lax.fori_loop(0, INST, gather, tuple(jnp.zeros(TILE, jnp.float32) for _ in keys))
+    sums = lax.fori_loop(0, INST // 4, gather, tuple(jnp.zeros(TILE, jnp.float32) for _ in pairs))
+    column = lane % 32
+    own = ((part == 1) | (part == 2)) & (column >= HALO) & (column < HALO + COLS)
     entry = {}
-    for p, (x, y, move) in enumerate(keys):
-        for q in range(4):
-            for r in range(4):
-                a, b = 4 * x + q, 4 * y + r
-                if (OFFSETS[q] - OFFSETS[r]) % 8 == move and (a, b) not in entry:
-                    entry[a, b] = entry[b, a] = (jnp.where(in_slot(seg, q), sums[p], 0.0), None)
+    for p, (a, b) in enumerate(pairs):
+        entry[a, b] = entry[b, a] = (jnp.where(own, sums[p], 0.0), None)
     columns = []
     for b in range(S):
         level = [entry[a, b] for a in range(S)]
@@ -277,7 +294,7 @@
             places[segs[part]] = (q, part)
     for tile in range(9):
         for wide in range(2):
-            tiles = [in_ref[8 * wide + q, tile * 8 : tile * 8 + 8, :] for q in range(8)]
+            tiles = [pltpu.roll(in_ref[8 * wide + q, tile * 8 : tile * 8 + 8, :], 128 - HALO, 1) for q in range(8)]
             for bit in (1, 2, 4):
                 off = (seg & bit) == 0
                 for q in range(8):
@@ -397,11 +414,16 @@
                     out_ref[(a, *place)] = total
 
 
-def edge_kernel(res_ref, gain_ref, tail_ref, head_ref):
+def edge_kernel(res_ref, gain_ref, tail_ref, head_ref, sems):
+    copies = []
     for ref, start in ((tail_ref, 8), (head_ref, 0)):
-        for f in range(FIELDS):
-            ref[f] = res_ref[0, f, start : start + 8, :]
-        ref[FIELDS] = gain_ref[0, start : start + 8, :]
+        rows = pl.ds(start, 8)
+        for source, target in ((res_ref.at[0, :, rows, :], ref.at[pl.ds(0, FIELDS)]), (gain_ref.at[:, rows, :], ref.at[pl.ds(FIELDS, 1)])):
+            copies.append(pltpu.make_async_copy(source, target, sems.at[len(copies)]))
+    for copy in copies:
+        copy.start()
+    for copy in copies:
+        copy.wait()
 
 
 def call(kernel, out_shape, in_specs, args, scratch=(), flops=10**6):
@@ -424,7 +446,13 @@
 
 def on_device(residual, diag_gain, flux_jac, omega, shifts):
     ends = CELLS - 1
-    tail, head = call(edge_kernel, ((STATE, 8, NC), (STATE, 8, NC)), [VMEM] * 2, (residual, diag_gain))
+    tail, head = call(
+        edge_kernel,
+        ((STATE, 8, NC), (STATE, 8, NC)),
+        [pl.BlockSpec(memory_space=pl.ANY)] * 2,
+        (residual, diag_gain),
+        scratch=[pltpu.SemaphoreType.DMA((4,))],
+    )
     below = lax.ppermute(tail, "cell", [(i, i + 1) for i in range(ends)])
     above = lax.ppermute(head, "cell", [(i + 1, i) for i in range(ends)])
     chunks = call(pack_kernel, (INST, STATE * 8, 128), [VMEM] * 4, (residual, diag_gain, below, above))
@@ -435,10 +463,11 @@
         [VMEM, SMEM, SMEM, SMEM],
         (patches, flux_jac, omega, shifts),
         scratch=[
-            pltpu.VMEM((S, INST, FIELDS, *TILE), jnp.float32),
+            pltpu.VMEM((S, PITCH * (TILES + 1), 128), jnp.float32),
             pltpu.VMEM((4 * FIELDS * FIELDS, *TILE), jnp.float32),
             pltpu.VMEM((INST, FIELDS, *TILE), jnp.float32),
             pltpu.VMEM((INST, *TILE), jnp.float32),
+            pltpu.VMEM((S - 1, INST, FIELDS, *TILE), jnp.float32),
         ],
         flops=10**8,
     )

time: 98.8 us -> 96.7 us (0.979)
  Pallas kernels: 14.9 us -> 13.6 us
    pallas_call x6, Pallas kernels: 14.9 us -> 13.6 us  [call(): pl.pallas_call(kernel, out_shape=shapes, in_specs=in_specs, out_specs=jax...]
  transfers between devices with their start and end apart: 4 -> 4, of which waited for: 3 -> 3; matrix products, arithmetic and copies ran while one was open for 0% -> 0% of each run, Pallas kernels for 2% -> 3%
where the time goes in v4:
time: 96.7 us; the launch traced here: 96.3 us
  starting transfers between devices  54.4 us (56%)
  blocking collectives  14.6 us (15%)
  Pallas kernels  13.6 us (14%)
  waiting for transfers between devices  10.8 us (11%)
  local copies, waits for them, and re-layouts  1.62 us (2%)
  between operations  1.38 us (1%)
    all_to_all x1, starting transfers between devices, on_device(): lax.all_to_all(row, 'cell', 0, 0, axis_index_groups=MEETING, tiled=True)  33.4 us
    all_to_all x1, blocking collectives, on_device(): back = lax.all_to_all(vectors, 'inst', 0, 0, tiled=True)  14.6 us
    pallas_call x6, Pallas kernels, call(): pl.pallas_call(kernel, out_shape=shapes, in_specs=in_specs, out_specs=jax...  13.6 us
    ppermute x1, starting transfers between devices, on_device(): above = lax.ppermute(head, 'cell', [(i + 1, i) for i in range(ends)])  12.4 us
    all_to_all x1, waiting for transfers between devices, on_device(): patches = lax.all_to_all(chunks, 'inst', 0, 0, tiled=True)  8.58 us
    ppermute x1, starting transfers between devices, on_device(): below = lax.ppermute(tail, 'cell', [(i, i + 1) for i in range(ends)])  4.92 us
    all_to_all x1, starting transfers between devices, on_device(): patches = lax.all_to_all(chunks, 'inst', 0, 0, tiled=True)  3.68 us
  transfers between devices with their start and end apart: 4, of which 3 were waited for; matrix products, arithmetic and copies ran while one was open for 0% of the time, Pallas kernels for 3%

profile of v4, /device:TPU:1, one launch (start us, length us, event | category | flops | bytes accessed | tf_op | source)
XLA Modules:
  0.0 96.3 jit_solution(9732998885671142)
XLA Ops:
  0.6 0.0 copy-start
  0.6 0.9 copy-done
  1.5 0.0 copy-start.2
  1.5 0.7 copy-done.2
  2.2 0.1 shard_map.68
  2.3 4.9 %collective-permute-start = (f32[6,8,256]{2,1,0:T(8,128)S(1)}, f32[6,8,256]{2,1,0:T(8,128)S(1)}, u32[]{:S(2)}, u32[]{:S(2)}) collective-permute-start(f32[6,8,256]{2,1,0:T(8,128)S(1)} %get-tuple-element.4), channel_id=1, source_target_pairs={{0,16},{16,32},{32,48},{48,64},{64,80},{80,96},{96,112},{112,128},... | collective-permute-start | bytes 147464 | tf_op jit(solution)/shard_map/ppermute | solution.py:456
  7.3 12.4 %collective-permute-start.1 = (f32[6,8,256]{2,1,0:T(8,128)S(1)}, f32[6,8,256]{2,1,0:T(8,128)S(1)}, u32[]{:S(2)}, u32[]{:S(2)}) collective-permute-start(f32[6,8,256]{2,1,0:T(8,128)S(1)} %get-tuple-element.5), channel_id=1, source_target_pairs={{16,0},{32,16},{48,32},{64,48},{80,64},{96,80},{112,96},{128,112},... | collective-permute-start | bytes 147464 | tf_op jit(solution)/shard_map/ppermute | solution.py:457
  19.7 0.0 collective-permute-done.below_ref
  19.7 0.8 collective-permute-done.1.above_ref
  20.5 0.9 shard_map.69
  21.4 0.0 copy-start.4
  21.4 3.7 %all-to-all-start = ((f32[16,48,128]{2,1,0:T(8,128)}), f32[16,48,128]{2,1,0:T(8,128)S(1)}, u32[]{:S(2)}, u32[]{:S(2)}) async-start(f32[16,48,128]{2,1,0:T(8,128)} %shard_map.69), calls=%async_computation | async-start | bytes 786432 | tf_op jit(solution)/shard_map/all_to_all | solution.py:459
  25.8 0.0 copy-done.4
  25.8 0.0 copy-start.3
  25.8 8.6 %all-to-all-done.in_ref = f32[16,48,128]{2,1,0:T(8,128)S(1)} async-done(((f32[16,48,128]{2,1,0:T(8,128)}), f32[16,48,128]{2,1,0:T(8,128)S(1)}, u32[]{:S(2)}, u32[]{:S(2)}) %all-to-all-start) | async-done | bytes 393248 | tf_op jit(solution)/shard_map/all_to_all | solution.py:459
  34.4 0.0 copy-done.3
  34.4 7.5 %shard_map.70 = f32[16,80,128]{2,1,0:T(8,128)S(1)} custom-call(f32[16,48,128]{2,1,0:T(8,128)S(1)} %all-to-all-done.in_ref, f32[4,5,5]{2,1,0:T(8,128)S(1)} %copy.8.jac_ref, f32[1]{0:T(128)S(6)} %copy.10.omega_ref, f32[7]{0:T(128)S(1)} %copy-done.3), custom_call_target="tpu_custom_call" | custom-call | flops 100000000 | bytes 2000000 | tf_op jit(solution)/shard_map/pallas_call | solution.py:431
  41.9 14.6 %all_to_all.21.in_ref = f32[16,80,128]{2,1,0:T(8,128)S(1)} all-to-all(f32[16,80,128]{2,1,0:T(8,128)S(1)} %shard_map.70), channel_id=1, replica_groups=mesh['cell'=64,'inst'=16] {'inst'}, dimensions={0} | all-to-all | bytes 1310720 | tf_op jit(solution)/shard_map/all_to_all | solution.py:474
  56.5 0.9 shard_map.71
  57.4 33.4 %all-to-all-start.2 = ((f32[64,1,128]{2,1,0:T(1,128)}), f32[64,1,128]{2,1,0:T(1,128)S(1)}, u32[]{:S(2)}, u32[]{:S(2)}) async-start(f32[64,1,128]{2,1,0:T(1,128)} %bitcast.1), calls=%async_computation.2 | async-start | bytes 65536 | tf_op jit(solution)/shard_map/all_to_all | solution.py:476
  90.8 0.0 copy-start.1
  90.8 2.5 %shard_map.72.vec_ref = f32[7,1,5,16,256]{4,3,2,1,0:T(8,128)S(1)} custom-call(f32[16,80,128]{2,1,0:T(8,128)S(1)} %all_to_all.21.in_ref), custom_call_target="tpu_custom_call" | custom-call | flops 1000000 | bytes 2000000 | tf_op jit(solution)/shard_map/pallas_call | solution.py:431
  93.3 1.3 %all-to-all-done.2 = f32[64,1,128]{2,1,0:T(1,128)S(1)} async-done(((f32[64,1,128]{2,1,0:T(1,128)}), f32[64,1,128]{2,1,0:T(1,128)S(1)}, u32[]{:S(2)}, u32[]{:S(2)}) %all-to-all-start.2) | async-done | bytes 32800 | tf_op jit(solution)/shard_map/all_to_all | solution.py:476
  94.6 0.0 copy-done.1
  94.6 1.7 %shard_map.73 = (f32[8,1,5,16,256]{4,3,2,1,0:T(8,128)}, f32[8,8]{1,0:T(8,128)}) custom-call(f32[64,128]{1,0:T(8,128)S(1)} %bitcast.4, f32[1,5,16,256]{3,2,1,0:T(8,128)S(1)} %copy-done.1, f32[7,1,5,16,256]{4,3,2,1,0:T(8,128)S(1)} %shard_map.72.vec_ref), custom_call_target="tpu_custom_call" | custom-call | flops 1000000 | bytes 2000000 | tf_op jit(solution)/shard_map/pallas_call | solution.py:431
  (1 shorter events, 0.0 us)
Async XLA Ops:
  0.6 0.9 copy-start
  1.5 0.7 copy-start.2
  2.3 17.3 %collective-permute-start = (f32[6,8,256]{2,1,0:T(8,128)S(1)}, f32[6,8,256]{2,1,0:T(8,128)S(1)}, u32[]{:S(2)}, u32[]{:S(2)}) collective-permute-start(f32[6,8,256]{2,1,0:T(8,128)S(1)} %get-tuple-element.4), channel_id=1, source_target_pairs={{0,16},{16,32},{32,48},{48,64},{64,80},{80,96},{96,112},{112,128},... | collective-permute-start | bytes 147464 | tf_op jit(solution)/shard_map/ppermute | solution.py:456
  7.3 13.3 %collective-permute-start.1 = (f32[6,8,256]{2,1,0:T(8,128)S(1)}, f32[6,8,256]{2,1,0:T(8,128)S(1)}, u32[]{:S(2)}, u32[]{:S(2)}) collective-permute-start(f32[6,8,256]{2,1,0:T(8,128)S(1)} %get-tuple-element.5), channel_id=1, source_target_pairs={{16,0},{32,16},{48,32},{64,48},{80,64},{96,80},{112,96},{128,112},... | collective-permute-start | bytes 147464 | tf_op jit(solution)/shard_map/ppermute | solution.py:457
  21.4 4.3 %copy-start.4 = (f32[4,5,5]{2,0,1:T(4,128)S(1)}, f32[4,5,5]{2,0,1:T(4,128)}, u32[]{:S(2)}) copy-start(f32[4,5,5]{2,0,1:T(4,128)} %param.7) | copy-start | bytes 1204
  21.4 12.9 %all-to-all-start = ((f32[16,48,128]{2,1,0:T(8,128)}), f32[16,48,128]{2,1,0:T(8,128)S(1)}, u32[]{:S(2)}, u32[]{:S(2)}) async-start(f32[16,48,128]{2,1,0:T(8,128)} %shard_map.69), calls=%async_computation | async-start | bytes 786432 | tf_op jit(solution)/shard_map/all_to_all | solution.py:459
  25.8 8.6 %copy-start.3 = (f32[7]{0:T(128)S(1)}, f32[7]{0:T(128)}, u32[]{:S(2)}) copy-start(f32[7]{0:T(128)} %shift_ref.1) | copy-start | bytes 88
  57.4 37.2 %all-to-all-start.2 = ((f32[64,1,128]{2,1,0:T(1,128)}), f32[64,1,128]{2,1,0:T(1,128)S(1)}, u32[]{:S(2)}, u32[]{:S(2)}) async-start(f32[64,1,128]{2,1,0:T(1,128)} %bitcast.1), calls=%async_computation.2 | async-start | bytes 65536 | tf_op jit(solution)/shard_map/all_to_all | solution.py:476
  90.8 3.8 %copy-start.1 = (f32[1,5,16,256]{3,2,1,0:T(8,128)S(1)}, f32[1,5,16,256]{3,2,1,0:T(8,128)}, u32[]{:S(2)}) copy-start(f32[1,5,16,256]{3,2,1,0:T(8,128)} %res_ref.5) | copy-start | bytes 245764

commit v5 on v4

--- a/solution.py
+++ b/solution.py
@@ -208,7 +208,12 @@
 
     lax.fori_loop(0, S - 1, step, 0)
 
-    pairs = [(a, b) for a in range(S) for b in range(a, S)]
+    packed = {}
+    for x, y in ((0, 0), (1, 1), (0, 1)):
+        for half in range(2):
+            packed[x, y, half] = [(4 * x + q, 4 * y + (q + 2 * half) % 4, q) for q in range(4)]
+    covered = {(min(a, b), max(a, b)) for entries in packed.values() for a, b, _ in entries}
+    plain = [(a, b) for a in range(S) for b in range(a, S) if (a, b) not in covered]
     last_move = lax.rem(SLOT_MOVES[3] + 128 - 32 * turn, 128)
 
     def gather(quarter, sums):
@@ -218,14 +223,17 @@
             for f in range(FIELDS):
                 at = pl.multiple_of(PITCH * FIELDS * i + tile_at(0, f), 8)
                 v = [vec_ref[s, pl.ds(at, 8), :] for s in range(S)]
-                for p, (a, b) in enumerate(pairs):
-                    sums[p] = sums[p] + v[a] * v[b]
                 moved = [slot_ref[s, i, f] for s in range(S - 1)] + [pltpu.roll(v[S - 1], last_move, 1)]
                 for x in range(2):
                     a, b, c, d = moved[4 * x : 4 * x + 4]
                     tiles[x, f] = jnp.where(
                         in_slot(seg, 0), a, jnp.where(in_slot(seg, 1), b, jnp.where(in_slot(seg, 2), c, d))
                     )
+                turned_tiles = [pltpu.roll(tiles[x, f], 64, 1) for x in range(2)]
+                for p, (a, b) in enumerate(plain):
+                    sums[p] = sums[p] + v[a] * v[b]
+                for p, (x, y, half) in enumerate(packed, len(plain)):
+                    sums[p] = sums[p] + tiles[x, f] * (turned_tiles[y] if half else tiles[y, f])
                 out_ref[i, (4 + f) * 8 : (4 + f) * 8 + 8, :] = tiles[1, f]
             for f in range(4):
                 tile = tiles[0, f]
@@ -235,12 +243,17 @@
                 out_ref[i, f * 8 : f * 8 + 8, :] = tile
         return tuple(sums)
 
-    sums = lax.fori_loop(0, INST // 4, gather, tuple(jnp.zeros(TILE, jnp.float32) for _ in pairs))
+    start = tuple(jnp.zeros(TILE, jnp.float32) for _ in range(len(plain) + len(packed)))
+    sums = lax.fori_loop(0, INST // 4, gather, start)
     column = lane % 32
     own = ((part == 1) | (part == 2)) & (column >= HALO) & (column < HALO + COLS)
     entry = {}
-    for p, (a, b) in enumerate(pairs):
+    for p, (a, b) in enumerate(plain):
         entry[a, b] = entry[b, a] = (jnp.where(own, sums[p], 0.0), None)
+    for p, entries in enumerate(packed.values(), len(plain)):
+        for a, b, q in entries:
+            if (a, b) not in entry:
+                entry[a, b] = entry[b, a] = (jnp.where(in_slot(seg, q), sums[p], 0.0), None)
     columns = []
     for b in range(S):
         level = [entry[a, b] for a in range(S)]
@@ -353,10 +366,8 @@
         for i in range(k, S):
             for j in range(k, i + 1):
                 (a_high, a_low), (b_high, b_low) = parts[i], parts[j]
-                product = lower[i, k] * lower[j, k]
-                error = ((a_high * b_high - product) + a_high * b_low + a_low * b_high) + a_low * b_low
-                high[i, j], rest = two_sum(high[i, j], -product)
-                low[i, j] = low[i, j] + (rest - error)
+                high[i, j], rest = two_sum(high[i, j], -(a_high * b_high))
+                low[i, j] = low[i, j] + (rest - (a_high * b_low + a_low * lower[j, k]))
     return lower, inverse_of(lower, scale), {at: high[at] + low[at] for at in TRIANGLE}
 
 
@@ -449,8 +460,8 @@
     tail, head = call(
         edge_kernel,
         ((STATE, 8, NC), (STATE, 8, NC)),
-        [pl.BlockSpec(memory_space=pl.ANY)] * 2,
-        (residual, diag_gain),
+        [pl.BlockSpec(memory_space=pltpu.HBM)] * 2,
+        [pltpu.with_memory_space_constraint(x, pltpu.HBM) for x in (residual, diag_gain)],
         scratch=[pltpu.SemaphoreType.DMA((4,))],
     )
     below = lax.ppermute(tail, "cell", [(i, i + 1) for i in range(ends)])

time: 96.7 us -> 95.3 us (0.986)
  local copies, waits for them, and re-layouts: 1.62 us -> 0.02 us
    unnamed x11 -> x9, local copies, waits for them, and re-layouts: 1.62 us -> 0.02 us
where the time goes in v5:
time: 95.3 us; the launch traced here: 94.9 us
  starting transfers between devices  54.4 us (57%)
  blocking collectives  14.6 us (15%)
  Pallas kernels  13.8 us (14%)
  waiting for transfers between devices  10.8 us (11%)
  between operations  1.38 us (1%)
    all_to_all x1, starting transfers between devices, on_device(): lax.all_to_all(row, 'cell', 0, 0, axis_index_groups=MEETING, tiled=True)  33.4 us
    all_to_all x1, blocking collectives, on_device(): back = lax.all_to_all(vectors, 'inst', 0, 0, tiled=True)  14.6 us
    pallas_call x6, Pallas kernels, call(): pl.pallas_call(kernel, out_shape=shapes, in_specs=in_specs, out_specs=jax...  13.8 us
    ppermute x1, starting transfers between devices, on_device(): above = lax.ppermute(head, 'cell', [(i + 1, i) for i in range(ends)])  12.4 us
    all_to_all x1, waiting for transfers between devices, on_device(): patches = lax.all_to_all(chunks, 'inst', 0, 0, tiled=True)  8.58 us
    ppermute x1, starting transfers between devices, on_device(): below = lax.ppermute(tail, 'cell', [(i, i + 1) for i in range(ends)])  4.92 us
    all_to_all x1, starting transfers between devices, on_device(): patches = lax.all_to_all(chunks, 'inst', 0, 0, tiled=True)  3.68 us
  transfers between devices with their start and end apart: 4, of which 3 were waited for; matrix products, arithmetic and copies ran while one was open for 0% of the time, Pallas kernels for 3%

profile of v5, /device:TPU:1, one launch (start us, length us, event | category | flops | bytes accessed | tf_op | source)
XLA Modules:
  0.0 94.9 jit_solution(10963522980347555007)
XLA Ops:
  0.6 0.0 copy-start
  0.6 0.0 copy-start.1
  0.6 0.9 shard_map.68
  1.5 4.9 %collective-permute-start = (f32[6,8,256]{2,1,0:T(8,128)S(1)}, f32[6,8,256]{2,1,0:T(8,128)S(1)}, u32[]{:S(2)}, u32[]{:S(2)}) collective-permute-start(f32[6,8,256]{2,1,0:T(8,128)S(1)} %get-tuple-element.4), channel_id=1, source_target_pairs={{0,16},{16,32},{32,48},{48,64},{64,80},{80,96},{96,112},{112,128},... | collective-permute-start | bytes 147464 | tf_op jit(solution)/shard_map/ppermute | solution.py:467
  6.5 12.4 %collective-permute-start.1 = (f32[6,8,256]{2,1,0:T(8,128)S(1)}, f32[6,8,256]{2,1,0:T(8,128)S(1)}, u32[]{:S(2)}, u32[]{:S(2)}) collective-permute-start(f32[6,8,256]{2,1,0:T(8,128)S(1)} %get-tuple-element.5), channel_id=1, source_target_pairs={{16,0},{32,16},{48,32},{64,48},{80,64},{96,80},{112,96},{128,112},... | collective-permute-start | bytes 147464 | tf_op jit(solution)/shard_map/ppermute | solution.py:468
  18.9 0.0 collective-permute-done.below_ref
  18.9 0.8 collective-permute-done.1.above_ref
  19.7 0.0 copy-done
  19.7 0.0 copy-done.1
  19.7 0.9 shard_map.69
  20.7 0.0 copy-start.3
  20.7 3.7 %all-to-all-start = ((f32[16,48,128]{2,1,0:T(8,128)}), f32[16,48,128]{2,1,0:T(8,128)S(1)}, u32[]{:S(2)}, u32[]{:S(2)}) async-start(f32[16,48,128]{2,1,0:T(8,128)} %shard_map.69), calls=%async_computation | async-start | bytes 786432 | tf_op jit(solution)/shard_map/all_to_all | solution.py:470
  25.0 0.0 copy-done.3
  25.0 0.0 copy-start.2
  25.0 8.6 %all-to-all-done.in_ref = f32[16,48,128]{2,1,0:T(8,128)S(1)} async-done(((f32[16,48,128]{2,1,0:T(8,128)}), f32[16,48,128]{2,1,0:T(8,128)S(1)}, u32[]{:S(2)}, u32[]{:S(2)}) %all-to-all-start) | async-done | bytes 393248 | tf_op jit(solution)/shard_map/all_to_all | solution.py:470
  33.6 0.0 copy-done.2
  33.6 6.9 %shard_map.70 = f32[16,80,128]{2,1,0:T(8,128)S(1)} custom-call(f32[16,48,128]{2,1,0:T(8,128)S(1)} %all-to-all-done.in_ref, f32[4,5,5]{2,1,0:T(8,128)S(1)} %copy.8.jac_ref, f32[1]{0:T(128)S(6)} %copy.10.omega_ref, f32[7]{0:T(128)S(1)} %copy-done.2), custom_call_target="tpu_custom_call" | custom-call | flops 100000000 | bytes 2000000 | tf_op jit(solution)/shard_map/pallas_call | solution.py:442
  40.6 14.6 %all_to_all.21.in_ref = f32[16,80,128]{2,1,0:T(8,128)S(1)} all-to-all(f32[16,80,128]{2,1,0:T(8,128)S(1)} %shard_map.70), channel_id=1, replica_groups=mesh['cell'=64,'inst'=16] {'inst'}, dimensions={0} | all-to-all | bytes 1310720 | tf_op jit(solution)/shard_map/all_to_all | solution.py:485
  55.1 0.9 shard_map.71
  56.1 33.4 %all-to-all-start.2 = ((f32[64,1,128]{2,1,0:T(1,128)}), f32[64,1,128]{2,1,0:T(1,128)S(1)}, u32[]{:S(2)}, u32[]{:S(2)}) async-start(f32[64,1,128]{2,1,0:T(1,128)} %bitcast.1), calls=%async_computation.2 | async-start | bytes 65536 | tf_op jit(solution)/shard_map/all_to_all | solution.py:487
  89.5 2.5 %shard_map.72.vec_ref = f32[7,1,5,16,256]{4,3,2,1,0:T(8,128)S(1)} custom-call(f32[16,80,128]{2,1,0:T(8,128)S(1)} %all_to_all.21.in_ref), custom_call_target="tpu_custom_call" | custom-call | flops 1000000 | bytes 2000000 | tf_op jit(solution)/shard_map/pallas_call | solution.py:442
  91.9 1.3 %all-to-all-done.2 = f32[64,1,128]{2,1,0:T(1,128)S(1)} async-done(((f32[64,1,128]{2,1,0:T(1,128)}), f32[64,1,128]{2,1,0:T(1,128)S(1)}, u32[]{:S(2)}, u32[]{:S(2)}) %all-to-all-start.2) | async-done | bytes 32800 | tf_op jit(solution)/shard_map/all_to_all | solution.py:487
  93.3 1.6 %shard_map.73 = (f32[8,1,5,16,256]{4,3,2,1,0:T(8,128)}, f32[8,8]{1,0:T(8,128)}) custom-call(f32[64,128]{1,0:T(8,128)S(1)} %bitcast.4, f32[1,5,16,256]{3,2,1,0:T(8,128)S(1)} %copy-done, f32[7,1,5,16,256]{4,3,2,1,0:T(8,128)S(1)} %shard_map.72.vec_ref), custom_call_target="tpu_custom_call" | custom-call | flops 1000000 | bytes 2000000 | tf_op jit(solution)/shard_map/pallas_call | solution.py:442
  (1 shorter events, 0.0 us)
Async XLA Ops:
  0.6 19.1 %copy-start = (f32[1,5,16,256]{3,2,1,0:T(8,128)S(1)}, f32[1,5,16,256]{3,2,1,0:T(8,128)}, u32[]{:S(2)}) copy-start(f32[1,5,16,256]{3,2,1,0:T(8,128)} %res_ref.5) | copy-start | bytes 245764
  0.6 19.1 %copy-start.1 = (f32[1,16,256]{2,1,0:T(8,128)S(1)}, f32[1,16,256]{2,1,0:T(8,128)}, u32[]{:S(2)}) copy-start(f32[1,16,256]{2,1,0:T(8,128)} %gain_ref.3) | copy-start | bytes 49156
  1.5 17.3 %collective-permute-start = (f32[6,8,256]{2,1,0:T(8,128)S(1)}, f32[6,8,256]{2,1,0:T(8,128)S(1)}, u32[]{:S(2)}, u32[]{:S(2)}) collective-permute-start(f32[6,8,256]{2,1,0:T(8,128)S(1)} %get-tuple-element.4), channel_id=1, source_target_pairs={{0,16},{16,32},{32,48},{48,64},{64,80},{80,96},{96,112},{112,128},... | collective-permute-start | bytes 147464 | tf_op jit(solution)/shard_map/ppermute | solution.py:467
  6.5 13.3 %collective-permute-start.1 = (f32[6,8,256]{2,1,0:T(8,128)S(1)}, f32[6,8,256]{2,1,0:T(8,128)S(1)}, u32[]{:S(2)}, u32[]{:S(2)}) collective-permute-start(f32[6,8,256]{2,1,0:T(8,128)S(1)} %get-tuple-element.5), channel_id=1, source_target_pairs={{16,0},{32,16},{48,32},{64,48},{80,64},{96,80},{112,96},{128,112},... | collective-permute-start | bytes 147464 | tf_op jit(solution)/shard_map/ppermute | solution.py:468
  20.7 4.3 %copy-start.3 = (f32[4,5,5]{2,0,1:T(4,128)S(1)}, f32[4,5,5]{2,0,1:T(4,128)}, u32[]{:S(2)}) copy-start(f32[4,5,5]{2,0,1:T(4,128)} %param.7) | copy-start | bytes 1204
  20.7 12.9 %all-to-all-start = ((f32[16,48,128]{2,1,0:T(8,128)}), f32[16,48,128]{2,1,0:T(8,128)S(1)}, u32[]{:S(2)}, u32[]{:S(2)}) async-start(f32[16,48,128]{2,1,0:T(8,128)} %shard_map.69), calls=%async_computation | async-start | bytes 786432 | tf_op jit(solution)/shard_map/all_to_all | solution.py:470
  25.0 8.6 %copy-start.2 = (f32[7]{0:T(128)S(1)}, f32[7]{0:T(128)}, u32[]{:S(2)}) copy-start(f32[7]{0:T(128)} %shift_ref.1) | copy-start | bytes 88
  56.1 37.2 %all-to-all-start.2 = ((f32[64,1,128]{2,1,0:T(1,128)}), f32[64,1,128]{2,1,0:T(1,128)S(1)}, u32[]{:S(2)}, u32[]{:S(2)}) async-start(f32[64,1,128]{2,1,0:T(1,128)} %bitcast.1), calls=%async_computation.2 | async-start | bytes 65536 | tf_op jit(solution)/shard_map/all_to_all | solution.py:487

commit v6 on v5

--- a/solution.py
+++ b/solution.py
@@ -21,6 +21,7 @@
 MEETING = [[(i + CELLS // 2) % CELLS for i in range(CELLS)]]
 VMEM = pl.BlockSpec(memory_space=pltpu.VMEM)
 SMEM = pl.BlockSpec(memory_space=pltpu.SMEM)
+HBM = pl.BlockSpec(memory_space=pltpu.HBM)
 TILE = (8, 128)
 
 
@@ -44,12 +45,19 @@
     return high, a - high
 
 
-def pack_kernel(res_ref, gain_ref, below_ref, above_ref, out_ref):
+def pack_kernel(res_ref, gain_ref, near_ref, far_ref, jac_ref, omega_ref, shift_ref, out_ref, coef_ref):
     lane = lanes()
+    first = lax.rem(lax.axis_index("cell"), 2) == 0
+    numbers = [jac_ref[d, f, e] for d in range(4) for f in range(FIELDS) for e in range(FIELDS)]
+    numbers += [shift_ref[n] for n in range(S - 1)] + [omega_ref[0]]
+    for at, number in enumerate(numbers):
+        coef_ref[at : at + 1, :] = jnp.full((1, 128), number)
     group, place = lane // 32, lane % 32
     for field in range(STATE):
         own = res_ref.at[0, field] if field < FIELDS else gain_ref.at[0]
-        rows = [below_ref[field], own[0:8, :], own[8:16, :], above_ref[field]]
+        below = jnp.where(first, far_ref[field], near_ref[field])
+        above = jnp.where(first, near_ref[field], far_ref[field])
+        rows = [below, own[0:8, :], own[8:16, :], above]
         for parity in range(2):
             moved = []
             for part in range(4):
@@ -140,6 +148,7 @@
 
 
 TILES = INST * FIELDS
+JAC = 4 * FIELDS * FIELDS
 PITCH = 16
 
 
@@ -147,7 +156,7 @@
     return PITCH * (i * FIELDS + f) + 8
 
 
-def step_kernel(rotation, in_ref, jac_ref, omega_ref, shift_ref, out_ref, vec_ref, coef_ref, mix_ref, gain_ref, slot_ref):
+def step_kernel(rotation, in_ref, number_ref, out_ref, vec_ref, coef_ref, mix_ref, gain_ref, slot_ref):
     lane, sub = lanes(), sublanes()
     seg = segments()
     cell, inst = lax.axis_index("cell"), lax.axis_index("inst")
@@ -156,18 +165,17 @@
     row = cell * ROWS - HALO + part * 8 + sub
     col = inst * COLS - HALO + lane % 32
     inside = (row >= 0) & (row < NR) & (col >= 0) & (col < NC)
-    for d in range(4):
-        for f in range(FIELDS):
-            for e in range(FIELDS):
-                coef_ref[(d * FIELDS + f) * FIELDS + e] = jnp.full(TILE, jac_ref[d, f, e])
+    for at in range(JAC):
+        coef_ref[at] = jnp.broadcast_to(number_ref[at : at + 1, :], TILE)
     for i in range(INST):
         for f in range(FIELDS):
             vec_ref[0, pl.ds(tile_at(i, f), 8), :] = jnp.where(inside, in_ref[i, f * 8 : f * 8 + 8, :], 0.0)
         gain_ref[i] = in_ref[i, FIELDS * 8 : FIELDS * 8 + 8, :]
-    weights = [jnp.full(TILE, omega_ref[0] * w) for w in rotation]
+    omega = jnp.broadcast_to(number_ref[JAC + S - 1 : JAC + S, :], TILE)
+    weights = [omega * w for w in rotation]
 
     def step(n, carry):
-        shift = shift_ref[n]
+        shift = jnp.broadcast_to(number_ref[pl.ds(JAC + n, 1), :], TILE)
         slot = lax.rem(n, 4)
         aligned = lax.rem(lax.rem(slot, 2) * 16 + (slot // 2) * 64 + 128 - 32 * turn, 128)
         now, later = vec_ref.at[n], vec_ref.at[n + 1]
@@ -264,23 +272,23 @@
     for bit in (1, 2, 4):
         mask = (lane & bit) != 0
         columns = [merge_pair(columns[2 * q], columns[2 * q + 1], mask, bit, 1) for q in range(len(columns) // 2)]
-    high, low = fold_pair(columns[0], 64, 1)
-    pair = jnp.where(lane < 64, high, low)
+    pair = columns[0]
+    for shift in (64, 32, 16):
+        pair = fold_pair(pair, shift, 1)
+    pair = jnp.where(seg == SLOTS[0][0], pair[0], pair[1])
     for i in range(INST):
-        out_ref[i, 72:80, :] = pair
+        out_ref[i, 24:32, :] = jnp.where(in_slot(seg, 0), pair, out_ref[i, 24:32, :])
 
 
 def gram_kernel(in_ref, out_ref):
     lane, sub = lanes(), sublanes()
-    total, error = sum_pairs([in_ref[i, 72:80, :] for i in range(INST)])
-    lower = lane < 64
-    other = pltpu.roll(total, 64, 1)
-    low = jnp.where(lower, other, total) + jnp.where(lower, error, pltpu.roll(error, 64, 1))
-    pair = (jnp.where(lower, total, other), low)
-    for shift in (8, 16, 32):
-        pair = fold_pair(pair, shift, 1)
-    slot = lane // 8
-    row = jnp.where(slot == sub, pair[0], jnp.where(slot == sub + 8, pair[1], 0.0))
+    total, error = sum_pairs([in_ref[i, 24:32, :] for i in range(INST)])
+    high, low = fold_pair((total, error + pltpu.roll(total, 96, 1)), 8, 1)
+    here = (lane >= 48) & (lane < 56)
+    both = jnp.where(here, high, 0.0) + pltpu.roll(jnp.where(here, low, 0.0), 8, 1)
+    for shift in (16, 32, 64):
+        both = both + pltpu.roll(both, shift, 1)
+    row = jnp.where(lane // 16 == sub, both, 0.0)
     row = jnp.broadcast_to(jnp.sum(row, axis=0, keepdims=True), TILE)
     for q in range(CELLS // 8):
         out_ref[q * 8 : q * 8 + 8, :] = row
@@ -383,14 +391,14 @@
     return lower, inverse_of(lower, scale)
 
 
-def finish_kernel(rows_ref, res_ref, vec_ref, out_ref, factor_ref):
+def finish_kernel(rows_ref, res_ref, vec_ref, out_ref, factor_ref, done_ref, sems):
     lane, sub = lanes(), sublanes()
     pair = sum_pairs([rows_ref[q * 8 : q * 8 + 8, :] for q in range(CELLS // 8)])
     for shift in (1, 2, 4):
         pair = fold_pair(pair, shift, 0)
-    low_row = pair[1] + pltpu.roll(pair[0], 64, 1)
-    high = {(i, j): jnp.broadcast_to(pair[0][:, 8 * i + j : 8 * i + j + 1], TILE) for i, j in TRIANGLE}
-    low = {(i, j): jnp.broadcast_to(low_row[:, 8 * i + j : 8 * i + j + 1], TILE) for i, j in TRIANGLE}
+    low_row = pair[1] + pltpu.roll(pair[0], 128 - S, 1)
+    high = {(i, j): jnp.broadcast_to(pair[0][:, 16 * i + j : 16 * i + j + 1], TILE) for i, j in TRIANGLE}
+    low = {(i, j): jnp.broadcast_to(low_row[:, 16 * i + j : 16 * i + j + 1], TILE) for i, j in TRIANGLE}
     lower_one, inverse_one, rest = factor_pairs(high, low)
     half = {}
     for i in range(S):
@@ -413,6 +421,7 @@
     for i, j in TRIANGLE:
         block = jnp.where((sub == j) & (lane == i), lower[i, j], block)
     factor_ref[...] = block[:, :S]
+    copies = [pltpu.make_async_copy(done_ref.at[:, :, f], out_ref.at[:, :, f], sems.at[f]) for f in range(FIELDS)]
     for f in range(FIELDS):
         for part in range(2):
             for wide in range(2):
@@ -422,13 +431,17 @@
                     total = weight[a, 0] * v[0]
                     for b in range(1, a + 1):
                         total = total + weight[a, b] * v[b]
-                    out_ref[(a, *place)] = total
-
-
-def edge_kernel(res_ref, gain_ref, tail_ref, head_ref, sems):
+                    done_ref[(a, *place)] = total
+        copies[f].start()
+    for copy in copies:
+        copy.wait()
+
+
+def edge_kernel(res_ref, gain_ref, near_ref, far_ref, sems):
+    odd = lax.rem(lax.axis_index("cell"), 2)
     copies = []
-    for ref, start in ((tail_ref, 8), (head_ref, 0)):
-        rows = pl.ds(start, 8)
+    for ref, start in ((near_ref, 8 * (1 - odd)), (far_ref, 8 * odd)):
+        rows = pl.ds(pl.multiple_of(start, 8), 8)
         for source, target in ((res_ref.at[0, :, rows, :], ref.at[pl.ds(0, FIELDS)]), (gain_ref.at[:, rows, :], ref.at[pl.ds(FIELDS, 1)])):
             copies.append(pltpu.make_async_copy(source, target, sems.at[len(copies)]))
     for copy in copies:
@@ -437,13 +450,13 @@
         copy.wait()
 
 
-def call(kernel, out_shape, in_specs, args, scratch=(), flops=10**6):
+def call(kernel, out_shape, in_specs, args, scratch=(), flops=10**6, out_specs=None):
     shapes = jax.tree.map(lambda s: jax.ShapeDtypeStruct(s, jnp.float32), out_shape, is_leaf=lambda s: isinstance(s[0], int))
     return pl.pallas_call(
         kernel,
         out_shape=shapes,
         in_specs=in_specs,
-        out_specs=jax.tree.map(lambda _: VMEM, shapes),
+        out_specs=out_specs or jax.tree.map(lambda _: VMEM, shapes),
         scratch_shapes=scratch,
         compiler_params=pltpu.CompilerParams(vmem_limit_bytes=40 * 2**20),
         cost_estimate=pl.CostEstimate(flops=flops, transcendentals=0, bytes_accessed=2 * 10**6),
@@ -456,23 +469,30 @@
 
 
 def on_device(residual, diag_gain, flux_jac, omega, shifts):
-    ends = CELLS - 1
-    tail, head = call(
+    pairs = [(i, i + 1) for i in range(CELLS - 1)]
+    pairs = [pairs[0::2], pairs[1::2]]
+    near, far = call(
         edge_kernel,
         ((STATE, 8, NC), (STATE, 8, NC)),
-        [pl.BlockSpec(memory_space=pltpu.HBM)] * 2,
+        [HBM] * 2,
         [pltpu.with_memory_space_constraint(x, pltpu.HBM) for x in (residual, diag_gain)],
         scratch=[pltpu.SemaphoreType.DMA((4,))],
     )
-    below = lax.ppermute(tail, "cell", [(i, i + 1) for i in range(ends)])
-    above = lax.ppermute(head, "cell", [(i + 1, i) for i in range(ends)])
-    chunks = call(pack_kernel, (INST, STATE * 8, 128), [VMEM] * 4, (residual, diag_gain, below, above))
+    near, far = [
+        lax.ppermute(x, "cell", p + [(b, a) for a, b in p]) for x, p in zip((near, far), pairs)
+    ]
+    chunks, numbers = call(
+        pack_kernel,
+        ((INST, STATE * 8, 128), (JAC + 12, 128)),
+        [VMEM] * 4 + [SMEM] * 3,
+        (residual, diag_gain, near, far, flux_jac, omega, shifts),
+    )
     patches = lax.all_to_all(chunks, "inst", 0, 0, tiled=True)
     vectors = call(
         functools.partial(step_kernel, rotations(coupling_table())),
-        (INST, 80, 128),
-        [VMEM, SMEM, SMEM, SMEM],
-        (patches, flux_jac, omega, shifts),
+        (INST, 72, 128),
+        [VMEM, VMEM],
+        (patches, numbers),
         scratch=[
             pltpu.VMEM((S, PITCH * (TILES + 1), 128), jnp.float32),
             pltpu.VMEM((4 * FIELDS * FIELDS, *TILE), jnp.float32),
@@ -487,7 +507,12 @@
     rows = lax.all_to_all(row, "cell", 0, 0, axis_index_groups=MEETING, tiled=True)
     others = call(unpack_kernel, (S - 1, 1, FIELDS, ROWS, NC), [VMEM], (back,))
     return call(
-        finish_kernel, ((S, 1, FIELDS, ROWS, NC), (S, S)), [VMEM] * 3, (rows, residual, others)
+        finish_kernel,
+        ((S, 1, FIELDS, ROWS, NC), (S, S)),
+        [VMEM] * 3,
+        (rows, residual, others),
+        scratch=[pltpu.VMEM((S, 1, FIELDS, ROWS, NC), jnp.float32), pltpu.SemaphoreType.DMA((FIELDS,))],
+        out_specs=(HBM, VMEM),
     )
 
 

time: 95.3 us -> 93.4 us (0.980)
  blocking collectives: 14.6 us -> 24.8 us
  waiting for transfers between devices: 10.8 us -> 4.13 us
  starting transfers between devices: 54.4 us -> 48.7 us
    all_to_all x0 -> x1, blocking collectives: none -> 10.6 us  [on_device(): patches = lax.all_to_all(chunks, 'inst', 0, 0, tiled=True)]
    all_to_all x1 -> x0, waiting for transfers between devices: 8.58 us -> none  [on_device(): patches = lax.all_to_all(chunks, 'inst', 0, 0, tiled=True)]
    all_to_all x1 -> x0, starting transfers between devices: 3.68 us -> none  [on_device(): patches = lax.all_to_all(chunks, 'inst', 0, 0, tiled=True)]
    all_to_all x1, starting transfers between devices: 33.4 us -> 30.7 us  [on_device(): lax.all_to_all(row, 'cell', 0, 0, axis_index_groups=MEETING, tiled=True)]
    ppermute x2, waiting for transfers between devices: 0.85 us -> 2.79 us  [on_device(): lax.ppermute(x, 'cell', p + [(b, a) for a, b in p])]
  transfers between devices with their start and end apart: 4 -> 3, of which waited for: 3 -> 2; matrix products, arithmetic and copies ran while one was open for 0% -> 0% of each run, Pallas kernels for 3% -> 3%
where the time goes in v6:
time: 93.4 us; the launch traced here: 93 us
  starting transfers between devices  48.7 us (52%)
  blocking collectives  24.8 us (27%)
  Pallas kernels  14 us (15%)
  waiting for transfers between devices  4.13 us (4%)
  between operations  1.39 us (1%)
    all_to_all x1, starting transfers between devices, on_device(): lax.all_to_all(row, 'cell', 0, 0, axis_index_groups=MEETING, tiled=True)  30.7 us
    ppermute x2, starting transfers between devices, on_device(): lax.ppermute(x, 'cell', p + [(b, a) for a, b in p])  17.9 us
    all_to_all x1, blocking collectives, on_device(): back = lax.all_to_all(vectors, 'inst', 0, 0, tiled=True)  14.2 us
    pallas_call x6, Pallas kernels, call(): pl.pallas_call(kernel, out_shape=shapes, in_specs=in_specs, out_specs=out...  14 us
    all_to_all x1, blocking collectives, on_device(): patches = lax.all_to_all(chunks, 'inst', 0, 0, tiled=True)  10.6 us
    ppermute x2, waiting for transfers between devices, on_device(): lax.ppermute(x, 'cell', p + [(b, a) for a, b in p])  2.79 us
  transfers between devices with their start and end apart: 3, of which 2 were waited for; matrix products, arithmetic and copies ran while one was open for 0% of the time, Pallas kernels for 3%

profile of v6, /device:TPU:1, one launch (start us, length us, event | category | flops | bytes accessed | tf_op | source)
XLA Modules:
  0.0 93.0 jit_solution(9289512399891530935)
XLA Ops:
  0.6 0.0 copy-start
  0.6 0.0 copy-start.3
  0.6 0.9 shard_map.68
  1.6 0.0 copy-start.1
  1.6 16.0 %collective-permute-start = (f32[6,8,256]{2,1,0:T(8,128)S(1)}, f32[6,8,256]{2,1,0:T(8,128)S(1)}, u32[]{:S(2)}, u32[]{:S(2)}) collective-permute-start(f32[6,8,256]{2,1,0:T(8,128)S(1)} %get-tuple-element.6), channel_id=1, source_target_pairs={{0,16},{32,48},{64,80},{96,112},{128,144},{160,176},{192,208},{224... | collective-permute-start | bytes 147464 | tf_op jit(solution)/shard_map/ppermute | solution.py:482
  17.6 1.9 %collective-permute-start.1 = (f32[6,8,256]{2,1,0:T(8,128)S(1)}, f32[6,8,256]{2,1,0:T(8,128)S(1)}, u32[]{:S(2)}, u32[]{:S(2)}) collective-permute-start(f32[6,8,256]{2,1,0:T(8,128)S(1)} %get-tuple-element.7), channel_id=1, source_target_pairs={{16,32},{48,64},{80,96},{112,128},{144,160},{176,192},{208,224},{2... | collective-permute-start | bytes 147464 | tf_op jit(solution)/shard_map/ppermute | solution.py:482
  20.2 0.0 copy-done.3
  20.2 0.0 copy-start.2
  20.2 0.0 collective-permute-done.near_ref
  20.2 2.8 %collective-permute-done.1.far_ref = f32[6,8,256]{2,1,0:T(8,128)S(1)} collective-permute-done((f32[6,8,256]{2,1,0:T(8,128)S(1)}, f32[6,8,256]{2,1,0:T(8,128)S(1)}, u32[]{:S(2)}, u32[]{:S(2)}) %collective-permute-start.1) | collective-permute-done | bytes 49184 | tf_op jit(solution)/shard_map/ppermute | solution.py:482
  23.0 0.0 copy-done
  23.0 0.0 copy-done.1
  23.0 0.0 copy-done.2
  23.0 1.0 %shard_map.69 = (f32[16,48,128]{2,1,0:T(8,128)S(1)}, f32[112,128]{1,0:T(8,128)S(1)}) custom-call(f32[1,5,16,256]{3,2,1,0:T(8,128)S(1)} %copy-done, f32[1,16,256]{2,1,0:T(8,128)S(1)} %copy-done.1, f32[6,8,256]{2,1,0:T(8,128)S(1)} %collective-permute-done.near_ref, f32[6,8,256]{2,1,0:T(8,128)S(1)} %collective-permute-done.1.far_ref, ...), custom_call_target="tpu_custom_call" | custom-call | flops 1000000 | bytes 2000000 | tf_op jit(solution)/shard_map/pallas_call | solution.py:455
  24.0 10.6 %all_to_all.21.in_ref = f32[16,48,128]{2,1,0:T(8,128)S(1)} all-to-all(f32[16,48,128]{2,1,0:T(8,128)S(1)} %get-tuple-element.8), channel_id=1, replica_groups=mesh['cell'=64,'inst'=16] {'inst'}, dimensions={0} | all-to-all | bytes 786432 | tf_op jit(solution)/shard_map/all_to_all | solution.py:490
  34.6 6.4 %shard_map.70 = f32[16,72,128]{2,1,0:T(8,128)S(1)} custom-call(f32[16,48,128]{2,1,0:T(8,128)S(1)} %all_to_all.21.in_ref, f32[112,128]{1,0:T(8,128)S(1)} %get-tuple-element.9.number_ref), custom_call_target="tpu_custom_call" | custom-call | flops 100000000 | bytes 2000000 | tf_op jit(solution)/shard_map/pallas_call | solution.py:455
  41.0 14.2 %all_to_all.22.in_ref = f32[16,72,128]{2,1,0:T(8,128)S(1)} all-to-all(f32[16,72,128]{2,1,0:T(8,128)S(1)} %shard_map.70), channel_id=1, replica_groups=mesh['cell'=64,'inst'=16] {'inst'}, dimensions={0} | all-to-all | bytes 1179648 | tf_op jit(solution)/shard_map/all_to_all | solution.py:505
  55.2 1.0 %shard_map.71 = f32[64,128]{1,0:T(8,128)} custom-call(f32[16,72,128]{2,1,0:T(8,128)S(1)} %all_to_all.22.in_ref), custom_call_target="tpu_custom_call" | custom-call | flops 1000000 | bytes 2000000 | tf_op jit(solution)/shard_map/pallas_call | solution.py:455
  56.2 30.7 %all-to-all-start.2 = ((f32[64,1,128]{2,1,0:T(1,128)}), f32[64,1,128]{2,1,0:T(1,128)S(1)}, u32[]{:S(2)}, u32[]{:S(2)}) async-start(f32[64,1,128]{2,1,0:T(1,128)} %bitcast.1), calls=%async_computation.2 | async-start | bytes 65536 | tf_op jit(solution)/shard_map/all_to_all | solution.py:507
  87.0 2.5 %shard_map.72.vec_ref = f32[7,1,5,16,256]{4,3,2,1,0:T(8,128)S(1)} custom-call(f32[16,72,128]{2,1,0:T(8,128)S(1)} %all_to_all.22.in_ref), custom_call_target="tpu_custom_call" | custom-call | flops 1000000 | bytes 2000000 | tf_op jit(solution)/shard_map/pallas_call | solution.py:455
  89.4 1.3 %all-to-all-done.2 = f32[64,1,128]{2,1,0:T(1,128)S(1)} async-done(((f32[64,1,128]{2,1,0:T(1,128)}), f32[64,1,128]{2,1,0:T(1,128)S(1)}, u32[]{:S(2)}, u32[]{:S(2)}) %all-to-all-start.2) | async-done | bytes 32800 | tf_op jit(solution)/shard_map/all_to_all | solution.py:507
  90.8 2.2 %shard_map.73 = (f32[8,1,5,16,256]{4,3,2,1,0:T(8,128)}, f32[8,8]{1,0:T(8,128)}) custom-call(f32[64,128]{1,0:T(8,128)S(1)} %bitcast.4, f32[1,5,16,256]{3,2,1,0:T(8,128)S(1)} %copy-done, f32[7,1,5,16,256]{4,3,2,1,0:T(8,128)S(1)} %shard_map.72.vec_ref), custom_call_target="tpu_custom_call" | custom-call | flops 1000000 | bytes 2000000 | tf_op jit(solution)/shard_map/pallas_call | solution.py:455
  (1 shorter events, 0.0 us)
Async XLA Ops:
  0.6 22.4 %copy-start = (f32[1,5,16,256]{3,2,1,0:T(8,128)S(1)}, f32[1,5,16,256]{3,2,1,0:T(8,128)}, u32[]{:S(2)}) copy-start(f32[1,5,16,256]{3,2,1,0:T(8,128)} %res_ref.5) | copy-start | bytes 245764
  0.6 19.5 %copy-start.3 = (f32[4,5,5]{2,0,1:T(4,128)S(1)}, f32[4,5,5]{2,0,1:T(4,128)}, u32[]{:S(2)}) copy-start(f32[4,5,5]{2,0,1:T(4,128)} %param.7) | copy-start | bytes 1204
  1.6 21.5 %copy-start.1 = (f32[1,16,256]{2,1,0:T(8,128)S(1)}, f32[1,16,256]{2,1,0:T(8,128)}, u32[]{:S(2)}) copy-start(f32[1,16,256]{2,1,0:T(8,128)} %gain_ref.3) | copy-start | bytes 49156
  1.6 18.6 %collective-permute-start = (f32[6,8,256]{2,1,0:T(8,128)S(1)}, f32[6,8,256]{2,1,0:T(8,128)S(1)}, u32[]{:S(2)}, u32[]{:S(2)}) collective-permute-start(f32[6,8,256]{2,1,0:T(8,128)S(1)} %get-tuple-element.6), channel_id=1, source_target_pairs={{0,16},{32,48},{64,80},{96,112},{128,144},{160,176},{192,208},{224... | collective-permute-start | bytes 147464 | tf_op jit(solution)/shard_map/ppermute | solution.py:482
  17.6 5.4 %collective-permute-start.1 = (f32[6,8,256]{2,1,0:T(8,128)S(1)}, f32[6,8,256]{2,1,0:T(8,128)S(1)}, u32[]{:S(2)}, u32[]{:S(2)}) collective-permute-start(f32[6,8,256]{2,1,0:T(8,128)S(1)} %get-tuple-element.7), channel_id=1, source_target_pairs={{16,32},{48,64},{80,96},{112,128},{144,160},{176,192},{208,224},{2... | collective-permute-start | bytes 147464 | tf_op jit(solution)/shard_map/ppermute | solution.py:482
  20.2 2.8 %copy-start.2 = (f32[7]{0:T(128)S(1)}, f32[7]{0:T(128)}, u32[]{:S(2)}) copy-start(f32[7]{0:T(128)} %shift_ref.1) | copy-start | bytes 88
  56.2 34.5 %all-to-all-start.2 = ((f32[64,1,128]{2,1,0:T(1,128)}), f32[64,1,128]{2,1,0:T(1,128)S(1)}, u32[]{:S(2)}, u32[]{:S(2)}) async-start(f32[64,1,128]{2,1,0:T(1,128)} %bitcast.1), calls=%async_computation.2 | async-start | bytes 65536 | tf_op jit(solution)/shard_map/all_to_all | solution.py:507

commit v7 on v6

--- a/solution.py
+++ b/solution.py
@@ -7,6 +7,7 @@
 from jax.experimental import pallas as pl
 from jax.experimental.pallas import tpu as pltpu
 from jax.sharding import PartitionSpec as P
+
 
 S = 8
 FIELDS = 5
@@ -20,9 +21,10 @@
 STATE = FIELDS + 1
 MEETING = [[(i + CELLS // 2) % CELLS for i in range(CELLS)]]
 VMEM = pl.BlockSpec(memory_space=pltpu.VMEM)
-SMEM = pl.BlockSpec(memory_space=pltpu.SMEM)
 HBM = pl.BlockSpec(memory_space=pltpu.HBM)
 TILE = (8, 128)
+JAC = 4 * FIELDS * FIELDS
+NUMBERS = JAC + S - 1 + 7
 
 
 def lanes():
@@ -45,14 +47,19 @@
     return high, a - high
 
 
-def pack_kernel(res_ref, gain_ref, near_ref, far_ref, jac_ref, omega_ref, shift_ref, out_ref, coef_ref):
+def pack_kernel(rotation, res_ref, gain_ref, near_ref, far_ref, jac_ref, scalar_ref, out_ref, coef_ref):
     lane = lanes()
     first = lax.rem(lax.axis_index("cell"), 2) == 0
-    numbers = [jac_ref[d, f, e] for d in range(4) for f in range(FIELDS) for e in range(FIELDS)]
-    numbers += [shift_ref[n] for n in range(S - 1)] + [omega_ref[0]]
-    for at, number in enumerate(numbers):
-        coef_ref[at : at + 1, :] = jnp.full((1, 128), number)
     group, place = lane // 32, lane % 32
+    for f in range(FIELDS):
+        for e in range(FIELDS):
+            at = 4 * (f * FIELDS + e)
+            coef_ref[at : at + 4, :] = jnp.broadcast_to(jac_ref[f, :, e : e + 1], (4, 128))
+    for n in range(S - 1):
+        coef_ref[JAC + n : JAC + n + 1, :] = jnp.broadcast_to(scalar_ref[:, n : n + 1], (1, 128))
+    omega = jnp.broadcast_to(scalar_ref[:, S - 1 : S], (1, 128))
+    for at, weight in enumerate(rotation, JAC + S - 1):
+        coef_ref[at : at + 1, :] = omega * weight
     for field in range(STATE):
         own = res_ref.at[0, field] if field < FIELDS else gain_ref.at[0]
         below = jnp.where(first, far_ref[field], near_ref[field])
@@ -148,7 +155,6 @@
 
 
 TILES = INST * FIELDS
-JAC = 4 * FIELDS * FIELDS
 PITCH = 16
 
 
@@ -156,7 +162,7 @@
     return PITCH * (i * FIELDS + f) + 8
 
 
-def step_kernel(rotation, in_ref, number_ref, out_ref, vec_ref, coef_ref, mix_ref, gain_ref, slot_ref):
+def step_kernel(in_ref, number_ref, out_ref, vec_ref, coef_ref, mix_ref, gain_ref, slot_ref):
     lane, sub = lanes(), sublanes()
     seg = segments()
     cell, inst = lax.axis_index("cell"), lax.axis_index("inst")
@@ -165,14 +171,17 @@
     row = cell * ROWS - HALO + part * 8 + sub
     col = inst * COLS - HALO + lane % 32
     inside = (row >= 0) & (row < NR) & (col >= 0) & (col < NC)
-    for at in range(JAC):
-        coef_ref[at] = jnp.broadcast_to(number_ref[at : at + 1, :], TILE)
+    for d in range(4):
+        for f in range(FIELDS):
+            for e in range(FIELDS):
+                at = 4 * (f * FIELDS + e) + d
+                coef_ref[(d * FIELDS + f) * FIELDS + e] = jnp.broadcast_to(number_ref[at : at + 1, :], TILE)
     for i in range(INST):
         for f in range(FIELDS):
             vec_ref[0, pl.ds(tile_at(i, f), 8), :] = jnp.where(inside, in_ref[i, f * 8 : f * 8 + 8, :], 0.0)
         gain_ref[i] = in_ref[i, FIELDS * 8 : FIELDS * 8 + 8, :]
-    omega = jnp.broadcast_to(number_ref[JAC + S - 1 : JAC + S, :], TILE)
-    weights = [omega * w for w in rotation]
+
+    weights = [jnp.broadcast_to(number_ref[at : at + 1, :], TILE) for at in range(JAC + S - 1, NUMBERS)]
 
     def step(n, carry):
         shift = jnp.broadcast_to(number_ref[pl.ds(JAC + n, 1), :], TILE)
@@ -391,7 +400,7 @@
     return lower, inverse_of(lower, scale)
 
 
-def finish_kernel(rows_ref, res_ref, vec_ref, out_ref, factor_ref, done_ref, sems):
+def finish_kernel(rows_ref, res_ref, vec_ref, out_ref, factor_ref):
     lane, sub = lanes(), sublanes()
     pair = sum_pairs([rows_ref[q * 8 : q * 8 + 8, :] for q in range(CELLS // 8)])
     for shift in (1, 2, 4):
@@ -421,7 +430,6 @@
     for i, j in TRIANGLE:
         block = jnp.where((sub == j) & (lane == i), lower[i, j], block)
     factor_ref[...] = block[:, :S]
-    copies = [pltpu.make_async_copy(done_ref.at[:, :, f], out_ref.at[:, :, f], sems.at[f]) for f in range(FIELDS)]
     for f in range(FIELDS):
         for part in range(2):
             for wide in range(2):
@@ -431,10 +439,7 @@
                     total = weight[a, 0] * v[0]
                     for b in range(1, a + 1):
                         total = total + weight[a, b] * v[b]
-                    done_ref[(a, *place)] = total
-        copies[f].start()
-    for copy in copies:
-        copy.wait()
+                    out_ref[(a, *place)] = total
 
 
 def edge_kernel(res_ref, gain_ref, near_ref, far_ref, sems):
@@ -450,13 +455,13 @@
         copy.wait()
 
 
-def call(kernel, out_shape, in_specs, args, scratch=(), flops=10**6, out_specs=None):
+def call(kernel, out_shape, in_specs, args, scratch=(), flops=10**6):
     shapes = jax.tree.map(lambda s: jax.ShapeDtypeStruct(s, jnp.float32), out_shape, is_leaf=lambda s: isinstance(s[0], int))
     return pl.pallas_call(
         kernel,
         out_shape=shapes,
         in_specs=in_specs,
-        out_specs=out_specs or jax.tree.map(lambda _: VMEM, shapes),
+        out_specs=jax.tree.map(lambda _: VMEM, shapes),
         scratch_shapes=scratch,
         compiler_params=pltpu.CompilerParams(vmem_limit_bytes=40 * 2**20),
         cost_estimate=pl.CostEstimate(flops=flops, transcendentals=0, bytes_accessed=2 * 10**6),
@@ -478,24 +483,23 @@
         [pltpu.with_memory_space_constraint(x, pltpu.HBM) for x in (residual, diag_gain)],
         scratch=[pltpu.SemaphoreType.DMA((4,))],
     )
-    near, far = [
-        lax.ppermute(x, "cell", p + [(b, a) for a, b in p]) for x, p in zip((near, far), pairs)
-    ]
+    far = lax.ppermute(far, "cell", pairs[1] + [(b, a) for a, b in pairs[1]])
+    near = lax.ppermute(near, "cell", pairs[0] + [(b, a) for a, b in pairs[0]])
     chunks, numbers = call(
-        pack_kernel,
-        ((INST, STATE * 8, 128), (JAC + 12, 128)),
-        [VMEM] * 4 + [SMEM] * 3,
-        (residual, diag_gain, near, far, flux_jac, omega, shifts),
+        functools.partial(pack_kernel, rotations(coupling_table())),
+        ((INST, STATE * 8, 128), (NUMBERS + 6, 128)),
+        [VMEM] * 6,
+        (residual, diag_gain, near, far, flux_jac.transpose(1, 0, 2), jnp.concatenate([shifts, omega])[None]),
     )
     patches = lax.all_to_all(chunks, "inst", 0, 0, tiled=True)
     vectors = call(
-        functools.partial(step_kernel, rotations(coupling_table())),
+        step_kernel,
         (INST, 72, 128),
         [VMEM, VMEM],
         (patches, numbers),
         scratch=[
             pltpu.VMEM((S, PITCH * (TILES + 1), 128), jnp.float32),
-            pltpu.VMEM((4 * FIELDS * FIELDS, *TILE), jnp.float32),
+            pltpu.VMEM((JAC, *TILE), jnp.float32),
             pltpu.VMEM((INST, FIELDS, *TILE), jnp.float32),
             pltpu.VMEM((INST, *TILE), jnp.float32),
             pltpu.VMEM((S - 1, INST, FIELDS, *TILE), jnp.float32),
@@ -511,8 +515,6 @@
         ((S, 1, FIELDS, ROWS, NC), (S, S)),
         [VMEM] * 3,
         (rows, residual, others),
-        scratch=[pltpu.VMEM((S, 1, FIELDS, ROWS, NC), jnp.float32), pltpu.SemaphoreType.DMA((FIELDS,))],
-        out_specs=(HBM, VMEM),
     )
 
 

time: 93.4 us -> 92.6 us (level)
  Pallas kernels: 14 us -> 12.6 us
    pallas_call x6, Pallas kernels: 14 us -> 12.6 us  [call(): pl.pallas_call(kernel, out_shape=shapes, in_specs=in_specs, out_specs=jax...]
where the time goes in v7:
time: 92.6 us; the launch traced here: 92.2 us
  starting transfers between devices  49.2 us (53%)
  blocking collectives  24.2 us (26%)
  Pallas kernels  12.6 us (14%)
  waiting for transfers between devices  4.08 us (4%)
  between operations  1.36 us (1%)
    all_to_all x1, starting transfers between devices, on_device(): lax.all_to_all(row, 'cell', 0, 0, axis_index_groups=MEETING, tiled=True)  31.3 us
    ppermute x1, starting transfers between devices, on_device(): near = lax.ppermute(near, 'cell', pairs[0] + [(b, a) for a, b in pairs[0]])  16 us
    all_to_all x1, blocking collectives, on_device(): back = lax.all_to_all(vectors, 'inst', 0, 0, tiled=True)  13.7 us
    pallas_call x6, Pallas kernels, call(): pl.pallas_call(kernel, out_shape=shapes, in_specs=in_specs, out_specs=jax...  12.6 us
    all_to_all x1, blocking collectives, on_device(): patches = lax.all_to_all(chunks, 'inst', 0, 0, tiled=True)  10.6 us
    ppermute x1, waiting for transfers between devices, on_device(): far = lax.ppermute(far, 'cell', pairs[1] + [(b, a) for a, b in pairs[1]])  2.74 us
    ppermute x1, starting transfers between devices, on_device(): far = lax.ppermute(far, 'cell', pairs[1] + [(b, a) for a, b in pairs[1]])  1.92 us
  transfers between devices with their start and end apart: 3, of which 2 were waited for; matrix products, arithmetic and copies ran while one was open for 0% of the time, Pallas kernels for 3%

profile of v7, /device:TPU:1, one launch (start us, length us, event | category | flops | bytes accessed | tf_op | source)
XLA Modules:
  0.0 92.2 jit_solution(8505580714627503696)
XLA Ops:
  0.6 0.0 copy-start
  0.6 0.0 copy-start.1
  0.6 0.9 shard_map.68
  1.6 16.0 %collective-permute-start = (f32[6,8,256]{2,1,0:T(8,128)S(1)}, f32[6,8,256]{2,1,0:T(8,128)S(1)}, u32[]{:S(2)}, u32[]{:S(2)}) collective-permute-start(f32[6,8,256]{2,1,0:T(8,128)S(1)} %get-tuple-element.6), channel_id=1, source_target_pairs={{0,16},{32,48},{64,80},{96,112},{128,144},{160,176},{192,208},{224... | collective-permute-start | bytes 147464 | tf_op jit(solution)/shard_map/ppermute | solution.py:487
  17.6 0.0 copy-start.3
  17.6 1.9 %collective-permute-start.1 = (f32[6,8,256]{2,1,0:T(8,128)S(1)}, f32[6,8,256]{2,1,0:T(8,128)S(1)}, u32[]{:S(2)}, u32[]{:S(2)}) collective-permute-start(f32[6,8,256]{2,1,0:T(8,128)S(1)} %get-tuple-element.7), channel_id=1, source_target_pairs={{16,32},{48,64},{80,96},{112,128},{144,160},{176,192},{208,224},{2... | collective-permute-start | bytes 147464 | tf_op jit(solution)/shard_map/ppermute | solution.py:486
  20.2 0.0 copy-done.3
  20.2 0.1 maximum_bitcast_fusion.scalar_ref
  20.3 0.0 collective-permute-done.near_ref
  20.3 2.7 %collective-permute-done.1.far_ref = f32[6,8,256]{2,1,0:T(8,128)S(1)} collective-permute-done((f32[6,8,256]{2,1,0:T(8,128)S(1)}, f32[6,8,256]{2,1,0:T(8,128)S(1)}, u32[]{:S(2)}, u32[]{:S(2)}) %collective-permute-start.1) | collective-permute-done | bytes 49184 | tf_op jit(solution)/shard_map/ppermute | solution.py:486
  23.0 0.0 copy-done
  23.0 0.0 copy-done.1
  23.0 0.0 copy-start.2
  23.0 0.7 copy-done.2
  23.7 0.2 shard_map.69
  23.9 10.6 %all_to_all.21.in_ref = f32[16,48,128]{2,1,0:T(8,128)S(1)} all-to-all(f32[16,48,128]{2,1,0:T(8,128)S(1)} %get-tuple-element.8), channel_id=1, replica_groups=mesh['cell'=64,'inst'=16] {'inst'}, dimensions={0} | all-to-all | bytes 786432 | tf_op jit(solution)/shard_map/all_to_all | solution.py:494
  34.5 6.3 %shard_map.70 = f32[16,72,128]{2,1,0:T(8,128)S(1)} custom-call(f32[16,48,128]{2,1,0:T(8,128)S(1)} %all_to_all.21.in_ref, f32[120,128]{1,0:T(8,128)S(1)} %get-tuple-element.9.number_ref), custom_call_target="tpu_custom_call" | custom-call | flops 100000000 | bytes 2000000 | tf_op jit(solution)/shard_map/pallas_call | solution.py:460
  40.8 13.7 %all_to_all.22.in_ref = f32[16,72,128]{2,1,0:T(8,128)S(1)} all-to-all(f32[16,72,128]{2,1,0:T(8,128)S(1)} %shard_map.70), channel_id=1, replica_groups=mesh['cell'=64,'inst'=16] {'inst'}, dimensions={0} | all-to-all | bytes 1179648 | tf_op jit(solution)/shard_map/all_to_all | solution.py:509
  54.5 1.0 %shard_map.71 = f32[64,128]{1,0:T(8,128)} custom-call(f32[16,72,128]{2,1,0:T(8,128)S(1)} %all_to_all.22.in_ref), custom_call_target="tpu_custom_call" | custom-call | flops 1000000 | bytes 2000000 | tf_op jit(solution)/shard_map/pallas_call | solution.py:460
  55.5 31.3 %all-to-all-start.2 = ((f32[64,1,128]{2,1,0:T(1,128)}), f32[64,1,128]{2,1,0:T(1,128)S(1)}, u32[]{:S(2)}, u32[]{:S(2)}) async-start(f32[64,1,128]{2,1,0:T(1,128)} %bitcast.3), calls=%async_computation.2 | async-start | bytes 65536 | tf_op jit(solution)/shard_map/all_to_all | solution.py:511
  86.8 2.5 %shard_map.72.vec_ref = f32[7,1,5,16,256]{4,3,2,1,0:T(8,128)S(1)} custom-call(f32[16,72,128]{2,1,0:T(8,128)S(1)} %all_to_all.22.in_ref), custom_call_target="tpu_custom_call" | custom-call | flops 1000000 | bytes 2000000 | tf_op jit(solution)/shard_map/pallas_call | solution.py:460
  89.3 1.3 %all-to-all-done.2 = f32[64,1,128]{2,1,0:T(1,128)S(1)} async-done(((f32[64,1,128]{2,1,0:T(1,128)}), f32[64,1,128]{2,1,0:T(1,128)S(1)}, u32[]{:S(2)}, u32[]{:S(2)}) %all-to-all-start.2) | async-done | bytes 32800 | tf_op jit(solution)/shard_map/all_to_all | solution.py:511
  90.6 1.6 %shard_map.73 = (f32[8,1,5,16,256]{4,3,2,1,0:T(8,128)}, f32[8,8]{1,0:T(8,128)}) custom-call(f32[64,128]{1,0:T(8,128)S(1)} %bitcast.7, f32[1,5,16,256]{3,2,1,0:T(8,128)S(1)} %copy-done, f32[7,1,5,16,256]{4,3,2,1,0:T(8,128)S(1)} %shard_map.72.vec_ref), custom_call_target="tpu_custom_call" | custom-call | flops 1000000 | bytes 2000000 | tf_op jit(solution)/shard_map/pallas_call | solution.py:460
Async XLA Ops:
  0.6 22.4 %copy-start = (f32[1,5,16,256]{3,2,1,0:T(8,128)S(1)}, f32[1,5,16,256]{3,2,1,0:T(8,128)}, u32[]{:S(2)}) copy-start(f32[1,5,16,256]{3,2,1,0:T(8,128)} %res_ref.5) | copy-start | bytes 245764
  0.6 22.4 %copy-start.1 = (f32[1,16,256]{2,1,0:T(8,128)S(1)}, f32[1,16,256]{2,1,0:T(8,128)}, u32[]{:S(2)}) copy-start(f32[1,16,256]{2,1,0:T(8,128)} %gain_ref.3) | copy-start | bytes 49156
  1.6 18.7 %collective-permute-start = (f32[6,8,256]{2,1,0:T(8,128)S(1)}, f32[6,8,256]{2,1,0:T(8,128)S(1)}, u32[]{:S(2)}, u32[]{:S(2)}) collective-permute-start(f32[6,8,256]{2,1,0:T(8,128)S(1)} %get-tuple-element.6), channel_id=1, source_target_pairs={{0,16},{32,48},{64,80},{96,112},{128,144},{160,176},{192,208},{224... | collective-permute-start | bytes 147464 | tf_op jit(solution)/shard_map/ppermute | solution.py:487
  17.6 2.6 %copy-start.3 = (f32[7]{0:T(128)S(1)}, f32[7]{0:T(128)}, u32[]{:S(2)}) copy-start(f32[7]{0:T(128)} %param.9) | copy-start | bytes 88
  17.6 5.4 %collective-permute-start.1 = (f32[6,8,256]{2,1,0:T(8,128)S(1)}, f32[6,8,256]{2,1,0:T(8,128)S(1)}, u32[]{:S(2)}, u32[]{:S(2)}) collective-permute-start(f32[6,8,256]{2,1,0:T(8,128)S(1)} %get-tuple-element.7), channel_id=1, source_target_pairs={{16,32},{48,64},{80,96},{112,128},{144,160},{176,192},{208,224},{2... | collective-permute-start | bytes 147464 | tf_op jit(solution)/shard_map/ppermute | solution.py:486
  23.0 0.7 copy-start.2
  55.5 35.1 %all-to-all-start.2 = ((f32[64,1,128]{2,1,0:T(1,128)}), f32[64,1,128]{2,1,0:T(1,128)S(1)}, u32[]{:S(2)}, u32[]{:S(2)}) async-start(f32[64,1,128]{2,1,0:T(1,128)} %bitcast.3), calls=%async_computation.2 | async-start | bytes 65536 | tf_op jit(solution)/shard_map/all_to_all | solution.py:511

commit v8 on v7

--- a/solution.py
+++ b/solution.py
@@ -47,7 +47,7 @@
     return high, a - high
 
 
-def pack_kernel(rotation, res_ref, gain_ref, near_ref, far_ref, jac_ref, scalar_ref, out_ref, coef_ref):
+def pack_kernel(rotation, res_ref, gain_ref, near_ref, far_ref, jac_ref, omega_ref, shift_ref, out_ref, coef_ref):
     lane = lanes()
     first = lax.rem(lax.axis_index("cell"), 2) == 0
     group, place = lane // 32, lane % 32
@@ -56,8 +56,8 @@
             at = 4 * (f * FIELDS + e)
             coef_ref[at : at + 4, :] = jnp.broadcast_to(jac_ref[f, :, e : e + 1], (4, 128))
     for n in range(S - 1):
-        coef_ref[JAC + n : JAC + n + 1, :] = jnp.broadcast_to(scalar_ref[:, n : n + 1], (1, 128))
-    omega = jnp.broadcast_to(scalar_ref[:, S - 1 : S], (1, 128))
+        coef_ref[JAC + n : JAC + n + 1, :] = jnp.broadcast_to(shift_ref[:, n : n + 1], (1, 128))
+    omega = jnp.full((1, 128), omega_ref[0])
     for at, weight in enumerate(rotation, JAC + S - 1):
         coef_ref[at : at + 1, :] = omega * weight
     for field in range(STATE):
@@ -198,8 +198,8 @@
             mixed = coupled([now[pl.ds(tile_at(i, f), 8), :] for i in range(INST)], weights)
             for i in range(INST):
                 mix_ref[i, f] = mixed[i]
-        for pair in range(0, INST, 2):
-            members = (pair, pair + 1)
+        for pair in range(0, INST, 4):
+            members = (pair, pair + 1, pair + 2, pair + 3)
             near, center, gain = {}, {}, {}
             for i in members:
                 gain[i] = gain_ref[i] - shift
@@ -212,15 +212,16 @@
                     near[i, 1, e] = now[pl.ds(at + 1, 8), :]
                     near[i, 2, e] = pltpu.roll(v, 1, 1)
                     near[i, 3, e] = pltpu.roll(v, 127, 1)
-            for f in range(FIELDS):
-                total = {i: mix_ref[i, f] + gain[i] * center[i, f] for i in members}
+            total = {(i, f): mix_ref[i, f] + gain[i] * center[i, f] for i in members for f in range(FIELDS)}
+            for e in range(FIELDS):
                 for d in range(4):
-                    for e in range(FIELDS):
+                    for f in range(FIELDS):
                         c = coef_ref[(d * FIELDS + f) * FIELDS + e]
                         for i in members:
-                            total[i] = total[i] - c * near[i, d, e]
-                for i in members:
-                    later[pl.ds(tile_at(i, f), 8), :] = jnp.where(inside, total[i], 0.0)
+                            total[i, f] = total[i, f] - c * near[i, d, e]
+            for i in members:
+                for f in range(FIELDS):
+                    later[pl.ds(tile_at(i, f), 8), :] = jnp.where(inside, total[i, f], 0.0)
         return carry
 
     lax.fori_loop(0, S - 1, step, 0)
@@ -442,13 +443,14 @@
                     out_ref[(a, *place)] = total
 
 
-def edge_kernel(res_ref, gain_ref, near_ref, far_ref, sems):
+def edge_kernel(res_ref, gain_ref, jac_ref, shift_ref, near_ref, far_ref, jac_out, shift_out, sems):
     odd = lax.rem(lax.axis_index("cell"), 2)
-    copies = []
-    for ref, start in ((near_ref, 8 * (1 - odd)), (far_ref, 8 * odd)):
+    moves = [(jac_ref, jac_out), (shift_ref, shift_out)]
+    for ref, start in ((far_ref, 8 * odd), (near_ref, 8 * (1 - odd))):
         rows = pl.ds(pl.multiple_of(start, 8), 8)
-        for source, target in ((res_ref.at[0, :, rows, :], ref.at[pl.ds(0, FIELDS)]), (gain_ref.at[:, rows, :], ref.at[pl.ds(FIELDS, 1)])):
-            copies.append(pltpu.make_async_copy(source, target, sems.at[len(copies)]))
+        moves.append((res_ref.at[0, :, rows, :], ref.at[pl.ds(0, FIELDS)]))
+        moves.append((gain_ref.at[:, rows, :], ref.at[pl.ds(FIELDS, 1)]))
+    copies = [pltpu.make_async_copy(*move, sems.at[n]) for n, move in enumerate(moves)]
     for copy in copies:
         copy.start()
     for copy in copies:
@@ -476,20 +478,21 @@
 def on_device(residual, diag_gain, flux_jac, omega, shifts):
     pairs = [(i, i + 1) for i in range(CELLS - 1)]
     pairs = [pairs[0::2], pairs[1::2]]
-    near, far = call(
+    held = (residual, diag_gain, flux_jac.transpose(1, 0, 2), shifts[None])
+    near, far, jac, shift = call(
         edge_kernel,
-        ((STATE, 8, NC), (STATE, 8, NC)),
-        [HBM] * 2,
-        [pltpu.with_memory_space_constraint(x, pltpu.HBM) for x in (residual, diag_gain)],
-        scratch=[pltpu.SemaphoreType.DMA((4,))],
+        ((STATE, 8, NC), (STATE, 8, NC), *[x.shape for x in held[2:]]),
+        [HBM] * 4,
+        [pltpu.with_memory_space_constraint(x, pltpu.HBM) for x in held],
+        scratch=[pltpu.SemaphoreType.DMA((6,))],
     )
     far = lax.ppermute(far, "cell", pairs[1] + [(b, a) for a, b in pairs[1]])
     near = lax.ppermute(near, "cell", pairs[0] + [(b, a) for a, b in pairs[0]])
     chunks, numbers = call(
         functools.partial(pack_kernel, rotations(coupling_table())),
         ((INST, STATE * 8, 128), (NUMBERS + 6, 128)),
-        [VMEM] * 6,
-        (residual, diag_gain, near, far, flux_jac.transpose(1, 0, 2), jnp.concatenate([shifts, omega])[None]),
+        [VMEM] * 5 + [pl.BlockSpec(memory_space=pltpu.SMEM), VMEM],
+        (residual, diag_gain, near, far, jac, omega, shift),
     )
     patches = lax.all_to_all(chunks, "inst", 0, 0, tiled=True)
     vectors = call(

time: 92.6 us -> 91.6 us (0.989)
  no operation moved by 1% of the time
where the time goes in v8:
time: 91.6 us; the launch traced here: 91.3 us
  starting transfers between devices  49.3 us (54%)
  blocking collectives  24.2 us (26%)
  Pallas kernels  12.4 us (14%)
  waiting for transfers between devices  4.16 us (5%)
  between operations  1.35 us (1%)
    all_to_all x1, starting transfers between devices, on_device(): lax.all_to_all(row, 'cell', 0, 0, axis_index_groups=MEETING, tiled=True)  31.3 us
    ppermute x1, starting transfers between devices, on_device(): near = lax.ppermute(near, 'cell', pairs[0] + [(b, a) for a, b in pairs[0]])  16 us
    all_to_all x1, blocking collectives, on_device(): back = lax.all_to_all(vectors, 'inst', 0, 0, tiled=True)  13.6 us
    pallas_call x6, Pallas kernels, call(): pl.pallas_call(kernel, out_shape=shapes, in_specs=in_specs, out_specs=jax...  12.4 us
    all_to_all x1, blocking collectives, on_device(): patches = lax.all_to_all(chunks, 'inst', 0, 0, tiled=True)  10.6 us
    ppermute x1, waiting for transfers between devices, on_device(): far = lax.ppermute(far, 'cell', pairs[1] + [(b, a) for a, b in pairs[1]])  2.82 us
    ppermute x1, starting transfers between devices, on_device(): far = lax.ppermute(far, 'cell', pairs[1] + [(b, a) for a, b in pairs[1]])  1.92 us
  transfers between devices with their start and end apart: 3, of which 2 were waited for; matrix products, arithmetic and copies ran while one was open for 0% of the time, Pallas kernels for 3%

profile of v8, /device:TPU:1, one launch (start us, length us, event | category | flops | bytes accessed | tf_op | source)
XLA Modules:
  0.0 91.3 jit_solution(12969835513115206523)
XLA Ops:
  0.6 0.0 copy-start
  0.6 0.0 copy-start.1
  0.7 0.9 %shard_map.68 = (f32[6,8,256]{2,1,0:T(8,128)S(1)}, f32[6,8,256]{2,1,0:T(8,128)S(1)}, f32[5,4,5]{2,1,0:T(4,128)S(1)}, f32[1,7]{1,0:T(1,128)S(1)}) custom-call(f32[1,5,16,256]{3,2,1,0:T(8,128)} %res_ref.5, f32[1,16,256]{2,1,0:T(8,128)} %gain_ref.3, f32[5,4,5]{2,1,0:T(4,128)} %bitcast.7, f32[1,7]{1,0:T(1,128)} %bitcast.8), custom_call_target="tpu_custom_call" | custom-call | flops 1000000 | bytes 2000000 | tf_op jit(solution)/shard_map/pallas_call | solution.py:462
  1.6 16.0 %collective-permute-start = (f32[6,8,256]{2,1,0:T(8,128)S(1)}, f32[6,8,256]{2,1,0:T(8,128)S(1)}, u32[]{:S(2)}, u32[]{:S(2)}) collective-permute-start(f32[6,8,256]{2,1,0:T(8,128)S(1)} %get-tuple-element.8), channel_id=1, source_target_pairs={{0,16},{32,48},{64,80},{96,112},{128,144},{160,176},{192,208},{224... | collective-permute-start | bytes 147464 | tf_op jit(solution)/shard_map/ppermute | solution.py:490
  17.6 1.9 %collective-permute-start.1 = (f32[6,8,256]{2,1,0:T(8,128)S(1)}, f32[6,8,256]{2,1,0:T(8,128)S(1)}, u32[]{:S(2)}, u32[]{:S(2)}) collective-permute-start(f32[6,8,256]{2,1,0:T(8,128)S(1)} %get-tuple-element.9), channel_id=1, source_target_pairs={{16,32},{48,64},{80,96},{112,128},{144,160},{176,192},{208,224},{2... | collective-permute-start | bytes 147464 | tf_op jit(solution)/shard_map/ppermute | solution.py:489
  20.2 0.0 collective-permute-done.near_ref
  20.2 2.8 %collective-permute-done.1.far_ref = f32[6,8,256]{2,1,0:T(8,128)S(1)} collective-permute-done((f32[6,8,256]{2,1,0:T(8,128)S(1)}, f32[6,8,256]{2,1,0:T(8,128)S(1)}, u32[]{:S(2)}, u32[]{:S(2)}) %collective-permute-start.1) | collective-permute-done | bytes 49184 | tf_op jit(solution)/shard_map/ppermute | solution.py:489
  23.0 0.0 copy-done
  23.0 0.0 copy-done.1
  23.0 0.2 shard_map.69
  23.3 10.6 %all_to_all.21.in_ref = f32[16,48,128]{2,1,0:T(8,128)S(1)} all-to-all(f32[16,48,128]{2,1,0:T(8,128)S(1)} %get-tuple-element.12), channel_id=1, replica_groups=mesh['cell'=64,'inst'=16] {'inst'}, dimensions={0} | all-to-all | bytes 786432 | tf_op jit(solution)/shard_map/all_to_all | solution.py:497
  33.8 6.1 %shard_map.70 = f32[16,72,128]{2,1,0:T(8,128)S(1)} custom-call(f32[16,48,128]{2,1,0:T(8,128)S(1)} %all_to_all.21.in_ref, f32[120,128]{1,0:T(8,128)S(1)} %get-tuple-element.13.number_ref), custom_call_target="tpu_custom_call" | custom-call | flops 100000000 | bytes 2000000 | tf_op jit(solution)/shard_map/pallas_call | solution.py:462
  39.9 13.6 %all_to_all.22.in_ref = f32[16,72,128]{2,1,0:T(8,128)S(1)} all-to-all(f32[16,72,128]{2,1,0:T(8,128)S(1)} %shard_map.70), channel_id=1, replica_groups=mesh['cell'=64,'inst'=16] {'inst'}, dimensions={0} | all-to-all | bytes 1179648 | tf_op jit(solution)/shard_map/all_to_all | solution.py:512
  53.5 1.0 %shard_map.71 = f32[64,128]{1,0:T(8,128)} custom-call(f32[16,72,128]{2,1,0:T(8,128)S(1)} %all_to_all.22.in_ref), custom_call_target="tpu_custom_call" | custom-call | flops 1000000 | bytes 2000000 | tf_op jit(solution)/shard_map/pallas_call | solution.py:462
  54.5 31.3 %all-to-all-start.2 = ((f32[64,1,128]{2,1,0:T(1,128)}), f32[64,1,128]{2,1,0:T(1,128)S(1)}, u32[]{:S(2)}, u32[]{:S(2)}) async-start(f32[64,1,128]{2,1,0:T(1,128)} %bitcast.3), calls=%async_computation.2 | async-start | bytes 65536 | tf_op jit(solution)/shard_map/all_to_all | solution.py:514
  85.9 2.5 %shard_map.72.vec_ref = f32[7,1,5,16,256]{4,3,2,1,0:T(8,128)S(1)} custom-call(f32[16,72,128]{2,1,0:T(8,128)S(1)} %all_to_all.22.in_ref), custom_call_target="tpu_custom_call" | custom-call | flops 1000000 | bytes 2000000 | tf_op jit(solution)/shard_map/pallas_call | solution.py:462
  88.4 1.3 %all-to-all-done.2 = f32[64,1,128]{2,1,0:T(1,128)S(1)} async-done(((f32[64,1,128]{2,1,0:T(1,128)}), f32[64,1,128]{2,1,0:T(1,128)S(1)}, u32[]{:S(2)}, u32[]{:S(2)}) %all-to-all-start.2) | async-done | bytes 32800 | tf_op jit(solution)/shard_map/all_to_all | solution.py:514
  89.7 1.6 %shard_map.73 = (f32[8,1,5,16,256]{4,3,2,1,0:T(8,128)}, f32[8,8]{1,0:T(8,128)}) custom-call(f32[64,128]{1,0:T(8,128)S(1)} %bitcast.6, f32[1,5,16,256]{3,2,1,0:T(8,128)S(1)} %copy-done, f32[7,1,5,16,256]{4,3,2,1,0:T(8,128)S(1)} %shard_map.72.vec_ref), custom_call_target="tpu_custom_call" | custom-call | flops 1000000 | bytes 2000000 | tf_op jit(solution)/shard_map/pallas_call | solution.py:462
Async XLA Ops:
  0.6 22.4 %copy-start = (f32[1,5,16,256]{3,2,1,0:T(8,128)S(1)}, f32[1,5,16,256]{3,2,1,0:T(8,128)}, u32[]{:S(2)}) copy-start(f32[1,5,16,256]{3,2,1,0:T(8,128)} %res_ref.5) | copy-start | bytes 245764
  0.6 22.4 %copy-start.1 = (f32[1,16,256]{2,1,0:T(8,128)S(1)}, f32[1,16,256]{2,1,0:T(8,128)}, u32[]{:S(2)}) copy-start(f32[1,16,256]{2,1,0:T(8,128)} %gain_ref.3) | copy-start | bytes 49156
  1.6 18.6 %collective-permute-start = (f32[6,8,256]{2,1,0:T(8,128)S(1)}, f32[6,8,256]{2,1,0:T(8,128)S(1)}, u32[]{:S(2)}, u32[]{:S(2)}) collective-permute-start(f32[6,8,256]{2,1,0:T(8,128)S(1)} %get-tuple-element.8), channel_id=1, source_target_pairs={{0,16},{32,48},{64,80},{96,112},{128,144},{160,176},{192,208},{224... | collective-permute-start | bytes 147464 | tf_op jit(solution)/shard_map/ppermute | solution.py:490
  17.6 5.4 %collective-permute-start.1 = (f32[6,8,256]{2,1,0:T(8,128)S(1)}, f32[6,8,256]{2,1,0:T(8,128)S(1)}, u32[]{:S(2)}, u32[]{:S(2)}) collective-permute-start(f32[6,8,256]{2,1,0:T(8,128)S(1)} %get-tuple-element.9), channel_id=1, source_target_pairs={{16,32},{48,64},{80,96},{112,128},{144,160},{176,192},{208,224},{2... | collective-permute-start | bytes 147464 | tf_op jit(solution)/shard_map/ppermute | solution.py:489
  54.5 35.2 %all-to-all-start.2 = ((f32[64,1,128]{2,1,0:T(1,128)}), f32[64,1,128]{2,1,0:T(1,128)S(1)}, u32[]{:S(2)}, u32[]{:S(2)}) async-start(f32[64,1,128]{2,1,0:T(1,128)} %bitcast.3), calls=%async_computation.2 | async-start | bytes 65536 | tf_op jit(solution)/shard_map/all_to_all | solution.py:514

commit v9 on v8

--- a/solution.py
+++ b/solution.py
@@ -20,6 +20,7 @@
 NR = 1024
 STATE = FIELDS + 1
 MEETING = [[(i + CELLS // 2) % CELLS for i in range(CELLS)]]
+TURN = [(i + INST - 1) % INST for i in range(INST)]
 VMEM = pl.BlockSpec(memory_space=pltpu.VMEM)
 HBM = pl.BlockSpec(memory_space=pltpu.HBM)
 TILE = (8, 128)
@@ -78,7 +79,7 @@
                     if inst in (7, 8):
                         piece = jnp.where(place < (24 if inst == 7 else 8), left, right)
                     chunk = piece if chunk is None else jnp.where(group == (part + inst // 2) % 4, piece, chunk)
-                out_ref[inst, field * 8 : field * 8 + 8, :] = chunk
+                out_ref[TURN.index(inst), field * 8 : field * 8 + 8, :] = chunk
 
 
 def merge_pair(first, second, mask, shift, axis):
@@ -178,8 +179,8 @@
                 coef_ref[(d * FIELDS + f) * FIELDS + e] = jnp.broadcast_to(number_ref[at : at + 1, :], TILE)
     for i in range(INST):
         for f in range(FIELDS):
-            vec_ref[0, pl.ds(tile_at(i, f), 8), :] = jnp.where(inside, in_ref[i, f * 8 : f * 8 + 8, :], 0.0)
-        gain_ref[i] = in_ref[i, FIELDS * 8 : FIELDS * 8 + 8, :]
+            vec_ref[0, pl.ds(tile_at(i, f), 8), :] = jnp.where(inside, in_ref[TURN.index(i), f * 8 : f * 8 + 8, :], 0.0)
+        gain_ref[i] = in_ref[TURN.index(i), FIELDS * 8 : FIELDS * 8 + 8, :]
 
     weights = [jnp.broadcast_to(number_ref[at : at + 1, :], TILE) for at in range(JAC + S - 1, NUMBERS)]
 
@@ -494,7 +495,7 @@
         [VMEM] * 5 + [pl.BlockSpec(memory_space=pltpu.SMEM), VMEM],
         (residual, diag_gain, near, far, jac, omega, shift),
     )
-    patches = lax.all_to_all(chunks, "inst", 0, 0, tiled=True)
+    patches = lax.all_to_all(chunks, "inst", 0, 0, axis_index_groups=[TURN], tiled=True)
     vectors = call(
         step_kernel,
         (INST, 72, 128),

time: 91.6 us -> 91 us (level)
  starting transfers between devices: 49.3 us -> 46.8 us
  blocking collectives: 24.2 us -> 26.1 us
    all_to_all x1, starting transfers between devices: 31.3 us -> 28.8 us  [on_device(): lax.all_to_all(row, 'cell', 0, 0, axis_index_groups=MEETING, tiled=True)]
    all_to_all x1, blocking collectives: 13.6 us -> 15.7 us  [on_device(): back = lax.all_to_all(vectors, 'inst', 0, 0, tiled=True)]
where the time goes in v9:
time: 91 us; the launch traced here: 90.7 us
  starting transfers between devices  46.8 us (51%)
  blocking collectives  26.1 us (29%)
  Pallas kernels  12.4 us (14%)
  waiting for transfers between devices  4.16 us (5%)
  between operations  1.35 us (1%)
    all_to_all x1, starting transfers between devices, on_device(): lax.all_to_all(row, 'cell', 0, 0, axis_index_groups=MEETING, tiled=True)  28.8 us
    ppermute x1, starting transfers between devices, on_device(): near = lax.ppermute(near, 'cell', pairs[0] + [(b, a) for a, b in pairs[0]])  16 us
    all_to_all x1, blocking collectives, on_device(): back = lax.all_to_all(vectors, 'inst', 0, 0, tiled=True)  15.7 us
    pallas_call x6, Pallas kernels, call(): pl.pallas_call(kernel, out_shape=shapes, in_specs=in_specs, out_specs=jax...  12.4 us
    all_to_all x1, blocking collectives, on_device(): lax.all_to_all(chunks, 'inst', 0, 0, axis_index_groups=[TURN], tiled=True)  10.3 us
    ppermute x1, waiting for transfers between devices, on_device(): far = lax.ppermute(far, 'cell', pairs[1] + [(b, a) for a, b in pairs[1]])  2.82 us
    ppermute x1, starting transfers between devices, on_device(): far = lax.ppermute(far, 'cell', pairs[1] + [(b, a) for a, b in pairs[1]])  1.92 us
  transfers between devices with their start and end apart: 3, of which 2 were waited for; matrix products, arithmetic and copies ran while one was open for 0% of the time, Pallas kernels for 3%

profile of v9, /device:TPU:1, one launch (start us, length us, event | category | flops | bytes accessed | tf_op | source)
XLA Modules:
  0.0 90.7 jit_solution(6845170233919718056)
XLA Ops:
  0.6 0.0 copy-start
  0.6 0.0 copy-start.1
  0.7 0.9 %shard_map.68 = (f32[6,8,256]{2,1,0:T(8,128)S(1)}, f32[6,8,256]{2,1,0:T(8,128)S(1)}, f32[5,4,5]{2,1,0:T(4,128)S(1)}, f32[1,7]{1,0:T(1,128)S(1)}) custom-call(f32[1,5,16,256]{3,2,1,0:T(8,128)} %res_ref.5, f32[1,16,256]{2,1,0:T(8,128)} %gain_ref.3, f32[5,4,5]{2,1,0:T(4,128)} %bitcast.7, f32[1,7]{1,0:T(1,128)} %bitcast.8), custom_call_target="tpu_custom_call" | custom-call | flops 1000000 | bytes 2000000 | tf_op jit(solution)/shard_map/pallas_call | solution.py:463
  1.6 16.0 %collective-permute-start = (f32[6,8,256]{2,1,0:T(8,128)S(1)}, f32[6,8,256]{2,1,0:T(8,128)S(1)}, u32[]{:S(2)}, u32[]{:S(2)}) collective-permute-start(f32[6,8,256]{2,1,0:T(8,128)S(1)} %get-tuple-element.8), channel_id=1, source_target_pairs={{0,16},{32,48},{64,80},{96,112},{128,144},{160,176},{192,208},{224... | collective-permute-start | bytes 147464 | tf_op jit(solution)/shard_map/ppermute | solution.py:491
  17.6 1.9 %collective-permute-start.1 = (f32[6,8,256]{2,1,0:T(8,128)S(1)}, f32[6,8,256]{2,1,0:T(8,128)S(1)}, u32[]{:S(2)}, u32[]{:S(2)}) collective-permute-start(f32[6,8,256]{2,1,0:T(8,128)S(1)} %get-tuple-element.9), channel_id=1, source_target_pairs={{16,32},{48,64},{80,96},{112,128},{144,160},{176,192},{208,224},{2... | collective-permute-start | bytes 147464 | tf_op jit(solution)/shard_map/ppermute | solution.py:490
  20.2 0.0 collective-permute-done.near_ref
  20.2 2.8 %collective-permute-done.1.far_ref = f32[6,8,256]{2,1,0:T(8,128)S(1)} collective-permute-done((f32[6,8,256]{2,1,0:T(8,128)S(1)}, f32[6,8,256]{2,1,0:T(8,128)S(1)}, u32[]{:S(2)}, u32[]{:S(2)}) %collective-permute-start.1) | collective-permute-done | bytes 49184 | tf_op jit(solution)/shard_map/ppermute | solution.py:490
  23.0 0.0 copy-done
  23.0 0.0 copy-done.1
  23.0 0.2 shard_map.69
  23.3 10.3 %all_to_all.21.in_ref = f32[16,48,128]{2,1,0:T(8,128)S(1)} all-to-all(f32[16,48,128]{2,1,0:T(8,128)S(1)} %get-tuple-element.12), channel_id=1, replica_groups={{15,0,1,2,3,4,5,6,7,8,9,10,11,12,13,14},{31,16,17,18,19,20,21,22,23,24,..., dimensions={0} | all-to-all | bytes 786432 | tf_op jit(solution)/shard_map/all_to_all | solution.py:498
  33.6 6.1 %shard_map.70 = f32[16,72,128]{2,1,0:T(8,128)S(1)} custom-call(f32[16,48,128]{2,1,0:T(8,128)S(1)} %all_to_all.21.in_ref, f32[120,128]{1,0:T(8,128)S(1)} %get-tuple-element.13.number_ref), custom_call_target="tpu_custom_call" | custom-call | flops 100000000 | bytes 2000000 | tf_op jit(solution)/shard_map/pallas_call | solution.py:463
  39.7 15.7 %all_to_all.22.in_ref = f32[16,72,128]{2,1,0:T(8,128)S(1)} all-to-all(f32[16,72,128]{2,1,0:T(8,128)S(1)} %shard_map.70), channel_id=1, replica_groups=mesh['cell'=64,'inst'=16] {'inst'}, dimensions={0} | all-to-all | bytes 1179648 | tf_op jit(solution)/shard_map/all_to_all | solution.py:513
  55.4 1.0 %shard_map.71 = f32[64,128]{1,0:T(8,128)} custom-call(f32[16,72,128]{2,1,0:T(8,128)S(1)} %all_to_all.22.in_ref), custom_call_target="tpu_custom_call" | custom-call | flops 1000000 | bytes 2000000 | tf_op jit(solution)/shard_map/pallas_call | solution.py:463
  56.5 28.8 %all-to-all-start.2 = ((f32[64,1,128]{2,1,0:T(1,128)}), f32[64,1,128]{2,1,0:T(1,128)S(1)}, u32[]{:S(2)}, u32[]{:S(2)}) async-start(f32[64,1,128]{2,1,0:T(1,128)} %bitcast.3), calls=%async_computation.2 | async-start | bytes 65536 | tf_op jit(solution)/shard_map/all_to_all | solution.py:515
  85.3 2.5 %shard_map.72.vec_ref = f32[7,1,5,16,256]{4,3,2,1,0:T(8,128)S(1)} custom-call(f32[16,72,128]{2,1,0:T(8,128)S(1)} %all_to_all.22.in_ref), custom_call_target="tpu_custom_call" | custom-call | flops 1000000 | bytes 2000000 | tf_op jit(solution)/shard_map/pallas_call | solution.py:463
  87.8 1.3 %all-to-all-done.2 = f32[64,1,128]{2,1,0:T(1,128)S(1)} async-done(((f32[64,1,128]{2,1,0:T(1,128)}), f32[64,1,128]{2,1,0:T(1,128)S(1)}, u32[]{:S(2)}, u32[]{:S(2)}) %all-to-all-start.2) | async-done | bytes 32800 | tf_op jit(solution)/shard_map/all_to_all | solution.py:515
  89.1 1.6 %shard_map.73 = (f32[8,1,5,16,256]{4,3,2,1,0:T(8,128)}, f32[8,8]{1,0:T(8,128)}) custom-call(f32[64,128]{1,0:T(8,128)S(1)} %bitcast.6, f32[1,5,16,256]{3,2,1,0:T(8,128)S(1)} %copy-done, f32[7,1,5,16,256]{4,3,2,1,0:T(8,128)S(1)} %shard_map.72.vec_ref), custom_call_target="tpu_custom_call" | custom-call | flops 1000000 | bytes 2000000 | tf_op jit(solution)/shard_map/pallas_call | solution.py:463
Async XLA Ops:
  0.6 22.4 %copy-start = (f32[1,5,16,256]{3,2,1,0:T(8,128)S(1)}, f32[1,5,16,256]{3,2,1,0:T(8,128)}, u32[]{:S(2)}) copy-start(f32[1,5,16,256]{3,2,1,0:T(8,128)} %res_ref.5) | copy-start | bytes 245764
  0.6 22.4 %copy-start.1 = (f32[1,16,256]{2,1,0:T(8,128)S(1)}, f32[1,16,256]{2,1,0:T(8,128)}, u32[]{:S(2)}) copy-start(f32[1,16,256]{2,1,0:T(8,128)} %gain_ref.3) | copy-start | bytes 49156
  1.6 18.6 %collective-permute-start = (f32[6,8,256]{2,1,0:T(8,128)S(1)}, f32[6,8,256]{2,1,0:T(8,128)S(1)}, u32[]{:S(2)}, u32[]{:S(2)}) collective-permute-start(f32[6,8,256]{2,1,0:T(8,128)S(1)} %get-tuple-element.8), channel_id=1, source_target_pairs={{0,16},{32,48},{64,80},{96,112},{128,144},{160,176},{192,208},{224... | collective-permute-start | bytes 147464 | tf_op jit(solution)/shard_map/ppermute | solution.py:491
  17.6 5.4 %collective-permute-start.1 = (f32[6,8,256]{2,1,0:T(8,128)S(1)}, f32[6,8,256]{2,1,0:T(8,128)S(1)}, u32[]{:S(2)}, u32[]{:S(2)}) collective-permute-start(f32[6,8,256]{2,1,0:T(8,128)S(1)} %get-tuple-element.9), channel_id=1, source_target_pairs={{16,32},{48,64},{80,96},{112,128},{144,160},{176,192},{208,224},{2... | collective-permute-start | bytes 147464 | tf_op jit(solution)/shard_map/ppermute | solution.py:490
  56.5 32.6 %all-to-all-start.2 = ((f32[64,1,128]{2,1,0:T(1,128)}), f32[64,1,128]{2,1,0:T(1,128)S(1)}, u32[]{:S(2)}, u32[]{:S(2)}) async-start(f32[64,1,128]{2,1,0:T(1,128)} %bitcast.3), calls=%async_computation.2 | async-start | bytes 65536 | tf_op jit(solution)/shard_map/all_to_all | solution.py:515

commit v10 on v9

--- a/solution.py
+++ b/solution.py
@@ -238,6 +238,7 @@
     def gather(quarter, sums):
         sums = list(sums)
         for i in [quarter * 4 + q for q in range(4)]:
+            chunk = lax.rem(i + 1, INST)
             tiles = {}
             for f in range(FIELDS):
                 at = pl.multiple_of(PITCH * FIELDS * i + tile_at(0, f), 8)
@@ -253,13 +254,13 @@
                     sums[p] = sums[p] + v[a] * v[b]
                 for p, (x, y, half) in enumerate(packed, len(plain)):
                     sums[p] = sums[p] + tiles[x, f] * (turned_tiles[y] if half else tiles[y, f])
-                out_ref[i, (4 + f) * 8 : (4 + f) * 8 + 8, :] = tiles[1, f]
+                out_ref[chunk, (4 + f) * 8 : (4 + f) * 8 + 8, :] = tiles[1, f]
             for f in range(4):
                 tile = tiles[0, f]
                 if f < 3:
                     move = (SLOT_MOVES[0] - SLOT_MOVES[f + 1]) % 128
                     tile = jnp.where(in_slot(seg, 0), pltpu.roll(tiles[0, 4], move, 1), tile)
-                out_ref[i, f * 8 : f * 8 + 8, :] = tile
+                out_ref[chunk, f * 8 : f * 8 + 8, :] = tile
         return tuple(sums)
 
     start = tuple(jnp.zeros(TILE, jnp.float32) for _ in range(len(plain) + len(packed)))
@@ -326,7 +327,7 @@
             places[segs[part]] = (q, part)
     for tile in range(9):
         for wide in range(2):
-            tiles = [pltpu.roll(in_ref[8 * wide + q, tile * 8 : tile * 8 + 8, :], 128 - HALO, 1) for q in range(8)]
+            tiles = [pltpu.roll(in_ref[TURN.index(8 * wide + q), tile * 8 : tile * 8 + 8, :], 128 - HALO, 1) for q in range(8)]
             for bit in (1, 2, 4):
                 off = (seg & bit) == 0
                 for q in range(8):
@@ -510,7 +511,7 @@
         ],
         flops=10**8,
     )
-    back = lax.all_to_all(vectors, "inst", 0, 0, tiled=True)
+    back = lax.all_to_all(vectors, "inst", 0, 0, axis_index_groups=[TURN], tiled=True)
     row = call(gram_kernel, (CELLS, 128), [VMEM], (back,))
     rows = lax.all_to_all(row, "cell", 0, 0, axis_index_groups=MEETING, tiled=True)
     others = call(unpack_kernel, (S - 1, 1, FIELDS, ROWS, NC), [VMEM], (back,))

time: 91 us -> 89.8 us (0.987)
  blocking collectives: 26.1 us -> 24.6 us
    all_to_all x1, blocking collectives: 15.7 us -> 14.2 us  [on_device(): lax.all_to_all(vectors, 'inst', 0, 0, axis_index_groups=[TURN], tiled=True)]
where the time goes in v10:
time: 89.8 us; the launch traced here: 89.5 us
  starting transfers between devices  47 us (52%)
  blocking collectives  24.6 us (27%)
  Pallas kernels  12.4 us (14%)
  waiting for transfers between devices  4.16 us (5%)
  between operations  1.35 us (2%)
    all_to_all x1, starting transfers between devices, on_device(): lax.all_to_all(row, 'cell', 0, 0, axis_index_groups=MEETING, tiled=True)  29.1 us
    ppermute x1, starting transfers between devices, on_device(): near = lax.ppermute(near, 'cell', pairs[0] + [(b, a) for a, b in pairs[0]])  16 us
    all_to_all x1, blocking collectives, on_device(): lax.all_to_all(vectors, 'inst', 0, 0, axis_index_groups=[TURN], tiled=True)  14.2 us
    pallas_call x6, Pallas kernels, call(): pl.pallas_call(kernel, out_shape=shapes, in_specs=in_specs, out_specs=jax...  12.4 us
    all_to_all x1, blocking collectives, on_device(): lax.all_to_all(chunks, 'inst', 0, 0, axis_index_groups=[TURN], tiled=True)  10.3 us
    ppermute x1, waiting for transfers between devices, on_device(): far = lax.ppermute(far, 'cell', pairs[1] + [(b, a) for a, b in pairs[1]])  2.82 us
    ppermute x1, starting transfers between devices, on_device(): far = lax.ppermute(far, 'cell', pairs[1] + [(b, a) for a, b in pairs[1]])  1.92 us
  transfers between devices with their start and end apart: 3, of which 2 were waited for; matrix products, arithmetic and copies ran while one was open for 0% of the time, Pallas kernels for 3%

profile of v10, /device:TPU:1, one launch (start us, length us, event | category | flops | bytes accessed | tf_op | source)
XLA Modules:
  0.0 89.5 jit_solution(7976917550965237483)
XLA Ops:
  0.6 0.0 copy-start
  0.6 0.0 copy-start.1
  0.7 0.9 %shard_map.68 = (f32[6,8,256]{2,1,0:T(8,128)S(1)}, f32[6,8,256]{2,1,0:T(8,128)S(1)}, f32[5,4,5]{2,1,0:T(4,128)S(1)}, f32[1,7]{1,0:T(1,128)S(1)}) custom-call(f32[1,5,16,256]{3,2,1,0:T(8,128)} %res_ref.5, f32[1,16,256]{2,1,0:T(8,128)} %gain_ref.3, f32[5,4,5]{2,1,0:T(4,128)} %bitcast.7, f32[1,7]{1,0:T(1,128)} %bitcast.8), custom_call_target="tpu_custom_call" | custom-call | flops 1000000 | bytes 2000000 | tf_op jit(solution)/shard_map/pallas_call | solution.py:464
  1.6 16.0 %collective-permute-start = (f32[6,8,256]{2,1,0:T(8,128)S(1)}, f32[6,8,256]{2,1,0:T(8,128)S(1)}, u32[]{:S(2)}, u32[]{:S(2)}) collective-permute-start(f32[6,8,256]{2,1,0:T(8,128)S(1)} %get-tuple-element.8), channel_id=1, source_target_pairs={{0,16},{32,48},{64,80},{96,112},{128,144},{160,176},{192,208},{224... | collective-permute-start | bytes 147464 | tf_op jit(solution)/shard_map/ppermute | solution.py:492
  17.6 1.9 %collective-permute-start.1 = (f32[6,8,256]{2,1,0:T(8,128)S(1)}, f32[6,8,256]{2,1,0:T(8,128)S(1)}, u32[]{:S(2)}, u32[]{:S(2)}) collective-permute-start(f32[6,8,256]{2,1,0:T(8,128)S(1)} %get-tuple-element.9), channel_id=1, source_target_pairs={{16,32},{48,64},{80,96},{112,128},{144,160},{176,192},{208,224},{2... | collective-permute-start | bytes 147464 | tf_op jit(solution)/shard_map/ppermute | solution.py:491
  20.2 0.0 collective-permute-done.near_ref
  20.2 2.8 %collective-permute-done.1.far_ref = f32[6,8,256]{2,1,0:T(8,128)S(1)} collective-permute-done((f32[6,8,256]{2,1,0:T(8,128)S(1)}, f32[6,8,256]{2,1,0:T(8,128)S(1)}, u32[]{:S(2)}, u32[]{:S(2)}) %collective-permute-start.1) | collective-permute-done | bytes 49184 | tf_op jit(solution)/shard_map/ppermute | solution.py:491
  23.0 0.0 copy-done
  23.0 0.0 copy-done.1
  23.0 0.2 shard_map.69
  23.3 10.3 %all_to_all.21.in_ref = f32[16,48,128]{2,1,0:T(8,128)S(1)} all-to-all(f32[16,48,128]{2,1,0:T(8,128)S(1)} %get-tuple-element.12), channel_id=1, replica_groups={{15,0,1,2,3,4,5,6,7,8,9,10,11,12,13,14},{31,16,17,18,19,20,21,22,23,24,..., dimensions={0} | all-to-all | bytes 786432 | tf_op jit(solution)/shard_map/all_to_all | solution.py:499
  33.6 6.1 %shard_map.70 = f32[16,72,128]{2,1,0:T(8,128)S(1)} custom-call(f32[16,48,128]{2,1,0:T(8,128)S(1)} %all_to_all.21.in_ref, f32[120,128]{1,0:T(8,128)S(1)} %get-tuple-element.13.number_ref), custom_call_target="tpu_custom_call" | custom-call | flops 100000000 | bytes 2000000 | tf_op jit(solution)/shard_map/pallas_call | solution.py:464
  39.7 14.2 %all_to_all.22.in_ref = f32[16,72,128]{2,1,0:T(8,128)S(1)} all-to-all(f32[16,72,128]{2,1,0:T(8,128)S(1)} %shard_map.70), channel_id=1, replica_groups={{15,0,1,2,3,4,5,6,7,8,9,10,11,12,13,14},{31,16,17,18,19,20,21,22,23,24,..., dimensions={0} | all-to-all | bytes 1179648 | tf_op jit(solution)/shard_map/all_to_all | solution.py:514
  53.9 1.0 %shard_map.71 = f32[64,128]{1,0:T(8,128)} custom-call(f32[16,72,128]{2,1,0:T(8,128)S(1)} %all_to_all.22.in_ref), custom_call_target="tpu_custom_call" | custom-call | flops 1000000 | bytes 2000000 | tf_op jit(solution)/shard_map/pallas_call | solution.py:464
  55.0 29.1 %all-to-all-start.2 = ((f32[64,1,128]{2,1,0:T(1,128)}), f32[64,1,128]{2,1,0:T(1,128)S(1)}, u32[]{:S(2)}, u32[]{:S(2)}) async-start(f32[64,1,128]{2,1,0:T(1,128)} %bitcast.3), calls=%async_computation.2 | async-start | bytes 65536 | tf_op jit(solution)/shard_map/all_to_all | solution.py:516
  84.1 2.5 %shard_map.72.vec_ref = f32[7,1,5,16,256]{4,3,2,1,0:T(8,128)S(1)} custom-call(f32[16,72,128]{2,1,0:T(8,128)S(1)} %all_to_all.22.in_ref), custom_call_target="tpu_custom_call" | custom-call | flops 1000000 | bytes 2000000 | tf_op jit(solution)/shard_map/pallas_call | solution.py:464
  86.5 1.3 %all-to-all-done.2 = f32[64,1,128]{2,1,0:T(1,128)S(1)} async-done(((f32[64,1,128]{2,1,0:T(1,128)}), f32[64,1,128]{2,1,0:T(1,128)S(1)}, u32[]{:S(2)}, u32[]{:S(2)}) %all-to-all-start.2) | async-done | bytes 32800 | tf_op jit(solution)/shard_map/all_to_all | solution.py:516
  87.9 1.6 %shard_map.73 = (f32[8,1,5,16,256]{4,3,2,1,0:T(8,128)}, f32[8,8]{1,0:T(8,128)}) custom-call(f32[64,128]{1,0:T(8,128)S(1)} %bitcast.6, f32[1,5,16,256]{3,2,1,0:T(8,128)S(1)} %copy-done, f32[7,1,5,16,256]{4,3,2,1,0:T(8,128)S(1)} %shard_map.72.vec_ref), custom_call_target="tpu_custom_call" | custom-call | flops 1000000 | bytes 2000000 | tf_op jit(solution)/shard_map/pallas_call | solution.py:464
Async XLA Ops:
  0.6 22.4 %copy-start = (f32[1,5,16,256]{3,2,1,0:T(8,128)S(1)}, f32[1,5,16,256]{3,2,1,0:T(8,128)}, u32[]{:S(2)}) copy-start(f32[1,5,16,256]{3,2,1,0:T(8,128)} %res_ref.5) | copy-start | bytes 245764
  0.6 22.4 %copy-start.1 = (f32[1,16,256]{2,1,0:T(8,128)S(1)}, f32[1,16,256]{2,1,0:T(8,128)}, u32[]{:S(2)}) copy-start(f32[1,16,256]{2,1,0:T(8,128)} %gain_ref.3) | copy-start | bytes 49156
  1.6 18.6 %collective-permute-start = (f32[6,8,256]{2,1,0:T(8,128)S(1)}, f32[6,8,256]{2,1,0:T(8,128)S(1)}, u32[]{:S(2)}, u32[]{:S(2)}) collective-permute-start(f32[6,8,256]{2,1,0:T(8,128)S(1)} %get-tuple-element.8), channel_id=1, source_target_pairs={{0,16},{32,48},{64,80},{96,112},{128,144},{160,176},{192,208},{224... | collective-permute-start | bytes 147464 | tf_op jit(solution)/shard_map/ppermute | solution.py:492
  17.6 5.4 %collective-permute-start.1 = (f32[6,8,256]{2,1,0:T(8,128)S(1)}, f32[6,8,256]{2,1,0:T(8,128)S(1)}, u32[]{:S(2)}, u32[]{:S(2)}) collective-permute-start(f32[6,8,256]{2,1,0:T(8,128)S(1)} %get-tuple-element.9), channel_id=1, source_target_pairs={{16,32},{48,64},{80,96},{112,128},{144,160},{176,192},{208,224},{2... | collective-permute-start | bytes 147464 | tf_op jit(solution)/shard_map/ppermute | solution.py:491
  55.0 32.9 %all-to-all-start.2 = ((f32[64,1,128]{2,1,0:T(1,128)}), f32[64,1,128]{2,1,0:T(1,128)S(1)}, u32[]{:S(2)}, u32[]{:S(2)}) async-start(f32[64,1,128]{2,1,0:T(1,128)} %bitcast.3), calls=%async_computation.2 | async-start | bytes 65536 | tf_op jit(solution)/shard_map/all_to_all | solution.py:516

commit v11 on v10

--- a/solution.py
+++ b/solution.py
@@ -238,10 +238,10 @@
     def gather(quarter, sums):
         sums = list(sums)
         for i in [quarter * 4 + q for q in range(4)]:
-            chunk = lax.rem(i + 1, INST)
+            chunk = (i + 1) % INST
             tiles = {}
             for f in range(FIELDS):
-                at = pl.multiple_of(PITCH * FIELDS * i + tile_at(0, f), 8)
+                at = tile_at(i, f)
                 v = [vec_ref[s, pl.ds(at, 8), :] for s in range(S)]
                 moved = [slot_ref[s, i, f] for s in range(S - 1)] + [pltpu.roll(v[S - 1], last_move, 1)]
                 for x in range(2):
@@ -264,7 +264,9 @@
         return tuple(sums)
 
     start = tuple(jnp.zeros(TILE, jnp.float32) for _ in range(len(plain) + len(packed)))
-    sums = lax.fori_loop(0, INST // 4, gather, start)
+    sums = start
+    for quarter in range(INST // 4):
+        sums = gather(quarter, sums)
     column = lane % 32
     own = ((part == 1) | (part == 2)) & (column >= HALO) & (column < HALO + COLS)
     entry = {}

time: 89.8 us -> 89.6 us (level)
  no operation moved by 1% of the time
where the time goes in v11:
time: 89.6 us; the launch traced here: 89.2 us
  starting transfers between devices  47 us (52%)
  blocking collectives  24.6 us (27%)
  Pallas kernels  12.1 us (14%)
  waiting for transfers between devices  4.16 us (5%)
  between operations  1.35 us (2%)
    all_to_all x1, starting transfers between devices, on_device(): lax.all_to_all(row, 'cell', 0, 0, axis_index_groups=MEETING, tiled=True)  29.1 us
    ppermute x1, starting transfers between devices, on_device(): near = lax.ppermute(near, 'cell', pairs[0] + [(b, a) for a, b in pairs[0]])  16 us
    all_to_all x1, blocking collectives, on_device(): lax.all_to_all(vectors, 'inst', 0, 0, axis_index_groups=[TURN], tiled=True)  14.2 us
    pallas_call x6, Pallas kernels, call(): pl.pallas_call(kernel, out_shape=shapes, in_specs=in_specs, out_specs=jax...  12.1 us
    all_to_all x1, blocking collectives, on_device(): lax.all_to_all(chunks, 'inst', 0, 0, axis_index_groups=[TURN], tiled=True)  10.3 us
    ppermute x1, waiting for transfers between devices, on_device(): far = lax.ppermute(far, 'cell', pairs[1] + [(b, a) for a, b in pairs[1]])  2.82 us
    ppermute x1, starting transfers between devices, on_device(): far = lax.ppermute(far, 'cell', pairs[1] + [(b, a) for a, b in pairs[1]])  1.92 us
  transfers between devices with their start and end apart: 3, of which 2 were waited for; matrix products, arithmetic and copies ran while one was open for 0% of the time, Pallas kernels for 3%

profile of v11, /device:TPU:1, one launch (start us, length us, event | category | flops | bytes accessed | tf_op | source)
XLA Modules:
  0.0 89.2 jit_solution(355573643421546723)
XLA Ops:
  0.6 0.0 copy-start
  0.6 0.0 copy-start.1
  0.7 0.9 %shard_map.68 = (f32[6,8,256]{2,1,0:T(8,128)S(1)}, f32[6,8,256]{2,1,0:T(8,128)S(1)}, f32[5,4,5]{2,1,0:T(4,128)S(1)}, f32[1,7]{1,0:T(1,128)S(1)}) custom-call(f32[1,5,16,256]{3,2,1,0:T(8,128)} %res_ref.5, f32[1,16,256]{2,1,0:T(8,128)} %gain_ref.3, f32[5,4,5]{2,1,0:T(4,128)} %bitcast.7, f32[1,7]{1,0:T(1,128)} %bitcast.8), custom_call_target="tpu_custom_call" | custom-call | flops 1000000 | bytes 2000000 | tf_op jit(solution)/shard_map/pallas_call | solution.py:466
  1.6 16.0 %collective-permute-start = (f32[6,8,256]{2,1,0:T(8,128)S(1)}, f32[6,8,256]{2,1,0:T(8,128)S(1)}, u32[]{:S(2)}, u32[]{:S(2)}) collective-permute-start(f32[6,8,256]{2,1,0:T(8,128)S(1)} %get-tuple-element.8), channel_id=1, source_target_pairs={{0,16},{32,48},{64,80},{96,112},{128,144},{160,176},{192,208},{224... | collective-permute-start | bytes 147464 | tf_op jit(solution)/shard_map/ppermute | solution.py:494
  17.6 1.9 %collective-permute-start.1 = (f32[6,8,256]{2,1,0:T(8,128)S(1)}, f32[6,8,256]{2,1,0:T(8,128)S(1)}, u32[]{:S(2)}, u32[]{:S(2)}) collective-permute-start(f32[6,8,256]{2,1,0:T(8,128)S(1)} %get-tuple-element.9), channel_id=1, source_target_pairs={{16,32},{48,64},{80,96},{112,128},{144,160},{176,192},{208,224},{2... | collective-permute-start | bytes 147464 | tf_op jit(solution)/shard_map/ppermute | solution.py:493
  20.2 0.0 collective-permute-done.near_ref
  20.2 2.8 %collective-permute-done.1.far_ref = f32[6,8,256]{2,1,0:T(8,128)S(1)} collective-permute-done((f32[6,8,256]{2,1,0:T(8,128)S(1)}, f32[6,8,256]{2,1,0:T(8,128)S(1)}, u32[]{:S(2)}, u32[]{:S(2)}) %collective-permute-start.1) | collective-permute-done | bytes 49184 | tf_op jit(solution)/shard_map/ppermute | solution.py:493
  23.0 0.0 copy-done
  23.0 0.0 copy-done.1
  23.0 0.2 shard_map.69
  23.3 10.3 %all_to_all.21.in_ref = f32[16,48,128]{2,1,0:T(8,128)S(1)} all-to-all(f32[16,48,128]{2,1,0:T(8,128)S(1)} %get-tuple-element.12), channel_id=1, replica_groups={{15,0,1,2,3,4,5,6,7,8,9,10,11,12,13,14},{31,16,17,18,19,20,21,22,23,24,..., dimensions={0} | all-to-all | bytes 786432 | tf_op jit(solution)/shard_map/all_to_all | solution.py:501
  33.6 5.8 %shard_map.70 = f32[16,72,128]{2,1,0:T(8,128)S(1)} custom-call(f32[16,48,128]{2,1,0:T(8,128)S(1)} %all_to_all.21.in_ref, f32[120,128]{1,0:T(8,128)S(1)} %get-tuple-element.13.number_ref), custom_call_target="tpu_custom_call" | custom-call | flops 100000000 | bytes 2000000 | tf_op jit(solution)/shard_map/pallas_call | solution.py:466
  39.4 14.2 %all_to_all.22.in_ref = f32[16,72,128]{2,1,0:T(8,128)S(1)} all-to-all(f32[16,72,128]{2,1,0:T(8,128)S(1)} %shard_map.70), channel_id=1, replica_groups={{15,0,1,2,3,4,5,6,7,8,9,10,11,12,13,14},{31,16,17,18,19,20,21,22,23,24,..., dimensions={0} | all-to-all | bytes 1179648 | tf_op jit(solution)/shard_map/all_to_all | solution.py:516
  53.7 1.0 %shard_map.71 = f32[64,128]{1,0:T(8,128)} custom-call(f32[16,72,128]{2,1,0:T(8,128)S(1)} %all_to_all.22.in_ref), custom_call_target="tpu_custom_call" | custom-call | flops 1000000 | bytes 2000000 | tf_op jit(solution)/shard_map/pallas_call | solution.py:466
  54.7 29.1 %all-to-all-start.2 = ((f32[64,1,128]{2,1,0:T(1,128)}), f32[64,1,128]{2,1,0:T(1,128)S(1)}, u32[]{:S(2)}, u32[]{:S(2)}) async-start(f32[64,1,128]{2,1,0:T(1,128)} %bitcast.3), calls=%async_computation.2 | async-start | bytes 65536 | tf_op jit(solution)/shard_map/all_to_all | solution.py:518
  83.8 2.5 %shard_map.72.vec_ref = f32[7,1,5,16,256]{4,3,2,1,0:T(8,128)S(1)} custom-call(f32[16,72,128]{2,1,0:T(8,128)S(1)} %all_to_all.22.in_ref), custom_call_target="tpu_custom_call" | custom-call | flops 1000000 | bytes 2000000 | tf_op jit(solution)/shard_map/pallas_call | solution.py:466
  86.3 1.3 %all-to-all-done.2 = f32[64,1,128]{2,1,0:T(1,128)S(1)} async-done(((f32[64,1,128]{2,1,0:T(1,128)}), f32[64,1,128]{2,1,0:T(1,128)S(1)}, u32[]{:S(2)}, u32[]{:S(2)}) %all-to-all-start.2) | async-done | bytes 32800 | tf_op jit(solution)/shard_map/all_to_all | solution.py:518
  87.6 1.6 %shard_map.73 = (f32[8,1,5,16,256]{4,3,2,1,0:T(8,128)}, f32[8,8]{1,0:T(8,128)}) custom-call(f32[64,128]{1,0:T(8,128)S(1)} %bitcast.6, f32[1,5,16,256]{3,2,1,0:T(8,128)S(1)} %copy-done, f32[7,1,5,16,256]{4,3,2,1,0:T(8,128)S(1)} %shard_map.72.vec_ref), custom_call_target="tpu_custom_call" | custom-call | flops 1000000 | bytes 2000000 | tf_op jit(solution)/shard_map/pallas_call | solution.py:466
Async XLA Ops:
  0.6 22.4 %copy-start = (f32[1,5,16,256]{3,2,1,0:T(8,128)S(1)}, f32[1,5,16,256]{3,2,1,0:T(8,128)}, u32[]{:S(2)}) copy-start(f32[1,5,16,256]{3,2,1,0:T(8,128)} %res_ref.5) | copy-start | bytes 245764
  0.6 22.4 %copy-start.1 = (f32[1,16,256]{2,1,0:T(8,128)S(1)}, f32[1,16,256]{2,1,0:T(8,128)}, u32[]{:S(2)}) copy-start(f32[1,16,256]{2,1,0:T(8,128)} %gain_ref.3) | copy-start | bytes 49156
  1.6 18.6 %collective-permute-start = (f32[6,8,256]{2,1,0:T(8,128)S(1)}, f32[6,8,256]{2,1,0:T(8,128)S(1)}, u32[]{:S(2)}, u32[]{:S(2)}) collective-permute-start(f32[6,8,256]{2,1,0:T(8,128)S(1)} %get-tuple-element.8), channel_id=1, source_target_pairs={{0,16},{32,48},{64,80},{96,112},{128,144},{160,176},{192,208},{224... | collective-permute-start | bytes 147464 | tf_op jit(solution)/shard_map/ppermute | solution.py:494
  17.6 5.4 %collective-permute-start.1 = (f32[6,8,256]{2,1,0:T(8,128)S(1)}, f32[6,8,256]{2,1,0:T(8,128)S(1)}, u32[]{:S(2)}, u32[]{:S(2)}) collective-permute-start(f32[6,8,256]{2,1,0:T(8,128)S(1)} %get-tuple-element.9), channel_id=1, source_target_pairs={{16,32},{48,64},{80,96},{112,128},{144,160},{176,192},{208,224},{2... | collective-permute-start | bytes 147464 | tf_op jit(solution)/shard_map/ppermute | solution.py:493
  54.7 32.9 %all-to-all-start.2 = ((f32[64,1,128]{2,1,0:T(1,128)}), f32[64,1,128]{2,1,0:T(1,128)S(1)}, u32[]{:S(2)}, u32[]{:S(2)}) async-start(f32[64,1,128]{2,1,0:T(1,128)} %bitcast.3), calls=%async_computation.2 | async-start | bytes 65536 | tf_op jit(solution)/shard_map/all_to_all | solution.py:518
